TPU v7x, 256 devices: a whole 4x4x8 slice. The times are simulated.
256 devices in a mesh: label: 8 (over x, core), dp: 8 (over z), basis: 4 (over y).
Axes of the slice: x: 4, y: 4, z: 8, core: 2. Of those that a mesh axis runs over, the one named last changes fastest.
Arguments:
- queries: bfloat16 [16384, 2048], P(('label', 'dp'), 'basis'), may hold values from -6 to 6
- basis: bfloat16 [256, 2048], P(None, 'basis'), may hold values from -0.125 to 0.125
- factors: bfloat16 [98304, 256], P('label'), may hold values from -0.375 to 0.375
- positives: int32 [16384, 16], P(('label', 'dp')), may hold values from 0 to 98303
- counts: int32 [16384], P(('label', 'dp')), may hold values from 1 to 16
- placement: int32 [98304], replicated, may hold values from 0 to 98303, each once
Outputs:
- grad_factors: float32 [98304, 256], P(('label', 'dp', 'basis'))
Inputs may be any that keep to these rules, and one draw needn't show every extreme that they name: `placement`: each row number appears exactly once.
All inputs are finite; a program needn't handle non-finite values.
Results may differ from a plain program's by a relative error of at most 0.0012.
Values may be sent and summed in bfloat16 or wider, within the bound.
No kernel may reach another device: no remote copies, remote signals or barrier semaphores. Data moves between devices by JAX's collectives and lax.ppermute only.
A program may use at most 64 MiB of HBM per device.

v0:
```python
import functools

import jax
import jax.numpy as jnp
from jax import lax
from jax.experimental import pallas as pl
from jax.experimental.pallas import tpu as pltpu
from jax.sharding import PartitionSpec as P


SLOTS = 16
OWN = 64
EXTRA = 16
PAIR = 2 * OWN
MIDDLE = 192
SCALE = 1.0 / 256.0
LINK = jnp.bfloat16
NOWHERE = -250.0


def digits_kernel(where_ref, pos_ref, counts_ref, place_ref, out_ref):
    shift, half = where_ref[0], where_ref[1]
    table = place_ref[...]
    high = ((table >> 8) - MIDDLE).astype(jnp.float32).astype(jnp.bfloat16)
    low = (table & 255).astype(jnp.float32).astype(jnp.bfloat16)
    tables = jnp.concatenate([high, low], axis=1)
    pos = pltpu.roll(pos_ref[...], shift, 1)[:, :128]
    counts = pltpu.roll(jnp.broadcast_to(counts_ref[...], (8, 256)), shift, 1)[0:1, :128]
    groups = table.shape[0]
    row = lax.broadcasted_iota(jnp.int32, (groups, 128), 0)
    lane = lax.broadcasted_iota(jnp.int32, (128, 128), 0)
    spot = lax.broadcasted_iota(jnp.int32, (1, 128), 1)
    mine = (spot >= half) & (spot < half + OWN)
    highs, lows = [], []
    for k in range(SLOTS):
        one = pos[k : k + 1, :]
        hot = jnp.where(row == (one >> 7), 1.0, 0.0).astype(jnp.bfloat16)
        both = lax.dot_general(tables, hot, (((0,), (0,)), ((), ())), preferred_element_type=jnp.float32)
        pick = lane == (one & 127)
        first = jnp.sum(jnp.where(pick, both[:128], 0.0), axis=0, keepdims=True)
        second = jnp.sum(jnp.where(pick, both[128:], 0.0), axis=0, keepdims=True)
        used = k < counts
        highs.append(jnp.where(mine, jnp.where(used, first, NOWHERE), 0.0))
        lows.append(jnp.where(mine & used, second, 0.0))
    out_ref[...] = jnp.concatenate(
        [jnp.concatenate(highs, axis=0), jnp.concatenate(lows, axis=0)], axis=1
    ).astype(jnp.bfloat16)


def build_words(base, payload_refs, words_ref, word_ref, bit_ref):
    spot = 0
    for payload_ref in payload_refs:
        for p in range(payload_ref.shape[0]):
            both = payload_ref[p, PAIR:, :].astype(jnp.float32).astype(jnp.int32)
            local = (both[:, :128] + MIDDLE) * 256 + both[:, 128:] - base
            word_ref[spot] = local >> 5
            bit_ref[spot] = jnp.left_shift(1, local & 31)
            spot += 1
    shape = words_ref.shape[1:]
    order = lax.broadcasted_iota(jnp.int32, shape, 0)

    def build(p, carry):
        found = jnp.zeros(shape, jnp.int32)
        for k in range(SLOTS):
            word = jnp.broadcast_to(word_ref[p, k : k + 1, :], shape)
            bit = jnp.broadcast_to(bit_ref[p, k : k + 1, :], shape)
            found = found | jnp.where(order == word, bit, 0)
        words_ref[p] = found
        return carry

    lax.fori_loop(0, spot, build, 0)


def block_grads(factor_ref, payload_refs, words_ref):
    word_count = words_ref.shape[1]
    bits = jnp.left_shift(1, lax.broadcasted_iota(jnp.int32, (32, 128), 0))
    proj = [ref[:, :PAIR, :].reshape(-1, 256) for ref in payload_refs]
    proj = proj[0] if len(proj) == 1 else jnp.concatenate(proj, axis=0)
    scores = lax.dot_general(
        factor_ref[...],
        proj * jnp.bfloat16(0.5),
        (((1,), (1,)), ((), ())),
        preferred_element_type=jnp.float32,
    )
    tanh = jnp.tanh(scores)
    columns = []
    for c in range(proj.shape[0] // 128):
        found = words_ref[c]
        rows = []
        for m in range(word_count):
            hit = (jnp.broadcast_to(found[m : m + 1, :], (32, 128)) & bits) != 0
            piece = tanh[m * 32 : m * 32 + 32, c * 128 : c * 128 + 128]
            rows.append((piece + jnp.where(hit, -1.0, 1.0)).astype(jnp.bfloat16))
        columns.append(jnp.concatenate(rows, axis=0))
    grad = jnp.concatenate(columns, axis=1)
    return jnp.dot(grad, proj, preferred_element_type=jnp.float32)


def grads_kernel(blocks, payloads, adds, where_ref, *refs):
    count = len(blocks)
    given = count + payloads + count * adds
    sources, refs = refs[:given], refs[given:]
    outs, refs = refs[:count], refs[count:]
    held, (words_ref, word_ref, bit_ref, sem) = refs[:given], refs[given:]
    copies = [
        pltpu.make_async_copy(source, hold, sem.at[i])
        for i, (source, hold) in enumerate(zip(sources, held))
    ]
    payload_refs = held[count : count + payloads]
    for copy in copies[count : count + payloads] + copies[:count] + copies[count + payloads :]:
        copy.start()
    for copy in copies[count : count + payloads]:
        copy.wait()
    for i, which in enumerate(blocks):
        build_words(where_ref[which], payload_refs, words_ref, word_ref, bit_ref)
        copies[i].wait()
        value = block_grads(held[i], payload_refs, words_ref)
        if adds:
            copies[count + payloads + i].wait()
            value = held[count + payloads + i][...] + value
        outs[i][...] = value


VMEM = pl.BlockSpec(memory_space=pltpu.VMEM)
SMEM = pl.BlockSpec(memory_space=pltpu.SMEM)
ANY = pl.BlockSpec(memory_space=pl.ANY)


def add_grads(where, blocks, factors, payloads, olds=()):
    rows = factors[0].shape[0]
    pairs = sum(payload.shape[0] for payload in payloads)
    work = len(blocks) * rows * pairs * PAIR
    operands = (*factors, *payloads, *olds)
    return pl.pallas_call(
        functools.partial(grads_kernel, blocks, len(payloads), bool(olds)),
        out_shape=[jax.ShapeDtypeStruct((rows, 256), jnp.float32)] * len(blocks),
        in_specs=[SMEM] + [ANY] * len(operands),
        out_specs=[VMEM] * len(blocks),
        scratch_shapes=[pltpu.VMEM(operand.shape, operand.dtype) for operand in operands]
        + [
            pltpu.VMEM((pairs, rows // 32, 128), jnp.int32),
            pltpu.VMEM((pairs, SLOTS, 128), jnp.int32),
            pltpu.VMEM((pairs, SLOTS, 128), jnp.int32),
            pltpu.SemaphoreType.DMA((len(operands),)),
        ],
        compiler_params=pltpu.CompilerParams(vmem_limit_bytes=60 * 1024 * 1024),
        cost_estimate=pl.CostEstimate(
            flops=4 * work * 256, bytes_accessed=1 << 22, transcendentals=work
        ),
    )(where, *operands)


def swap(value, axis, bit):
    size = lax.axis_size(axis)
    return lax.ppermute(value, axis, [(i, i ^ bit) for i in range(size)])


def shift_by(value, axis, step, inner=1):
    size = lax.axis_size(axis)
    return lax.ppermute(value, axis, [(i, (i + step * inner) % size) for i in range(size)])


def body(queries, basis, factors, positives, counts, placement):
    label, dp, part = lax.axis_index("label"), lax.axis_index("dp"), lax.axis_index("basis")
    block = factors.shape[0] // lax.axis_size("dp")
    half = (dp & 1) * OWN
    mine = lax.dynamic_slice_in_dim(factors, dp * block, block, 0)
    partial_value = lax.dot_general(
        queries, basis, (((1,), (1,)), ((), ())), preferred_element_type=jnp.float32
    )
    others = swap(mine, "label", 1)
    digits = pl.pallas_call(
        digits_kernel,
        out_shape=jax.ShapeDtypeStruct((EXTRA, 256), jnp.bfloat16),
        in_specs=[SMEM, VMEM, VMEM, VMEM],
        out_specs=VMEM,
        cost_estimate=pl.CostEstimate(flops=1 << 31, bytes_accessed=1 << 19, transcendentals=0),
    )(
        jnp.stack([(half - part * OWN) & 255, half]).astype(jnp.int32),
        positives.T,
        counts.reshape(1, -1),
        placement.reshape(-1, 128),
    )

    rows = partial_value
    for bit in (2, 1):
        count = rows.shape[0] // 2
        high = (part >> (bit - 1)) & 1
        keep = lax.dynamic_slice_in_dim(rows, high * count, count, 0)
        send = lax.dynamic_slice_in_dim(rows, (1 - high) * count, count, 0)
        rows = keep + swap(send, "basis", bit)
    own = jnp.concatenate([rows.astype(jnp.bfloat16), digits], axis=0)
    next_own = swap(own, "dp", 1)
    even = dp & 1 == 0
    pair = jnp.concatenate(
        [
            jnp.where(even, own[:OWN], next_own[:OWN]),
            jnp.where(even, next_own[:OWN], own[:OWN]),
            own[OWN:] + next_own[OWN:],
        ],
        axis=0,
    )[None]
    ring = jnp.concatenate([pair] + [shift_by(pair, "dp", step) for step in (2, 6, 4)], axis=0)

    first = label * factors.shape[0] + dp * block
    other = (label ^ 1) * factors.shape[0] + dp * block
    where = jnp.stack([first, other]).astype(jnp.int32)
    half_ring = ring.shape[0] // 2
    near = [shift_by(ring, "label", step, 2) for step in (1, 3)]
    far = [
        shift_by(near[0][:half_ring], "label", 1, 2),
        shift_by(near[1][half_ring:], "label", 3, 2),
    ]
    sum_mine, sum_other = add_grads(where, (0, 1), (mine, others), (ring,))
    (sum_other,) = add_grads(where, (1,), (others,), near, (sum_other,))
    (sum_other,) = add_grads(where, (1,), (others,), far, (sum_other,))
    received = swap(sum_other, "label", 1)
    (sum_mine,) = add_grads(where, (0,), (mine,), near + far, (sum_mine,))

    quarter = block // lax.axis_size("basis")

    def quarter_of(step):
        start = ((part + step) & 3) * quarter
        return lax.dynamic_slice_in_dim(sum_mine, start, quarter, 0) + lax.dynamic_slice_in_dim(
            received, start, quarter, 0
        )

    total = quarter_of(0)
    for step in (2, 1, 3):
        sent = (quarter_of(step) * SCALE).astype(LINK)
        total = total + shift_by(sent, "basis", step).astype(jnp.float32) * (1 / SCALE)
    return total * SCALE


def solution(mesh):
    placed = (
        P(("label", "dp"), "basis"),
        P(None, "basis"),
        P("label", None),
        P(("label", "dp"), None),
        P(("label", "dp")),
        P(),
    )
    return jax.shard_map(
        body,
        mesh=mesh,
        in_specs=placed,
        out_specs=P(("label", "dp", "basis"), None),
        check_vma=False,
    )
```

profile of v0, /device:TPU:33, one launch (start us, length us, event | category | flops | bytes accessed | tf_op | source)
XLA Modules:
  0.0 87.8 jit_solution(11154631424240319001)
XLA Ops:
  2.2 3.0 %collective-permute-start = (f32[128,256]{1,0:T(8,128)S(1)}, f32[128,256]{1,0:T(8,128)S(1)}, u32[]{:S(2)}, u32[]{:S(2)}) collective-permute-start(f32[128,256]{1,0:T(8,128)S(1)} %constant_dynamic-slice_fusion.1), channel_id=1, source_target_pairs={{0,2},{1,3},{2,0},{3,1},{4,6},{5,7},{6,4},{7,5},{8,10},{9,11},{10,... | collective-permute-start | bytes 393224 | tf_op jit(solution)/shard_map/ppermute | solution.py:155
  5.8 2.3 %collective-permute-done = f32[128,256]{1,0:T(8,128)S(1)} collective-permute-done((f32[128,256]{1,0:T(8,128)S(1)}, f32[128,256]{1,0:T(8,128)S(1)}, u32[]{:S(2)}, u32[]{:S(2)}) %collective-permute-start) | collective-permute-done | bytes 131104 | tf_op jit(solution)/shard_map/ppermute | solution.py:155
  8.2 1.4 %collective-permute-start.1 = (f32[64,256]{1,0:T(8,128)S(1)}, f32[64,256]{1,0:T(8,128)S(1)}, u32[]{:S(2)}, u32[]{:S(2)}) collective-permute-start(f32[64,256]{1,0:T(8,128)S(1)} %constant_dynamic-slice_fusion), channel_id=1, source_target_pairs={{0,1},{1,0},{2,3},{3,2},{4,5},{5,4},{6,7},{7,6},{8,9},{9,8},{10,11... | collective-permute-start | bytes 196616 | tf_op jit(solution)/shard_map/ppermute | solution.py:155
  9.6 3.6 %shard_map.64 = bf16[16,256]{1,0:T(8,128)(2,1)} custom-call(s32[2]{0:T(128)} %pad_add_fusion.1.where_ref, s32[16,256]{1,0:T(8,128)} %bitcast.12, s32[1,256]{1,0:T(1,128)} %bitcast.13, s32[768,128]{1,0:T(8,128)} %bitcast.11), custom_call_target="tpu_custom_call" | custom-call | flops 2147483648 | bytes 524288 | tf_op jit(solution)/shard_map/pallas_call | solution.py:172
  15.2 2.5 %collective-permute-start.10 = (bf16[1536,256]{1,0:T(8,128)(2,1)S(1)}, bf16[1536,256]{1,0:T(8,128)(2,1)S(1)}, u32[]{:S(2)}, u32[]{:S(2)}) collective-permute-start(bf16[1536,256]{1,0:T(8,128)(2,1)S(1)} %constant_dynamic-slice_fusion.2.refs_0_), channel_id=1, source_target_pairs={{0,32},{32,0},{64,96},{96,64},{128,160},{160,128},{192,224},{224,1... | collective-permute-start | bytes 2359304 | tf_op jit(solution)/shard_map/ppermute | solution.py:155
  17.7 2.6 %collective-permute-start.3 = (bf16[1,144,256]{2,1,0:T(8,128)(2,1)S(1)}, bf16[1,144,256]{2,1,0:T(8,128)(2,1)S(1)}, u32[]{:S(2)}, u32[]{:S(2)}) collective-permute-start(bf16[1,144,256]{2,1,0:T(8,128)(2,1)S(1)} %maximum_bitcast_fusion), channel_id=1, source_target_pairs={{0,8},{4,12},{8,16},{12,20},{16,24},{20,28},{24,0},{28,4},{1,9},{5... | collective-permute-start | bytes 221192 | tf_op jit(solution)/shard_map/ppermute | solution.py:160
  20.3 3.1 %collective-permute-start.4 = (bf16[1,144,256]{2,1,0:T(8,128)(2,1)S(1)}, bf16[1,144,256]{2,1,0:T(8,128)(2,1)S(1)}, u32[]{:S(2)}, u32[]{:S(2)}) collective-permute-start(bf16[1,144,256]{2,1,0:T(8,128)(2,1)S(1)} %maximum_bitcast_fusion), channel_id=1, source_target_pairs={{0,24},{4,28},{8,0},{12,4},{16,8},{20,12},{24,16},{28,20},{1,25},{... | collective-permute-start | bytes 221192 | tf_op jit(solution)/shard_map/ppermute | solution.py:160
  23.4 4.4 %collective-permute-start.5 = (bf16[1,144,256]{2,1,0:T(8,128)(2,1)S(1)}, bf16[1,144,256]{2,1,0:T(8,128)(2,1)S(1)}, u32[]{:S(2)}, u32[]{:S(2)}) collective-permute-start(bf16[1,144,256]{2,1,0:T(8,128)(2,1)S(1)} %maximum_bitcast_fusion), channel_id=1, source_target_pairs={{0,16},{4,20},{8,24},{12,28},{16,0},{20,4},{24,8},{28,12},{1,17},{... | collective-permute-start | bytes 221192 | tf_op jit(solution)/shard_map/ppermute | solution.py:160
  27.8 3.5 %collective-permute-done.5 = bf16[1,144,256]{2,1,0:T(8,128)(2,1)S(1)} collective-permute-done((bf16[1,144,256]{2,1,0:T(8,128)(2,1)S(1)}, bf16[1,144,256]{2,1,0:T(8,128)(2,1)S(1)}, u32[]{:S(2)}, u32[]{:S(2)}) %collective-permute-start.5) | collective-permute-done | bytes 73760 | tf_op jit(solution)/shard_map/ppermute | solution.py:160
  31.3 1.4 %collective-permute-start.6 = (bf16[4,144,256]{2,1,0:T(8,128)(2,1)S(1)}, bf16[4,144,256]{2,1,0:T(8,128)(2,1)S(1)}, u32[]{:S(2)}, u32[]{:S(2)}) collective-permute-start(bf16[4,144,256]{2,1,0:T(8,128)(2,1)S(1)} %pad_maximum_fusion.refs_2_), channel_id=1, source_target_pairs={{0,64},{32,96},{64,128},{96,160},{128,192},{160,224},{192,0},{224,... | collective-permute-start | bytes 884744 | tf_op jit(solution)/shard_map/ppermute | solution.py:160
  32.7 1.4 %collective-permute-start.7 = (bf16[4,144,256]{2,1,0:T(8,128)(2,1)S(1)}, bf16[4,144,256]{2,1,0:T(8,128)(2,1)S(1)}, u32[]{:S(2)}, u32[]{:S(2)}) collective-permute-start(bf16[4,144,256]{2,1,0:T(8,128)(2,1)S(1)} %pad_maximum_fusion.refs_2_), channel_id=1, source_target_pairs={{0,192},{32,224},{64,0},{96,32},{128,64},{160,96},{192,128},{224,1... | collective-permute-start | bytes 884744 | tf_op jit(solution)/shard_map/ppermute | solution.py:160
  34.7 3.6 %collective-permute-done.6.refs_1_ = bf16[4,144,256]{2,1,0:T(8,128)(2,1)S(1)} collective-permute-done((bf16[4,144,256]{2,1,0:T(8,128)(2,1)S(1)}, bf16[4,144,256]{2,1,0:T(8,128)(2,1)S(1)}, u32[]{:S(2)}, u32[]{:S(2)}) %collective-permute-start.6) | collective-permute-done | bytes 294944 | tf_op jit(solution)/shard_map/ppermute | solution.py:160
  38.4 2.9 %collective-permute-start.9 = (bf16[2,144,256]{2,1,0:T(8,128)(2,1)S(1)}, bf16[2,144,256]{2,1,0:T(8,128)(2,1)S(1)}, u32[]{:S(2)}, u32[]{:S(2)}) collective-permute-start(bf16[2,144,256]{2,1,0:T(8,128)(2,1)S(1)} %slice.20), channel_id=1, source_target_pairs={{0,192},{32,224},{64,0},{96,32},{128,64},{160,96},{192,128},{224,1... | collective-permute-start | bytes 442376 | tf_op jit(solution)/shard_map/ppermute | solution.py:160
  42.2 5.5 %shard_map.65 = (f32[1536,256]{1,0:T(8,128)}, f32[1536,256]{1,0:T(8,128)}) custom-call(s32[2]{0:T(128)} %pad_add_fusion.where_ref, bf16[1536,256]{1,0:T(8,128)(2,1)} %copy-done.2, bf16[1536,256]{1,0:T(8,128)(2,1)} %copy-done.1, bf16[4,144,256]{2,1,0:T(8,128)(2,1)} %copy-done.3), custom_call_target="tpu_custom_call" | custom-call | flops 1610612736 | bytes 4194304 | tf_op jit(solution)/shard_map/pallas_call | solution.py:134
  47.7 5.4 %shard_map.67.refs_3_ = f32[1536,256]{1,0:T(8,128)} custom-call(s32[2]{0:T(128)} %pad_add_fusion.where_ref, bf16[1536,256]{1,0:T(8,128)(2,1)} %copy-done.1, bf16[4,144,256]{2,1,0:T(8,128)(2,1)} %copy-done.6, bf16[4,144,256]{2,1,0:T(8,128)(2,1)} %copy-done.7, f32[1536,256]{1,0:T(8,128)} %get-tuple-element.8.refs_3_), custom_call_target="tpu_custom_call" | custom-call | flops 1610612736 | bytes 4194304 | tf_op jit(solution)/shard_map/pallas_call | solution.py:134
  54.5 4.4 %shard_map.68 = f32[1536,256]{1,0:T(8,128)} custom-call(s32[2]{0:T(128)} %pad_add_fusion.where_ref, bf16[1536,256]{1,0:T(8,128)(2,1)} %copy-done.1, bf16[2,144,256]{2,1,0:T(8,128)(2,1)} %copy-done.4, bf16[2,144,256]{2,1,0:T(8,128)(2,1)} %copy-done.5, f32[1536,256]{1,0:T(8,128)} %shard_map.67.refs_3_), custom_call_target="tpu_custom_call" | custom-call | flops 805306368 | bytes 4194304 | tf_op jit(solution)/shard_map/pallas_call | solution.py:134
  58.9 6.4 %collective-permute-start.11 = (f32[1536,256]{1,0:T(8,128)}, f32[1536,256]{1,0:T(8,128)S(1)}, u32[]{:S(2)}, u32[]{:S(2)}) collective-permute-start(f32[1536,256]{1,0:T(8,128)} %shard_map.68), channel_id=1, source_target_pairs={{0,32},{32,0},{64,96},{96,64},{128,160},{160,128},{192,224},{224,1... | collective-permute-start | bytes 4718600 | tf_op jit(solution)/shard_map/ppermute | solution.py:155
  65.3 6.5 %shard_map.66 = f32[1536,256]{1,0:T(8,128)} custom-call(s32[2]{0:T(128)} %pad_add_fusion.where_ref, bf16[1536,256]{1,0:T(8,128)(2,1)} %copy-done.2, bf16[4,144,256]{2,1,0:T(8,128)(2,1)} %copy-done.6, bf16[4,144,256]{2,1,0:T(8,128)(2,1)} %copy-done.7, bf16[2,144,256]{2,1,0:T(8,128)(2,1)} %copy-done.4, bf16[2,144,256]{2,1,0:T(8,128)(2,1)} %copy-done.5, ...), custom_call_target="tpu_custom_call" | custom-call | flops 2415919104 | bytes 4194304 | tf_op jit(solution)/shard_map/pallas_call | solution.py:134
  71.9 1.4 %multiply_convert_fusion.2 = (bf16[384,256]{1,0:T(8,128)(2,1)S(1)}, bf16[384,256]{1,0:T(8,128)(2,1)S(1)}, bf16[384,256]{1,0:T(8,128)(2,1)S(1)}) fusion(f32[1536,256]{1,0:T(8,128)S(1)} %collective-permute-done.11, s32[]{:T(128)S(6)} %select_n.52, f32[1536,256]{1,0:T(8,128)} %shard_map.66, s32[]{:T(128)S(6)} %select_n.54, s32[]{:T(128)S(6)} %select_n.53), kind=kLoop, calls=%fused_computation.3 | loop fusion | flops 884736 | bytes 2949132 | tf_op jit(solution)/shard_map/convert_element_type | solution.py:230
  73.3 2.7 %collective-permute-start.12 = (bf16[384,256]{1,0:T(8,128)(2,1)S(1)}, bf16[384,256]{1,0:T(8,128)(2,1)S(1)}, u32[]{:S(2)}, u32[]{:S(2)}) collective-permute-start(bf16[384,256]{1,0:T(8,128)(2,1)S(1)} %get-tuple-element.9), channel_id=1, source_target_pairs={{0,2},{1,3},{2,0},{3,1},{4,6},{5,7},{6,4},{7,5},{8,10},{9,11},{10,... | collective-permute-start | bytes 589832 | tf_op jit(solution)/shard_map/ppermute | solution.py:160
  76.0 2.7 %collective-permute-start.14 = (bf16[384,256]{1,0:T(8,128)(2,1)S(1)}, bf16[384,256]{1,0:T(8,128)(2,1)S(1)}, u32[]{:S(2)}, u32[]{:S(2)}) collective-permute-start(bf16[384,256]{1,0:T(8,128)(2,1)S(1)} %get-tuple-element.10), channel_id=1, source_target_pairs={{0,3},{1,0},{2,1},{3,2},{4,7},{5,4},{6,5},{7,6},{8,11},{9,8},{10,9... | collective-permute-start | bytes 589832 | tf_op jit(solution)/shard_map/ppermute | solution.py:160
  78.7 2.6 %collective-permute-done.12 = bf16[384,256]{1,0:T(8,128)(2,1)S(1)} collective-permute-done((bf16[384,256]{1,0:T(8,128)(2,1)S(1)}, bf16[384,256]{1,0:T(8,128)(2,1)S(1)}, u32[]{:S(2)}, u32[]{:S(2)}) %collective-permute-start.12) | collective-permute-done | bytes 196640 | tf_op jit(solution)/shard_map/ppermute | solution.py:160
  81.3 4.6 %collective-permute-done.13 = bf16[384,256]{1,0:T(8,128)(2,1)S(1)} collective-permute-done((bf16[384,256]{1,0:T(8,128)(2,1)S(1)}, bf16[384,256]{1,0:T(8,128)(2,1)S(1)}, u32[]{:S(2)}, u32[]{:S(2)}) %collective-permute-start.13) | collective-permute-done | bytes 196640 | tf_op jit(solution)/shard_map/ppermute | solution.py:160
  85.9 1.9 %add_multiply_fusion = f32[384,256]{1,0:T(8,128)} fusion(bf16[384,256]{1,0:T(8,128)(2,1)S(1)} %collective-permute-done.14, bf16[384,256]{1,0:T(8,128)(2,1)S(1)} %collective-permute-done.13, bf16[384,256]{1,0:T(8,128)(2,1)S(1)} %collective-permute-done.12, f32[1536,256]{1,0:T(8,128)S(1)} %collective-permute-done.11, s32[]{:T(128)S(6)} %select_n.51, ...), kind=kLoop, calls=%fused_computation | loop fusion | flops 1081344 | bytes 1769476 | tf_op jit(solution)/shard_map/mul | solution.py:232
  (46 shorter events, 7.8 us)
Async XLA Ops:
  0.0 1.0 %copy-start = (bf16[256,512]{1,0:T(8,128)(2,1)S(1)}, bf16[256,512]{1,0:T(8,128)(2,1)}, u32[]{:S(2)}) copy-start(bf16[256,512]{1,0:T(8,128)(2,1)} %param.6) | copy-start | bytes 786436
  2.2 6.0 %collective-permute-start = (f32[128,256]{1,0:T(8,128)S(1)}, f32[128,256]{1,0:T(8,128)S(1)}, u32[]{:S(2)}, u32[]{:S(2)}) collective-permute-start(f32[128,256]{1,0:T(8,128)S(1)} %constant_dynamic-slice_fusion.1), channel_id=1, source_target_pairs={{0,2},{1,3},{2,0},{3,1},{4,6},{5,7},{6,4},{7,5},{8,10},{9,11},{10,... | collective-permute-start | bytes 393224 | tf_op jit(solution)/shard_map/ppermute | solution.py:155
  8.2 5.0 %collective-permute-start.1 = (f32[64,256]{1,0:T(8,128)S(1)}, f32[64,256]{1,0:T(8,128)S(1)}, u32[]{:S(2)}, u32[]{:S(2)}) collective-permute-start(f32[64,256]{1,0:T(8,128)S(1)} %constant_dynamic-slice_fusion), channel_id=1, source_target_pairs={{0,1},{1,0},{2,3},{3,2},{4,5},{5,4},{6,7},{7,6},{8,9},{9,8},{10,11... | collective-permute-start | bytes 196616 | tf_op jit(solution)/shard_map/ppermute | solution.py:155
  13.2 4.4 %copy-start.8 = (bf16[16,256]{1,0:T(8,128)(2,1)S(1)}, bf16[16,256]{1,0:T(8,128)(2,1)}, u32[]{:S(2)}) copy-start(bf16[16,256]{1,0:T(8,128)(2,1)} %shard_map.64) | copy-start | bytes 24580
  14.0 3.7 %collective-permute-start.2 = (bf16[80,256]{1,0:T(8,128)(2,1)S(1)}, bf16[80,256]{1,0:T(8,128)(2,1)S(1)}, u32[]{:S(2)}, u32[]{:S(2)}) collective-permute-start(bf16[80,256]{1,0:T(8,128)(2,1)S(1)} %pad_maximum_fusion.1), channel_id=1, source_target_pairs={{0,4},{4,0},{8,12},{12,8},{16,20},{20,16},{24,28},{28,24},{1,5},{5... | collective-permute-start | bytes 122888 | tf_op jit(solution)/shard_map/ppermute | solution.py:155
  15.2 26.1 %copy-start.2 = (bf16[1536,256]{1,0:T(8,128)(2,1)}, bf16[1536,256]{1,0:T(8,128)(2,1)S(1)}, u32[]{:S(2)}) copy-start(bf16[1536,256]{1,0:T(8,128)(2,1)S(1)} %constant_dynamic-slice_fusion.2.refs_0_) | copy-start | bytes 2359300
  15.2 26.1 %collective-permute-start.10 = (bf16[1536,256]{1,0:T(8,128)(2,1)S(1)}, bf16[1536,256]{1,0:T(8,128)(2,1)S(1)}, u32[]{:S(2)}, u32[]{:S(2)}) collective-permute-start(bf16[1536,256]{1,0:T(8,128)(2,1)S(1)} %constant_dynamic-slice_fusion.2.refs_0_), channel_id=1, source_target_pairs={{0,32},{32,0},{64,96},{96,64},{128,160},{160,128},{192,224},{224,1... | collective-permute-start | bytes 2359304 | tf_op jit(solution)/shard_map/ppermute | solution.py:155
  17.7 10.1 %collective-permute-start.3 = (bf16[1,144,256]{2,1,0:T(8,128)(2,1)S(1)}, bf16[1,144,256]{2,1,0:T(8,128)(2,1)S(1)}, u32[]{:S(2)}, u32[]{:S(2)}) collective-permute-start(bf16[1,144,256]{2,1,0:T(8,128)(2,1)S(1)} %maximum_bitcast_fusion), channel_id=1, source_target_pairs={{0,8},{4,12},{8,16},{12,20},{16,24},{20,28},{24,0},{28,4},{1,9},{5... | collective-permute-start | bytes 221192 | tf_op jit(solution)/shard_map/ppermute | solution.py:160
  20.3 7.5 %collective-permute-start.4 = (bf16[1,144,256]{2,1,0:T(8,128)(2,1)S(1)}, bf16[1,144,256]{2,1,0:T(8,128)(2,1)S(1)}, u32[]{:S(2)}, u32[]{:S(2)}) collective-permute-start(bf16[1,144,256]{2,1,0:T(8,128)(2,1)S(1)} %maximum_bitcast_fusion), channel_id=1, source_target_pairs={{0,24},{4,28},{8,0},{12,4},{16,8},{20,12},{24,16},{28,20},{1,25},{... | collective-permute-start | bytes 221192 | tf_op jit(solution)/shard_map/ppermute | solution.py:160
  23.4 7.9 %collective-permute-start.5 = (bf16[1,144,256]{2,1,0:T(8,128)(2,1)S(1)}, bf16[1,144,256]{2,1,0:T(8,128)(2,1)S(1)}, u32[]{:S(2)}, u32[]{:S(2)}) collective-permute-start(bf16[1,144,256]{2,1,0:T(8,128)(2,1)S(1)} %maximum_bitcast_fusion), channel_id=1, source_target_pairs={{0,16},{4,20},{8,24},{12,28},{16,0},{20,4},{24,8},{28,12},{1,17},{... | collective-permute-start | bytes 221192 | tf_op jit(solution)/shard_map/ppermute | solution.py:160
  31.3 9.9 %copy-start.3 = (bf16[4,144,256]{2,1,0:T(8,128)(2,1)}, bf16[4,144,256]{2,1,0:T(8,128)(2,1)S(1)}, u32[]{:S(2)}) copy-start(bf16[4,144,256]{2,1,0:T(8,128)(2,1)S(1)} %pad_maximum_fusion.refs_2_) | copy-start | bytes 884740
  31.3 6.9 %collective-permute-start.6 = (bf16[4,144,256]{2,1,0:T(8,128)(2,1)S(1)}, bf16[4,144,256]{2,1,0:T(8,128)(2,1)S(1)}, u32[]{:S(2)}, u32[]{:S(2)}) collective-permute-start(bf16[4,144,256]{2,1,0:T(8,128)(2,1)S(1)} %pad_maximum_fusion.refs_2_), channel_id=1, source_target_pairs={{0,64},{32,96},{64,128},{96,160},{128,192},{160,224},{192,0},{224,... | collective-permute-start | bytes 884744 | tf_op jit(solution)/shard_map/ppermute | solution.py:160
  32.7 5.7 %collective-permute-start.7 = (bf16[4,144,256]{2,1,0:T(8,128)(2,1)S(1)}, bf16[4,144,256]{2,1,0:T(8,128)(2,1)S(1)}, u32[]{:S(2)}, u32[]{:S(2)}) collective-permute-start(bf16[4,144,256]{2,1,0:T(8,128)(2,1)S(1)} %pad_maximum_fusion.refs_2_), channel_id=1, source_target_pairs={{0,192},{32,224},{64,0},{96,32},{128,64},{160,96},{192,128},{224,1... | collective-permute-start | bytes 884744 | tf_op jit(solution)/shard_map/ppermute | solution.py:160
  38.2 9.5 %copy-start.6 = (bf16[4,144,256]{2,1,0:T(8,128)(2,1)}, bf16[4,144,256]{2,1,0:T(8,128)(2,1)S(1)}, u32[]{:S(2)}) copy-start(bf16[4,144,256]{2,1,0:T(8,128)(2,1)S(1)} %collective-permute-done.6.refs_1_) | copy-start | bytes 884740
  38.2 15.0 %collective-permute-start.8 = (bf16[2,144,256]{2,1,0:T(8,128)(2,1)S(1)}, bf16[2,144,256]{2,1,0:T(8,128)(2,1)S(1)}, u32[]{:S(2)}, u32[]{:S(2)}) collective-permute-start(bf16[2,144,256]{2,1,0:T(8,128)(2,1)S(1)} %slice.19), channel_id=1, source_target_pairs={{0,64},{32,96},{64,128},{96,160},{128,192},{160,224},{192,0},{224,... | collective-permute-start | bytes 442376 | tf_op jit(solution)/shard_map/ppermute | solution.py:160
  38.4 9.4 %copy-start.7 = (bf16[4,144,256]{2,1,0:T(8,128)(2,1)}, bf16[4,144,256]{2,1,0:T(8,128)(2,1)S(1)}, u32[]{:S(2)}) copy-start(bf16[4,144,256]{2,1,0:T(8,128)(2,1)S(1)} %collective-permute-done.7.refs_2_) | copy-start | bytes 884740
  38.4 14.8 %collective-permute-start.9 = (bf16[2,144,256]{2,1,0:T(8,128)(2,1)S(1)}, bf16[2,144,256]{2,1,0:T(8,128)(2,1)S(1)}, u32[]{:S(2)}, u32[]{:S(2)}) collective-permute-start(bf16[2,144,256]{2,1,0:T(8,128)(2,1)S(1)} %slice.20), channel_id=1, source_target_pairs={{0,192},{32,224},{64,0},{96,32},{128,64},{160,96},{192,128},{224,1... | collective-permute-start | bytes 442376 | tf_op jit(solution)/shard_map/ppermute | solution.py:160
  41.3 0.9 %copy-start.1 = (bf16[1536,256]{1,0:T(8,128)(2,1)}, bf16[1536,256]{1,0:T(8,128)(2,1)S(1)}, u32[]{:S(2)}) copy-start(bf16[1536,256]{1,0:T(8,128)(2,1)S(1)} %collective-permute-done.10.refs_1_.refs_0_) | copy-start | bytes 2359300
  53.2 0.6 copy-start.4
  53.8 0.7 copy-start.5
  58.9 12.9 %collective-permute-start.11 = (f32[1536,256]{1,0:T(8,128)}, f32[1536,256]{1,0:T(8,128)S(1)}, u32[]{:S(2)}, u32[]{:S(2)}) collective-permute-start(f32[1536,256]{1,0:T(8,128)} %shard_map.68), channel_id=1, source_target_pairs={{0,32},{32,0},{64,96},{96,64},{128,160},{160,128},{192,224},{224,1... | collective-permute-start | bytes 4718600 | tf_op jit(solution)/shard_map/ppermute | solution.py:155
  73.3 8.0 %collective-permute-start.12 = (bf16[384,256]{1,0:T(8,128)(2,1)S(1)}, bf16[384,256]{1,0:T(8,128)(2,1)S(1)}, u32[]{:S(2)}, u32[]{:S(2)}) collective-permute-start(bf16[384,256]{1,0:T(8,128)(2,1)S(1)} %get-tuple-element.9), channel_id=1, source_target_pairs={{0,2},{1,3},{2,0},{3,1},{4,6},{5,7},{6,4},{7,5},{8,10},{9,11},{10,... | collective-permute-start | bytes 589832 | tf_op jit(solution)/shard_map/ppermute | solution.py:160
  76.0 9.9 %collective-permute-start.13 = (bf16[384,256]{1,0:T(8,128)(2,1)S(1)}, bf16[384,256]{1,0:T(8,128)(2,1)S(1)}, u32[]{:S(2)}, u32[]{:S(2)}) collective-permute-start(bf16[384,256]{1,0:T(8,128)(2,1)S(1)} %get-tuple-element.11), channel_id=1, source_target_pairs={{0,1},{1,2},{2,3},{3,0},{4,5},{5,6},{6,7},{7,4},{8,9},{9,10},{10,1... | collective-permute-start | bytes 589832 | tf_op jit(solution)/shard_map/ppermute | solution.py:160
  76.0 9.9 %collective-permute-start.14 = (bf16[384,256]{1,0:T(8,128)(2,1)S(1)}, bf16[384,256]{1,0:T(8,128)(2,1)S(1)}, u32[]{:S(2)}, u32[]{:S(2)}) collective-permute-start(bf16[384,256]{1,0:T(8,128)(2,1)S(1)} %get-tuple-element.10), channel_id=1, source_target_pairs={{0,3},{1,0},{2,1},{3,2},{4,7},{5,4},{6,5},{7,6},{8,11},{9,8},{10,9... | collective-permute-start | bytes 589832 | tf_op jit(solution)/shard_map/ppermute | solution.py:160
where the time goes:
time: 88.2 us; the launch traced here: 87.8 us
  starting transfers between devices  34.5 us (39%)
  Pallas kernels  25.5 us (29%)
  waiting for transfers between devices  16.6 us (19%)
  other arithmetic  5.34 us (6%)
  local copies, waits for them, and re-layouts  4.4 us (5%)
  matrix products  1.21 us (1%)
    pallas_call x4, Pallas kernels, add_grads(): pl.pallas_call(functools.partial(grads_kernel, blocks, len(payloads), boo...  21.9 us
    ppermute x10, starting transfers between devices, shift_by(): lax.ppermute(value, axis, [(i, (i + step * inner) % size) for i in range(...  21.3 us
    ppermute x10, waiting for transfers between devices, shift_by(): lax.ppermute(value, axis, [(i, (i + step * inner) % size) for i in range(...  14.3 us
    ppermute x5, starting transfers between devices, swap(): return lax.ppermute(value, axis, [(i, i ^ bit) for i in range(size)])  13.2 us
    pallas_call x1, Pallas kernels, body(): pl.pallas_call(digits_kernel, out_shape=jax.ShapeDtypeStruct((EXTRA, 256)...  3.62 us
    unnamed x18, local copies, waits for them, and re-layouts  3.16 us
    ppermute x5, waiting for transfers between devices, swap(): return lax.ppermute(value, axis, [(i, i ^ bit) for i in range(size)])  2.34 us
    mul x1, other arithmetic, body(): return total * SCALE  1.89 us
  transfers between devices with their start and end apart: 15, of which 5 were waited for; matrix products, arithmetic and copies ran while one was open for 3% of the time, Pallas kernels for 24%

commit v1 on v0

--- a/solution.py
+++ b/solution.py
@@ -14,7 +14,8 @@
 PAIR = 2 * OWN
 MIDDLE = 192
 SCALE = 1.0 / 256.0
-LINK = jnp.bfloat16
+GRANT = 8
+LINK = jnp.float16
 NOWHERE = -250.0
 
 
@@ -98,56 +99,39 @@
 
 def grads_kernel(blocks, payloads, adds, where_ref, *refs):
     count = len(blocks)
-    given = count + payloads + count * adds
-    sources, refs = refs[:given], refs[given:]
-    outs, refs = refs[:count], refs[count:]
-    held, (words_ref, word_ref, bit_ref, sem) = refs[:given], refs[given:]
-    copies = [
-        pltpu.make_async_copy(source, hold, sem.at[i])
-        for i, (source, hold) in enumerate(zip(sources, held))
-    ]
-    payload_refs = held[count : count + payloads]
-    for copy in copies[count : count + payloads] + copies[:count] + copies[count + payloads :]:
-        copy.start()
-    for copy in copies[count : count + payloads]:
-        copy.wait()
+    factors, refs = refs[:count], refs[count:]
+    payload_refs, refs = refs[:payloads], refs[payloads:]
+    olds, refs = refs[: count * adds], refs[count * adds :]
+    outs, (words_ref, word_ref, bit_ref) = refs[:count], refs[count:]
     for i, which in enumerate(blocks):
         build_words(where_ref[which], payload_refs, words_ref, word_ref, bit_ref)
-        copies[i].wait()
-        value = block_grads(held[i], payload_refs, words_ref)
-        if adds:
-            copies[count + payloads + i].wait()
-            value = held[count + payloads + i][...] + value
-        outs[i][...] = value
+        value = block_grads(factors[i], payload_refs, words_ref)
+        outs[i][...] = olds[i][...] + value if adds else value
 
 
 VMEM = pl.BlockSpec(memory_space=pltpu.VMEM)
 SMEM = pl.BlockSpec(memory_space=pltpu.SMEM)
-ANY = pl.BlockSpec(memory_space=pl.ANY)
 
 
 def add_grads(where, blocks, factors, payloads, olds=()):
     rows = factors[0].shape[0]
     pairs = sum(payload.shape[0] for payload in payloads)
     work = len(blocks) * rows * pairs * PAIR
-    operands = (*factors, *payloads, *olds)
     return pl.pallas_call(
         functools.partial(grads_kernel, blocks, len(payloads), bool(olds)),
         out_shape=[jax.ShapeDtypeStruct((rows, 256), jnp.float32)] * len(blocks),
-        in_specs=[SMEM] + [ANY] * len(operands),
+        in_specs=[SMEM] + [VMEM] * (len(blocks) + len(payloads) + len(olds)),
         out_specs=[VMEM] * len(blocks),
-        scratch_shapes=[pltpu.VMEM(operand.shape, operand.dtype) for operand in operands]
-        + [
+        scratch_shapes=[
             pltpu.VMEM((pairs, rows // 32, 128), jnp.int32),
             pltpu.VMEM((pairs, SLOTS, 128), jnp.int32),
             pltpu.VMEM((pairs, SLOTS, 128), jnp.int32),
-            pltpu.SemaphoreType.DMA((len(operands),)),
         ],
-        compiler_params=pltpu.CompilerParams(vmem_limit_bytes=60 * 1024 * 1024),
+        compiler_params=pltpu.CompilerParams(vmem_limit_bytes=GRANT * 1024 * 1024),
         cost_estimate=pl.CostEstimate(
             flops=4 * work * 256, bytes_accessed=1 << 22, transcendentals=work
         ),
-    )(where, *operands)
+    )(where, *factors, *payloads, *olds)
 
 
 def swap(value, axis, bit):
@@ -158,6 +142,13 @@
 def shift_by(value, axis, step, inner=1):
     size = lax.axis_size(axis)
     return lax.ppermute(value, axis, [(i, (i + step * inner) % size) for i in range(size)])
+
+
+def turn(value, step):
+    size = lax.axis_size("label")
+    return lax.ppermute(
+        value, "label", [(i, (i + (2 - 4 * (i % 2)) * step) % size) for i in range(size)]
+    )
 
 
 def body(queries, basis, factors, positives, counts, placement):
@@ -174,7 +165,9 @@
         out_shape=jax.ShapeDtypeStruct((EXTRA, 256), jnp.bfloat16),
         in_specs=[SMEM, VMEM, VMEM, VMEM],
         out_specs=VMEM,
-        cost_estimate=pl.CostEstimate(flops=1 << 31, bytes_accessed=1 << 19, transcendentals=0),
+        cost_estimate=pl.CostEstimate(
+            flops=1 << 31, bytes_accessed=1 << 19, transcendentals=0
+        ),
     )(
         jnp.stack([(half - part * OWN) & 255, half]).astype(jnp.int32),
         positives.T,
@@ -182,13 +175,14 @@
         placement.reshape(-1, 128),
     )
 
-    rows = partial_value
-    for bit in (2, 1):
-        count = rows.shape[0] // 2
-        high = (part >> (bit - 1)) & 1
-        keep = lax.dynamic_slice_in_dim(rows, high * count, count, 0)
-        send = lax.dynamic_slice_in_dim(rows, (1 - high) * count, count, 0)
-        rows = keep + swap(send, "basis", bit)
+    def piece_of(value, step):
+        count = value.shape[0] // lax.axis_size("basis")
+        return lax.dynamic_slice_in_dim(value, ((part + step) & 3) * count, count, 0)
+
+    rows = piece_of(partial_value, 0)
+    moved = [shift_by(piece_of(partial_value, step), "basis", step) for step in (2, 1, 3)]
+    for value in moved:
+        rows = rows + value
     own = jnp.concatenate([rows.astype(jnp.bfloat16), digits], axis=0)
     next_own = swap(own, "dp", 1)
     even = dp & 1 == 0
@@ -205,31 +199,25 @@
     first = label * factors.shape[0] + dp * block
     other = (label ^ 1) * factors.shape[0] + dp * block
     where = jnp.stack([first, other]).astype(jnp.int32)
-    half_ring = ring.shape[0] // 2
-    near = [shift_by(ring, "label", step, 2) for step in (1, 3)]
-    far = [
-        shift_by(near[0][:half_ring], "label", 1, 2),
-        shift_by(near[1][half_ring:], "label", 3, 2),
-    ]
+    near = [turn(ring, 1), turn(ring, -1)]
+    far = [turn(near[0], 1)]
     sum_mine, sum_other = add_grads(where, (0, 1), (mine, others), (ring,))
     (sum_other,) = add_grads(where, (1,), (others,), near, (sum_other,))
     (sum_other,) = add_grads(where, (1,), (others,), far, (sum_other,))
     received = swap(sum_other, "label", 1)
     (sum_mine,) = add_grads(where, (0,), (mine,), near + far, (sum_mine,))
 
-    quarter = block // lax.axis_size("basis")
-
-    def quarter_of(step):
-        start = ((part + step) & 3) * quarter
-        return lax.dynamic_slice_in_dim(sum_mine, start, quarter, 0) + lax.dynamic_slice_in_dim(
-            received, start, quarter, 0
-        )
-
-    total = quarter_of(0)
-    for step in (2, 1, 3):
-        sent = (quarter_of(step) * SCALE).astype(LINK)
-        total = total + shift_by(sent, "basis", step).astype(jnp.float32) * (1 / SCALE)
-    return total * SCALE
+    order = (2, 1, 3)
+    quarters = [piece_of(sum_mine, step) + piece_of(received, step) for step in (0,) + order]
+    total, *sent = lax.optimization_barrier(
+        (quarters[0], *((value * SCALE).astype(LINK) for value in quarters[1:]))
+    )
+    total = total * SCALE
+    for i, step in enumerate(order):
+        total = total + shift_by(sent[i], "basis", step).astype(jnp.float32)
+        if i == 0:
+            total = lax.optimization_barrier(total)
+    return total
 
 
 def solution(mesh):

time: 88.2 us -> 76.7 us (0.87)
  the two profiles are of different devices: /device:TPU:33 before, /device:TPU:1 now
where the time goes in v1:
time: 76.7 us; the launch traced here: 76.3 us
  starting transfers between devices  27.8 us (36%)
  waiting for transfers between devices  20 us (26%)
  Pallas kernels  15.5 us (20%)
  local copies, waits for them, and re-layouts  7.63 us (10%)
  other arithmetic  3.95 us (5%)
  matrix products  1.21 us (2%)
    ppermute x9, starting transfers between devices, shift_by(): lax.ppermute(value, axis, [(i, (i + step * inner) % size) for i in range(...  16.7 us
    ppermute x9, waiting for transfers between devices, shift_by(): lax.ppermute(value, axis, [(i, (i + step * inner) % size) for i in range(...  15.1 us
    pallas_call x4, Pallas kernels, add_grads(): pl.pallas_call(functools.partial(grads_kernel, blocks, len(payloads), boo...  11.9 us
    unnamed x20, local copies, waits for them, and re-layouts  6.43 us
    ppermute x3, starting transfers between devices, turn(): lax.ppermute(value, 'label', [(i, (i + (2 - 4 * (i % 2)) * step) % size)...  5.97 us
    ppermute x3, starting transfers between devices, swap(): return lax.ppermute(value, axis, [(i, i ^ bit) for i in range(size)])  5.15 us
    ppermute x3, waiting for transfers between devices, turn(): lax.ppermute(value, 'label', [(i, (i + (2 - 4 * (i % 2)) * step) % size)...  4.91 us
    pallas_call x1, Pallas kernels, body(): pl.pallas_call(digits_kernel, out_shape=jax.ShapeDtypeStruct((EXTRA, 256)...  3.62 us
  transfers between devices with their start and end apart: 15, of which 4 were waited for; matrix products, arithmetic and copies ran while one was open for 3% of the time, Pallas kernels for 18%

profile of v1, /device:TPU:1, one launch (start us, length us, event | category | flops | bytes accessed | tf_op | source)
XLA Modules:
  0.0 76.3 jit_solution(8505599087327381756)
XLA Ops:
  1.0 1.2 %fusion = f32[256,256]{1,0:T(8,128)S(1)} fusion(bf16[256,512]{1,0:T(8,128)(2,1)S(1)} %copy-done, bf16[256,512]{1,0:T(8,128)(2,1)} %param.7), kind=kOutput, calls=%fused_computation.19 | convolution fusion | flops 67108864 | bytes 786432 | tf_op jit(solution)/shard_map/dot_general | solution.py:159
  2.2 3.8 %collective-permute-start = (f32[64,256]{1,0:T(8,128)S(1)}, f32[64,256]{1,0:T(8,128)S(1)}, u32[]{:S(2)}, u32[]{:S(2)}) collective-permute-start(f32[64,256]{1,0:T(8,128)S(1)} %get-tuple-element.21), channel_id=1, source_target_pairs={{0,2},{1,3},{2,0},{3,1},{4,6},{5,7},{6,4},{7,5},{8,10},{9,11},{10,... | collective-permute-start | bytes 196616 | tf_op jit(solution)/shard_map/ppermute | solution.py:144
  8.1 3.6 %shard_map.64 = bf16[16,256]{1,0:T(8,128)(2,1)} custom-call(s32[2]{0:T(128)} %pad_add_fusion.1.where_ref, s32[16,256]{1,0:T(8,128)} %bitcast.12, s32[1,256]{1,0:T(1,128)} %bitcast.13, s32[768,128]{1,0:T(8,128)} %bitcast.11), custom_call_target="tpu_custom_call" | custom-call | flops 2147483648 | bytes 524288 | tf_op jit(solution)/shard_map/pallas_call | solution.py:163
  12.5 1.6 %collective-permute-start.3 = (bf16[80,256]{1,0:T(8,128)(2,1)S(1)}, bf16[80,256]{1,0:T(8,128)(2,1)S(1)}, u32[]{:S(2)}, u32[]{:S(2)}) collective-permute-start(bf16[80,256]{1,0:T(8,128)(2,1)S(1)} %pad_maximum_fusion.1), channel_id=1, source_target_pairs={{0,4},{4,0},{8,12},{12,8},{16,20},{20,16},{24,28},{28,24},{1,5},{5... | collective-permute-start | bytes 122888 | tf_op jit(solution)/shard_map/ppermute | solution.py:139
  14.1 1.2 %constant_dynamic-slice_fusion.3.refs_0_ = bf16[1536,256]{1,0:T(8,128)(2,1)S(1)} fusion(bf16[12288,256]{1,0:T(8,128)(2,1)} %param.8, s32[]{:T(128)S(6)} %select_n.43), kind=kLoop, calls=%fused_computation.16 | loop fusion | bytes 1572868 | tf_op jit(solution)/shard_map/dynamic_slice | solution.py:158
  15.3 2.1 %collective-permute-start.10 = (bf16[1536,256]{1,0:T(8,128)(2,1)S(1)}, bf16[1536,256]{1,0:T(8,128)(2,1)S(1)}, u32[]{:S(2)}, u32[]{:S(2)}) collective-permute-start(bf16[1536,256]{1,0:T(8,128)(2,1)S(1)} %constant_dynamic-slice_fusion.3.refs_0_), channel_id=1, source_target_pairs={{0,32},{32,0},{64,96},{96,64},{128,160},{160,128},{192,224},{224,1... | collective-permute-start | bytes 2359304 | tf_op jit(solution)/shard_map/ppermute | solution.py:139
  17.5 6.1 %collective-permute-start.6 = (bf16[1,144,256]{2,1,0:T(8,128)(2,1)S(1)}, bf16[1,144,256]{2,1,0:T(8,128)(2,1)S(1)}, u32[]{:S(2)}, u32[]{:S(2)}) collective-permute-start(bf16[1,144,256]{2,1,0:T(8,128)(2,1)S(1)} %maximum_bitcast_fusion), channel_id=1, source_target_pairs={{0,16},{4,20},{8,24},{12,28},{16,0},{20,4},{24,8},{28,12},{1,17},{... | collective-permute-start | bytes 221192 | tf_op jit(solution)/shard_map/ppermute | solution.py:144
  23.8 2.1 %collective-permute-start.4 = (bf16[1,144,256]{2,1,0:T(8,128)(2,1)S(1)}, bf16[1,144,256]{2,1,0:T(8,128)(2,1)S(1)}, u32[]{:S(2)}, u32[]{:S(2)}) collective-permute-start(bf16[1,144,256]{2,1,0:T(8,128)(2,1)S(1)} %maximum_bitcast_fusion), channel_id=1, source_target_pairs={{0,8},{4,12},{8,16},{12,20},{16,24},{20,28},{24,0},{28,4},{1,9},{5... | collective-permute-start | bytes 221192 | tf_op jit(solution)/shard_map/ppermute | solution.py:144
  25.9 5.7 %collective-permute-done.5 = bf16[1,144,256]{2,1,0:T(8,128)(2,1)S(1)} collective-permute-done((bf16[1,144,256]{2,1,0:T(8,128)(2,1)S(1)}, bf16[1,144,256]{2,1,0:T(8,128)(2,1)S(1)}, u32[]{:S(2)}, u32[]{:S(2)}) %collective-permute-start.5) | collective-permute-done | bytes 73760 | tf_op jit(solution)/shard_map/ppermute | solution.py:144
  31.6 2.6 %collective-permute-start.7 = (bf16[4,144,256]{2,1,0:T(8,128)(2,1)S(1)}, bf16[4,144,256]{2,1,0:T(8,128)(2,1)S(1)}, u32[]{:S(2)}, u32[]{:S(2)}) collective-permute-start(bf16[4,144,256]{2,1,0:T(8,128)(2,1)S(1)} %pad_maximum_fusion.refs_2_), channel_id=1, source_target_pairs={{0,64},{32,224},{64,128},{96,32},{128,192},{160,96},{192,0},{224,1... | collective-permute-start | bytes 884744 | tf_op jit(solution)/shard_map/ppermute | solution.py:149
  34.3 4.9 %collective-permute-done.7.refs_1_ = bf16[4,144,256]{2,1,0:T(8,128)(2,1)S(1)} collective-permute-done((bf16[4,144,256]{2,1,0:T(8,128)(2,1)S(1)}, bf16[4,144,256]{2,1,0:T(8,128)(2,1)S(1)}, u32[]{:S(2)}, u32[]{:S(2)}) %collective-permute-start.7) | collective-permute-done | bytes 294944 | tf_op jit(solution)/shard_map/ppermute | solution.py:149
  39.2 3.4 %collective-permute-start.9 = (bf16[4,144,256]{2,1,0:T(8,128)(2,1)S(1)}, bf16[4,144,256]{2,1,0:T(8,128)(2,1)S(1)}, u32[]{:S(2)}, u32[]{:S(2)}) collective-permute-start(bf16[4,144,256]{2,1,0:T(8,128)(2,1)S(1)} %collective-permute-done.7.refs_1_), channel_id=1, source_target_pairs={{0,64},{32,224},{64,128},{96,32},{128,192},{160,96},{192,0},{224,1... | collective-permute-start | bytes 884744 | tf_op jit(solution)/shard_map/ppermute | solution.py:149
  42.6 3.2 %shard_map.65 = (f32[1536,256]{1,0:T(8,128)S(1)}, f32[1536,256]{1,0:T(8,128)S(1)}) custom-call(s32[2]{0:T(128)S(1)} %pad_add_fusion.where_ref, bf16[1536,256]{1,0:T(8,128)(2,1)S(1)} %constant_dynamic-slice_fusion.3.refs_0_, bf16[1536,256]{1,0:T(8,128)(2,1)S(1)} %collective-permute-done.10.refs_1_.refs_0_, bf16[4,144,256]{2,1,0:T(8,128)(2,1)S(1)} %pad_maximum_fusion.refs_2_), custom_call_target="tpu_custom_call" | custom-call | flops 1610612736 | bytes 4194304 | tf_op jit(solution)/shard_map/pallas_call | solution.py:120
  45.8 1.2 %copy-done.7 = f32[1536,256]{1,0:T(8,128)} copy-done((f32[1536,256]{1,0:T(8,128)}, f32[1536,256]{1,0:T(8,128)S(1)}, u32[]{:S(2)}) %copy-start.7) | copy-done | bytes 1572888
  47.0 2.9 %shard_map.67.refs_2_ = f32[1536,256]{1,0:T(8,128)S(1)} custom-call(s32[2]{0:T(128)S(1)} %pad_add_fusion.where_ref, bf16[1536,256]{1,0:T(8,128)(2,1)S(1)} %collective-permute-done.10.refs_1_.refs_0_, bf16[4,144,256]{2,1,0:T(8,128)(2,1)S(1)} %collective-permute-done.7.refs_1_, bf16[4,144,256]{2,1,0:T(8,128)(2,1)S(1)} %collective-permute-done.8.refs_2_, ...), custom_call_target="tpu_custom_call" | custom-call | flops 1610612736 | bytes 4194304 | tf_op jit(solution)/shard_map/pallas_call | solution.py:120
  49.9 1.9 %shard_map.68 = f32[1536,256]{1,0:T(8,128)S(1)} custom-call(s32[2]{0:T(128)S(1)} %pad_add_fusion.where_ref, bf16[1536,256]{1,0:T(8,128)(2,1)S(1)} %collective-permute-done.10.refs_1_.refs_0_, bf16[4,144,256]{2,1,0:T(8,128)(2,1)S(1)} %collective-permute-done.9.refs_3_.refs_1_, f32[1536,256]{1,0:T(8,128)S(1)} %shard_map.67.refs_2_), custom_call_target="tpu_custom_call" | custom-call | flops 805306368 | bytes 4194304 | tf_op jit(solution)/shard_map/pallas_call | solution.py:120
  51.8 1.4 %collective-permute-start.11 = (f32[1536,256]{1,0:T(8,128)S(1)}, f32[1536,256]{1,0:T(8,128)}, u32[]{:S(2)}, u32[]{:S(2)}) collective-permute-start(f32[1536,256]{1,0:T(8,128)S(1)} %shard_map.68), channel_id=1, source_target_pairs={{0,32},{32,0},{64,96},{96,64},{128,160},{160,128},{192,224},{224,1... | collective-permute-start | bytes 4718600 | tf_op jit(solution)/shard_map/ppermute | solution.py:139
  53.2 1.0 %copy-done.2 = bf16[4,144,256]{2,1,0:T(8,128)(2,1)S(1)} copy-done((bf16[4,144,256]{2,1,0:T(8,128)(2,1)S(1)}, bf16[4,144,256]{2,1,0:T(8,128)(2,1)}, u32[]{:S(2)}) %copy-start.2) | copy-done | bytes 294936
  56.1 1.4 %copy-done.8 = f32[1536,256]{1,0:T(8,128)S(1)} copy-done((f32[1536,256]{1,0:T(8,128)S(1)}, f32[1536,256]{1,0:T(8,128)}, u32[]{:S(2)}) %copy-start.8) | copy-done | bytes 1572888
  57.5 3.9 %shard_map.66 = f32[1536,256]{1,0:T(8,128)S(1)} custom-call(s32[2]{0:T(128)S(1)} %pad_add_fusion.where_ref, bf16[1536,256]{1,0:T(8,128)(2,1)S(1)} %constant_dynamic-slice_fusion.3.refs_0_, bf16[4,144,256]{2,1,0:T(8,128)(2,1)S(1)} %copy-done.4, bf16[4,144,256]{2,1,0:T(8,128)(2,1)S(1)} %copy-done.6, bf16[4,144,256]{2,1,0:T(8,128)(2,1)S(1)} %copy-done.2, ...), custom_call_target="tpu_custom_call" | custom-call | flops 2415919104 | bytes 4194304 | tf_op jit(solution)/shard_map/pallas_call | solution.py:120
  61.4 1.6 %multiply_convert_fusion = (f16[384,256]{1,0:T(8,128)(2,1)S(1)}, f16[384,256]{1,0:T(8,128)(2,1)S(1)}, f16[384,256]{1,0:T(8,128)(2,1)S(1)}, f32[384,256]{1,0:T(8,128)S(1)}) fusion(f32[1536,256]{1,0:T(8,128)} %collective-permute-done.11, s32[]{:T(128)S(6)} %select_n.54, f32[1536,256]{1,0:T(8,128)S(1)} %shard_map.66, s32[]{:T(128)S(6)} %select_n.53, ...), kind=kLoop, calls=%fused_computation.2 | loop fusion | flops 983040 | bytes 4128784 | tf_op jit(solution)/shard_map/convert_element_type | solution.py:213
  63.4 2.1 %collective-permute-start.13 = (f16[384,256]{1,0:T(8,128)(2,1)S(1)}, f16[384,256]{1,0:T(8,128)(2,1)S(1)}, u32[]{:S(2)}, u32[]{:S(2)}) collective-permute-start(f16[384,256]{1,0:T(8,128)(2,1)S(1)} %get-tuple-element.15), channel_id=1, source_target_pairs={{0,1},{1,2},{2,3},{3,0},{4,5},{5,6},{6,7},{7,4},{8,9},{9,10},{10,1... | collective-permute-start | bytes 589832 | tf_op jit(solution)/shard_map/ppermute | solution.py:144
  66.0 5.1 %collective-permute-done.12 = f16[384,256]{1,0:T(8,128)(2,1)S(1)} collective-permute-done((f16[384,256]{1,0:T(8,128)(2,1)S(1)}, f16[384,256]{1,0:T(8,128)(2,1)S(1)}, u32[]{:S(2)}, u32[]{:S(2)}) %collective-permute-start.12) | collective-permute-done | bytes 196640 | tf_op jit(solution)/shard_map/ppermute | solution.py:144
  71.2 4.3 %collective-permute-done.13 = f16[384,256]{1,0:T(8,128)(2,1)S(1)} collective-permute-done((f16[384,256]{1,0:T(8,128)(2,1)S(1)}, f16[384,256]{1,0:T(8,128)(2,1)S(1)}, u32[]{:S(2)}, u32[]{:S(2)}) %collective-permute-start.13) | collective-permute-done | bytes 196640 | tf_op jit(solution)/shard_map/ppermute | solution.py:144
  (45 shorter events, 7.9 us)
Async XLA Ops:
  2.2 9.5 %collective-permute-start = (f32[64,256]{1,0:T(8,128)S(1)}, f32[64,256]{1,0:T(8,128)S(1)}, u32[]{:S(2)}, u32[]{:S(2)}) collective-permute-start(f32[64,256]{1,0:T(8,128)S(1)} %get-tuple-element.21), channel_id=1, source_target_pairs={{0,2},{1,3},{2,0},{3,1},{4,6},{5,7},{6,4},{7,5},{8,10},{9,11},{10,... | collective-permute-start | bytes 196616 | tf_op jit(solution)/shard_map/ppermute | solution.py:144
  6.0 5.7 %collective-permute-start.2 = (f32[64,256]{1,0:T(8,128)S(1)}, f32[64,256]{1,0:T(8,128)S(1)}, u32[]{:S(2)}, u32[]{:S(2)}) collective-permute-start(f32[64,256]{1,0:T(8,128)S(1)} %get-tuple-element.22), channel_id=1, source_target_pairs={{0,3},{1,0},{2,1},{3,2},{4,7},{5,4},{6,5},{7,6},{8,11},{9,8},{10,9... | collective-permute-start | bytes 196616 | tf_op jit(solution)/shard_map/ppermute | solution.py:144
  6.8 4.9 %collective-permute-start.1 = (f32[64,256]{1,0:T(8,128)S(1)}, f32[64,256]{1,0:T(8,128)S(1)}, u32[]{:S(2)}, u32[]{:S(2)}) collective-permute-start(f32[64,256]{1,0:T(8,128)S(1)} %get-tuple-element.23), channel_id=1, source_target_pairs={{0,1},{1,2},{2,3},{3,0},{4,5},{5,6},{6,7},{7,4},{8,9},{9,10},{10,1... | collective-permute-start | bytes 196616 | tf_op jit(solution)/shard_map/ppermute | solution.py:144
  11.7 5.7 %copy-start.9 = (bf16[16,256]{1,0:T(8,128)(2,1)S(1)}, bf16[16,256]{1,0:T(8,128)(2,1)}, u32[]{:S(2)}) copy-start(bf16[16,256]{1,0:T(8,128)(2,1)} %shard_map.64) | copy-start | bytes 24580
  12.5 4.9 %collective-permute-start.3 = (bf16[80,256]{1,0:T(8,128)(2,1)S(1)}, bf16[80,256]{1,0:T(8,128)(2,1)S(1)}, u32[]{:S(2)}, u32[]{:S(2)}) collective-permute-start(bf16[80,256]{1,0:T(8,128)(2,1)S(1)} %pad_maximum_fusion.1), channel_id=1, source_target_pairs={{0,4},{4,0},{8,12},{12,8},{16,20},{20,16},{24,28},{28,24},{1,5},{5... | collective-permute-start | bytes 122888 | tf_op jit(solution)/shard_map/ppermute | solution.py:139
  15.3 27.3 %collective-permute-start.10 = (bf16[1536,256]{1,0:T(8,128)(2,1)S(1)}, bf16[1536,256]{1,0:T(8,128)(2,1)S(1)}, u32[]{:S(2)}, u32[]{:S(2)}) collective-permute-start(bf16[1536,256]{1,0:T(8,128)(2,1)S(1)} %constant_dynamic-slice_fusion.3.refs_0_), channel_id=1, source_target_pairs={{0,32},{32,0},{64,96},{96,64},{128,160},{160,128},{192,224},{224,1... | collective-permute-start | bytes 2359304 | tf_op jit(solution)/shard_map/ppermute | solution.py:139
  17.5 8.5 %collective-permute-start.6 = (bf16[1,144,256]{2,1,0:T(8,128)(2,1)S(1)}, bf16[1,144,256]{2,1,0:T(8,128)(2,1)S(1)}, u32[]{:S(2)}, u32[]{:S(2)}) collective-permute-start(bf16[1,144,256]{2,1,0:T(8,128)(2,1)S(1)} %maximum_bitcast_fusion), channel_id=1, source_target_pairs={{0,16},{4,20},{8,24},{12,28},{16,0},{20,4},{24,8},{28,12},{1,17},{... | collective-permute-start | bytes 221192 | tf_op jit(solution)/shard_map/ppermute | solution.py:144
  23.6 8.0 %collective-permute-start.5 = (bf16[1,144,256]{2,1,0:T(8,128)(2,1)S(1)}, bf16[1,144,256]{2,1,0:T(8,128)(2,1)S(1)}, u32[]{:S(2)}, u32[]{:S(2)}) collective-permute-start(bf16[1,144,256]{2,1,0:T(8,128)(2,1)S(1)} %maximum_bitcast_fusion), channel_id=1, source_target_pairs={{0,24},{4,28},{8,0},{12,4},{16,8},{20,12},{24,16},{28,20},{1,25},{... | collective-permute-start | bytes 221192 | tf_op jit(solution)/shard_map/ppermute | solution.py:144
  23.8 7.8 %collective-permute-start.4 = (bf16[1,144,256]{2,1,0:T(8,128)(2,1)S(1)}, bf16[1,144,256]{2,1,0:T(8,128)(2,1)S(1)}, u32[]{:S(2)}, u32[]{:S(2)}) collective-permute-start(bf16[1,144,256]{2,1,0:T(8,128)(2,1)S(1)} %maximum_bitcast_fusion), channel_id=1, source_target_pairs={{0,8},{4,12},{8,16},{12,20},{16,24},{20,28},{24,0},{28,4},{1,9},{5... | collective-permute-start | bytes 221192 | tf_op jit(solution)/shard_map/ppermute | solution.py:144
  31.6 7.5 %collective-permute-start.7 = (bf16[4,144,256]{2,1,0:T(8,128)(2,1)S(1)}, bf16[4,144,256]{2,1,0:T(8,128)(2,1)S(1)}, u32[]{:S(2)}, u32[]{:S(2)}) collective-permute-start(bf16[4,144,256]{2,1,0:T(8,128)(2,1)S(1)} %pad_maximum_fusion.refs_2_), channel_id=1, source_target_pairs={{0,64},{32,224},{64,128},{96,32},{128,192},{160,96},{192,0},{224,1... | collective-permute-start | bytes 884744 | tf_op jit(solution)/shard_map/ppermute | solution.py:149
  34.2 12.8 %collective-permute-start.8 = (bf16[4,144,256]{2,1,0:T(8,128)(2,1)S(1)}, bf16[4,144,256]{2,1,0:T(8,128)(2,1)S(1)}, u32[]{:S(2)}, u32[]{:S(2)}) collective-permute-start(bf16[4,144,256]{2,1,0:T(8,128)(2,1)S(1)} %pad_maximum_fusion.refs_2_), channel_id=1, source_target_pairs={{0,192},{32,96},{64,0},{96,160},{128,64},{160,224},{192,128},{224,... | collective-permute-start | bytes 884744 | tf_op jit(solution)/shard_map/ppermute | solution.py:149
  39.2 7.8 %copy-start.3 = (bf16[4,144,256]{2,1,0:T(8,128)(2,1)}, bf16[4,144,256]{2,1,0:T(8,128)(2,1)S(1)}, u32[]{:S(2)}) copy-start(bf16[4,144,256]{2,1,0:T(8,128)(2,1)S(1)} %collective-permute-done.7.refs_1_) | copy-start | bytes 884740
  39.2 10.7 %collective-permute-start.9 = (bf16[4,144,256]{2,1,0:T(8,128)(2,1)S(1)}, bf16[4,144,256]{2,1,0:T(8,128)(2,1)S(1)}, u32[]{:S(2)}, u32[]{:S(2)}) collective-permute-start(bf16[4,144,256]{2,1,0:T(8,128)(2,1)S(1)} %collective-permute-done.7.refs_1_), channel_id=1, source_target_pairs={{0,64},{32,224},{64,128},{96,32},{128,192},{160,96},{192,0},{224,1... | collective-permute-start | bytes 884744 | tf_op jit(solution)/shard_map/ppermute | solution.py:149
  45.8 1.2 %copy-start.7 = (f32[1536,256]{1,0:T(8,128)}, f32[1536,256]{1,0:T(8,128)S(1)}, u32[]{:S(2)}) copy-start(f32[1536,256]{1,0:T(8,128)S(1)} %get-tuple-element.11.refs_4_) | copy-start | bytes 4718596
  47.0 2.9 %copy-start.5 = (bf16[4,144,256]{2,1,0:T(8,128)(2,1)}, bf16[4,144,256]{2,1,0:T(8,128)(2,1)S(1)}, u32[]{:S(2)}) copy-start(bf16[4,144,256]{2,1,0:T(8,128)(2,1)S(1)} %collective-permute-done.8.refs_2_) | copy-start | bytes 884740
  49.9 1.9 %copy-start.1 = (bf16[4,144,256]{2,1,0:T(8,128)(2,1)}, bf16[4,144,256]{2,1,0:T(8,128)(2,1)S(1)}, u32[]{:S(2)}) copy-start(bf16[4,144,256]{2,1,0:T(8,128)(2,1)S(1)} %collective-permute-done.9.refs_3_.refs_1_) | copy-start | bytes 884740
  51.8 9.6 %collective-permute-start.11 = (f32[1536,256]{1,0:T(8,128)S(1)}, f32[1536,256]{1,0:T(8,128)}, u32[]{:S(2)}, u32[]{:S(2)}) collective-permute-start(f32[1536,256]{1,0:T(8,128)S(1)} %shard_map.68), channel_id=1, source_target_pairs={{0,32},{32,0},{64,96},{96,64},{128,160},{160,128},{192,224},{224,1... | collective-permute-start | bytes 4718600 | tf_op jit(solution)/shard_map/ppermute | solution.py:139
  53.2 1.0 %copy-start.2 = (bf16[4,144,256]{2,1,0:T(8,128)(2,1)S(1)}, bf16[4,144,256]{2,1,0:T(8,128)(2,1)}, u32[]{:S(2)}) copy-start(bf16[4,144,256]{2,1,0:T(8,128)(2,1)} %copy-done.1) | copy-start | bytes 884740
  54.2 1.0 %copy-start.4 = (bf16[4,144,256]{2,1,0:T(8,128)(2,1)S(1)}, bf16[4,144,256]{2,1,0:T(8,128)(2,1)}, u32[]{:S(2)}) copy-start(bf16[4,144,256]{2,1,0:T(8,128)(2,1)} %copy-done.3) | copy-start | bytes 884740
  55.1 1.0 %copy-start.6 = (bf16[4,144,256]{2,1,0:T(8,128)(2,1)S(1)}, bf16[4,144,256]{2,1,0:T(8,128)(2,1)}, u32[]{:S(2)}) copy-start(bf16[4,144,256]{2,1,0:T(8,128)(2,1)} %copy-done.5) | copy-start | bytes 884740
  56.1 1.4 %copy-start.8 = (f32[1536,256]{1,0:T(8,128)S(1)}, f32[1536,256]{1,0:T(8,128)}, u32[]{:S(2)}) copy-start(f32[1536,256]{1,0:T(8,128)} %copy-done.7) | copy-start | bytes 4718596
  63.0 8.1 %collective-permute-start.12 = (f16[384,256]{1,0:T(8,128)(2,1)S(1)}, f16[384,256]{1,0:T(8,128)(2,1)S(1)}, u32[]{:S(2)}, u32[]{:S(2)}) collective-permute-start(f16[384,256]{1,0:T(8,128)(2,1)S(1)} %get-tuple-element.14), channel_id=1, source_target_pairs={{0,2},{1,3},{2,0},{3,1},{4,6},{5,7},{6,4},{7,5},{8,10},{9,11},{10,... | collective-permute-start | bytes 589832 | tf_op jit(solution)/shard_map/ppermute | solution.py:144
  63.4 12.2 %collective-permute-start.13 = (f16[384,256]{1,0:T(8,128)(2,1)S(1)}, f16[384,256]{1,0:T(8,128)(2,1)S(1)}, u32[]{:S(2)}, u32[]{:S(2)}) collective-permute-start(f16[384,256]{1,0:T(8,128)(2,1)S(1)} %get-tuple-element.15), channel_id=1, source_target_pairs={{0,1},{1,2},{2,3},{3,0},{4,5},{5,6},{6,7},{7,4},{8,9},{9,10},{10,1... | collective-permute-start | bytes 589832 | tf_op jit(solution)/shard_map/ppermute | solution.py:144
  65.5 10.1 %collective-permute-start.14 = (f16[384,256]{1,0:T(8,128)(2,1)S(1)}, f16[384,256]{1,0:T(8,128)(2,1)S(1)}, u32[]{:S(2)}, u32[]{:S(2)}) collective-permute-start(f16[384,256]{1,0:T(8,128)(2,1)S(1)} %get-tuple-element.16), channel_id=1, source_target_pairs={{0,3},{1,0},{2,1},{3,2},{4,7},{5,4},{6,5},{7,6},{8,11},{9,8},{10,9... | collective-permute-start | bytes 589832 | tf_op jit(solution)/shard_map/ppermute | solution.py:144
  (1 other events, 1.0 us)

commit v2 on v1

--- a/solution.py
+++ b/solution.py
@@ -202,10 +202,12 @@
     near = [turn(ring, 1), turn(ring, -1)]
     far = [turn(near[0], 1)]
     sum_mine, sum_other = add_grads(where, (0, 1), (mine, others), (ring,))
-    (sum_other,) = add_grads(where, (1,), (others,), near, (sum_other,))
+    sum_other, sum_mine = add_grads(
+        where, (1, 0), (others, mine), near, (sum_other, sum_mine)
+    )
     (sum_other,) = add_grads(where, (1,), (others,), far, (sum_other,))
     received = swap(sum_other, "label", 1)
-    (sum_mine,) = add_grads(where, (0,), (mine,), near + far, (sum_mine,))
+    (sum_mine,) = add_grads(where, (0,), (mine,), far, (sum_mine,))
 
     order = (2, 1, 3)
     quarters = [piece_of(sum_mine, step) + piece_of(received, step) for step in (0,) + order]

time: 76.7 us -> 75.6 us (0.986)
  local copies, waits for them, and re-layouts: 7.63 us -> 3.29 us
  starting transfers between devices: 27.8 us -> 32 us
  waiting for transfers between devices: 20 us -> 17.6 us
  Pallas kernels: 15.5 us -> 17.1 us
    unnamed x20 -> x8, local copies, waits for them, and re-layouts: 6.43 us -> 2.08 us
    ppermute x9, waiting for transfers between devices: 15.1 us -> 12.5 us  [shift_by(): lax.ppermute(value, axis, [(i, (i + step * inner) % size) for i in range(...]
    ppermute x9, starting transfers between devices: 16.7 us -> 19 us  [shift_by(): lax.ppermute(value, axis, [(i, (i + step * inner) % size) for i in range(...]
    ppermute x3, starting transfers between devices: 5.15 us -> 7.38 us  [swap(): return lax.ppermute(value, axis, [(i, i ^ bit) for i in range(size)])]
    pallas_call x4, Pallas kernels: 11.9 us -> 13.4 us  [add_grads(): pl.pallas_call(functools.partial(grads_kernel, blocks, len(payloads), boo...]
    ppermute x3, waiting for transfers between devices: 0.01 us -> 1.51 us  [swap(): return lax.ppermute(value, axis, [(i, i ^ bit) for i in range(size)])]
    ppermute x3, waiting for transfers between devices: 4.91 us -> 3.59 us  [turn(): lax.ppermute(value, 'label', [(i, (i + (2 - 4 * (i % 2)) * step) % size)...]
  transfers between devices with their start and end apart: 15 -> 15, of which waited for: 4 -> 5; matrix products, arithmetic and copies ran while one was open for 3% -> 3% of each run, Pallas kernels for 18% -> 19%
where the time goes in v2:
time: 75.6 us; the launch traced here: 75.3 us
  starting transfers between devices  32 us (42%)
  waiting for transfers between devices  17.6 us (23%)
  Pallas kernels  17.1 us (23%)
  other arithmetic  3.92 us (5%)
  local copies, waits for them, and re-layouts  3.29 us (4%)
  matrix products  1.21 us (2%)
    ppermute x9, starting transfers between devices, shift_by(): lax.ppermute(value, axis, [(i, (i + step * inner) % size) for i in range(...  19 us
    pallas_call x4, Pallas kernels, add_grads(): pl.pallas_call(functools.partial(grads_kernel, blocks, len(payloads), boo...  13.4 us
    ppermute x9, waiting for transfers between devices, shift_by(): lax.ppermute(value, axis, [(i, (i + step * inner) % size) for i in range(...  12.5 us
    ppermute x3, starting transfers between devices, swap(): return lax.ppermute(value, axis, [(i, i ^ bit) for i in range(size)])  7.38 us
    ppermute x3, starting transfers between devices, turn(): lax.ppermute(value, 'label', [(i, (i + (2 - 4 * (i % 2)) * step) % size)...  5.66 us
    pallas_call x1, Pallas kernels, body(): pl.pallas_call(digits_kernel, out_shape=jax.ShapeDtypeStruct((EXTRA, 256)...  3.62 us
    ppermute x3, waiting for transfers between devices, turn(): lax.ppermute(value, 'label', [(i, (i + (2 - 4 * (i % 2)) * step) % size)...  3.59 us
    unnamed x8, local copies, waits for them, and re-layouts  2.08 us
  transfers between devices with their start and end apart: 15, of which 5 were waited for; matrix products, arithmetic and copies ran while one was open for 3% of the time, Pallas kernels for 19%

profile of v2, /device:TPU:1, one launch (start us, length us, event | category | flops | bytes accessed | tf_op | source)
XLA Modules:
  0.0 75.3 jit_solution(2332914078415089844)
XLA Ops:
  1.0 1.2 %fusion = f32[256,256]{1,0:T(8,128)S(1)} fusion(bf16[256,512]{1,0:T(8,128)(2,1)S(1)} %copy-done, bf16[256,512]{1,0:T(8,128)(2,1)} %param.7), kind=kOutput, calls=%fused_computation.19 | convolution fusion | flops 67108864 | bytes 786432 | tf_op jit(solution)/shard_map/dot_general | solution.py:159
  2.2 3.8 %collective-permute-start = (f32[64,256]{1,0:T(8,128)S(1)}, f32[64,256]{1,0:T(8,128)S(1)}, u32[]{:S(2)}, u32[]{:S(2)}) collective-permute-start(f32[64,256]{1,0:T(8,128)S(1)} %get-tuple-element.25), channel_id=1, source_target_pairs={{0,2},{1,3},{2,0},{3,1},{4,6},{5,7},{6,4},{7,5},{8,10},{9,11},{10,... | collective-permute-start | bytes 196616 | tf_op jit(solution)/shard_map/ppermute | solution.py:144
  6.4 2.3 %collective-permute-start.2 = (f32[64,256]{1,0:T(8,128)S(1)}, f32[64,256]{1,0:T(8,128)S(1)}, u32[]{:S(2)}, u32[]{:S(2)}) collective-permute-start(f32[64,256]{1,0:T(8,128)S(1)} %get-tuple-element.26), channel_id=1, source_target_pairs={{0,3},{1,0},{2,1},{3,2},{4,7},{5,4},{6,5},{7,6},{8,11},{9,8},{10,9... | collective-permute-start | bytes 196616 | tf_op jit(solution)/shard_map/ppermute | solution.py:144
  9.3 3.6 %shard_map.64 = bf16[16,256]{1,0:T(8,128)(2,1)} custom-call(s32[2]{0:T(128)} %pad_add_fusion.1.where_ref, s32[16,256]{1,0:T(8,128)} %bitcast.12, s32[1,256]{1,0:T(1,128)} %bitcast.13, s32[768,128]{1,0:T(8,128)} %bitcast.11), custom_call_target="tpu_custom_call" | custom-call | flops 2147483648 | bytes 524288 | tf_op jit(solution)/shard_map/pallas_call | solution.py:163
  13.7 1.6 %collective-permute-start.3 = (bf16[80,256]{1,0:T(8,128)(2,1)S(1)}, bf16[80,256]{1,0:T(8,128)(2,1)S(1)}, u32[]{:S(2)}, u32[]{:S(2)}) collective-permute-start(bf16[80,256]{1,0:T(8,128)(2,1)S(1)} %pad_maximum_fusion.1), channel_id=1, source_target_pairs={{0,4},{4,0},{8,12},{12,8},{16,20},{20,16},{24,28},{28,24},{1,5},{5... | collective-permute-start | bytes 122888 | tf_op jit(solution)/shard_map/ppermute | solution.py:139
  16.5 1.9 %collective-permute-start.9 = (bf16[1536,256]{1,0:T(8,128)(2,1)S(1)}, bf16[1536,256]{1,0:T(8,128)(2,1)S(1)}, u32[]{:S(2)}, u32[]{:S(2)}) collective-permute-start(bf16[1536,256]{1,0:T(8,128)(2,1)S(1)} %constant_dynamic-slice_fusion.3.refs_0_.refs_1_), channel_id=1, source_target_pairs={{0,32},{32,0},{64,96},{96,64},{128,160},{160,128},{192,224},{224,1... | collective-permute-start | bytes 2359304 | tf_op jit(solution)/shard_map/ppermute | solution.py:139
  18.5 3.1 %collective-permute-start.4 = (bf16[1,144,256]{2,1,0:T(8,128)(2,1)S(1)}, bf16[1,144,256]{2,1,0:T(8,128)(2,1)S(1)}, u32[]{:S(2)}, u32[]{:S(2)}) collective-permute-start(bf16[1,144,256]{2,1,0:T(8,128)(2,1)S(1)} %maximum_bitcast_fusion), channel_id=1, source_target_pairs={{0,8},{4,12},{8,16},{12,20},{16,24},{20,28},{24,0},{28,4},{1,9},{5... | collective-permute-start | bytes 221192 | tf_op jit(solution)/shard_map/ppermute | solution.py:144
  21.5 2.2 %collective-permute-start.5 = (bf16[1,144,256]{2,1,0:T(8,128)(2,1)S(1)}, bf16[1,144,256]{2,1,0:T(8,128)(2,1)S(1)}, u32[]{:S(2)}, u32[]{:S(2)}) collective-permute-start(bf16[1,144,256]{2,1,0:T(8,128)(2,1)S(1)} %maximum_bitcast_fusion), channel_id=1, source_target_pairs={{0,24},{4,28},{8,0},{12,4},{16,8},{20,12},{24,16},{28,20},{1,25},{... | collective-permute-start | bytes 221192 | tf_op jit(solution)/shard_map/ppermute | solution.py:144
  23.7 4.4 %collective-permute-start.6 = (bf16[1,144,256]{2,1,0:T(8,128)(2,1)S(1)}, bf16[1,144,256]{2,1,0:T(8,128)(2,1)S(1)}, u32[]{:S(2)}, u32[]{:S(2)}) collective-permute-start(bf16[1,144,256]{2,1,0:T(8,128)(2,1)S(1)} %maximum_bitcast_fusion), channel_id=1, source_target_pairs={{0,16},{4,20},{8,24},{12,28},{16,0},{20,4},{24,8},{28,12},{1,17},{... | collective-permute-start | bytes 221192 | tf_op jit(solution)/shard_map/ppermute | solution.py:144
  28.1 3.2 %collective-permute-done.6 = bf16[1,144,256]{2,1,0:T(8,128)(2,1)S(1)} collective-permute-done((bf16[1,144,256]{2,1,0:T(8,128)(2,1)S(1)}, bf16[1,144,256]{2,1,0:T(8,128)(2,1)S(1)}, u32[]{:S(2)}, u32[]{:S(2)}) %collective-permute-start.6) | collective-permute-done | bytes 73760 | tf_op jit(solution)/shard_map/ppermute | solution.py:144
  31.4 2.5 %collective-permute-start.7 = (bf16[4,144,256]{2,1,0:T(8,128)(2,1)S(1)}, bf16[4,144,256]{2,1,0:T(8,128)(2,1)S(1)}, u32[]{:S(2)}, u32[]{:S(2)}) collective-permute-start(bf16[4,144,256]{2,1,0:T(8,128)(2,1)S(1)} %pad_maximum_fusion.refs_2_), channel_id=1, source_target_pairs={{0,64},{32,224},{64,128},{96,32},{128,192},{160,96},{192,0},{224,1... | collective-permute-start | bytes 884744 | tf_op jit(solution)/shard_map/ppermute | solution.py:149
  34.0 3.6 %collective-permute-done.7.refs_2_ = bf16[4,144,256]{2,1,0:T(8,128)(2,1)S(1)} collective-permute-done((bf16[4,144,256]{2,1,0:T(8,128)(2,1)S(1)}, bf16[4,144,256]{2,1,0:T(8,128)(2,1)S(1)}, u32[]{:S(2)}, u32[]{:S(2)}) %collective-permute-start.7) | collective-permute-done | bytes 294944 | tf_op jit(solution)/shard_map/ppermute | solution.py:149
  37.6 3.1 %collective-permute-start.8 = (bf16[4,144,256]{2,1,0:T(8,128)(2,1)S(1)}, bf16[4,144,256]{2,1,0:T(8,128)(2,1)S(1)}, u32[]{:S(2)}, u32[]{:S(2)}) collective-permute-start(bf16[4,144,256]{2,1,0:T(8,128)(2,1)S(1)} %collective-permute-done.7.refs_2_), channel_id=1, source_target_pairs={{0,64},{32,224},{64,128},{96,32},{128,192},{160,96},{192,0},{224,1... | collective-permute-start | bytes 884744 | tf_op jit(solution)/shard_map/ppermute | solution.py:149
  40.7 3.2 %shard_map.65 = (f32[1536,256]{1,0:T(8,128)S(1)}, f32[1536,256]{1,0:T(8,128)S(1)}) custom-call(s32[2]{0:T(128)S(1)} %pad_add_fusion.where_ref, bf16[1536,256]{1,0:T(8,128)(2,1)S(1)} %constant_dynamic-slice_fusion.3.refs_0_.refs_1_, bf16[1536,256]{1,0:T(8,128)(2,1)S(1)} %collective-permute-done.9.refs_1_.refs_0_, bf16[4,144,256]{2,1,0:T(8,128)(2,1)S(1)} %pad_maximum_fusion.refs_2_), custom_call_target="tpu_custom_call" | custom-call | flops 1610612736 | bytes 4194304 | tf_op jit(solution)/shard_map/pallas_call | solution.py:120
  45.0 5.3 %shard_map.66 = (f32[1536,256]{1,0:T(8,128)S(1)}, f32[1536,256]{1,0:T(8,128)S(1)}) custom-call(s32[2]{0:T(128)S(1)} %pad_add_fusion.where_ref, bf16[1536,256]{1,0:T(8,128)(2,1)S(1)} %copy-done.2, bf16[1536,256]{1,0:T(8,128)(2,1)S(1)} %constant_dynamic-slice_fusion.3.refs_0_.refs_1_, bf16[4,144,256]{2,1,0:T(8,128)(2,1)S(1)} %collective-permute-done.7.refs_2_, ...), custom_call_target="tpu_custom_call" | custom-call | flops 3221225472 | bytes 4194304 | tf_op jit(solution)/shard_map/pallas_call | solution.py:120
  50.4 3.0 %shard_map.68 = f32[1536,256]{1,0:T(8,128)} custom-call(s32[2]{0:T(128)S(1)} %pad_add_fusion.where_ref, bf16[1536,256]{1,0:T(8,128)(2,1)S(1)} %copy-done.2, bf16[4,144,256]{2,1,0:T(8,128)(2,1)S(1)} %collective-permute-done.8.refs_1_, f32[1536,256]{1,0:T(8,128)S(1)} %get-tuple-element.16.refs_2_), custom_call_target="tpu_custom_call" | custom-call | flops 805306368 | bytes 4194304 | tf_op jit(solution)/shard_map/pallas_call | solution.py:120
  53.4 3.9 %collective-permute-start.11 = (f32[1536,256]{1,0:T(8,128)}, f32[1536,256]{1,0:T(8,128)}, u32[]{:S(2)}, u32[]{:S(2)}) collective-permute-start(f32[1536,256]{1,0:T(8,128)} %shard_map.68), channel_id=1, source_target_pairs={{0,32},{32,0},{64,96},{96,64},{128,160},{160,128},{192,224},{224,1... | collective-permute-start | bytes 4718600 | tf_op jit(solution)/shard_map/ppermute | solution.py:139
  57.3 1.9 %shard_map.67 = f32[1536,256]{1,0:T(8,128)S(1)} custom-call(s32[2]{0:T(128)S(1)} %pad_add_fusion.where_ref, bf16[1536,256]{1,0:T(8,128)(2,1)S(1)} %constant_dynamic-slice_fusion.3.refs_0_.refs_1_, bf16[4,144,256]{2,1,0:T(8,128)(2,1)S(1)} %collective-permute-done.8.refs_1_, f32[1536,256]{1,0:T(8,128)S(1)} %get-tuple-element.15.refs_2_), custom_call_target="tpu_custom_call" | custom-call | flops 805306368 | bytes 4194304 | tf_op jit(solution)/shard_map/pallas_call | solution.py:120
  59.2 1.5 %collective-permute-done.11 = f32[1536,256]{1,0:T(8,128)} collective-permute-done((f32[1536,256]{1,0:T(8,128)}, f32[1536,256]{1,0:T(8,128)}, u32[]{:S(2)}, u32[]{:S(2)}) %collective-permute-start.11) | collective-permute-done | bytes 1572896 | tf_op jit(solution)/shard_map/ppermute | solution.py:139
  60.7 1.6 %multiply_convert_fusion = (f16[384,256]{1,0:T(8,128)(2,1)S(1)}, f16[384,256]{1,0:T(8,128)(2,1)S(1)}, f16[384,256]{1,0:T(8,128)(2,1)S(1)}, f32[384,256]{1,0:T(8,128)S(1)}) fusion(f32[1536,256]{1,0:T(8,128)} %collective-permute-done.11, s32[]{:T(128)S(6)} %select_n.54, f32[1536,256]{1,0:T(8,128)S(1)} %shard_map.67, s32[]{:T(128)S(6)} %select_n.53, ...), kind=kLoop, calls=%fused_computation.2 | loop fusion | flops 983040 | bytes 4128784 | tf_op jit(solution)/shard_map/convert_element_type | solution.py:215
  62.4 1.5 %collective-permute-start.13 = (f16[384,256]{1,0:T(8,128)(2,1)S(1)}, f16[384,256]{1,0:T(8,128)(2,1)S(1)}, u32[]{:S(2)}, u32[]{:S(2)}) collective-permute-start(f16[384,256]{1,0:T(8,128)(2,1)S(1)} %get-tuple-element.19), channel_id=1, source_target_pairs={{0,1},{1,2},{2,3},{3,0},{4,5},{5,6},{6,7},{7,4},{8,9},{9,10},{10,1... | collective-permute-start | bytes 589832 | tf_op jit(solution)/shard_map/ppermute | solution.py:144
  63.9 1.3 %collective-permute-start.14 = (f16[384,256]{1,0:T(8,128)(2,1)S(1)}, f16[384,256]{1,0:T(8,128)(2,1)S(1)}, u32[]{:S(2)}, u32[]{:S(2)}) collective-permute-start(f16[384,256]{1,0:T(8,128)(2,1)S(1)} %get-tuple-element.20), channel_id=1, source_target_pairs={{0,3},{1,0},{2,1},{3,2},{4,7},{5,4},{6,5},{7,6},{8,11},{9,8},{10,9... | collective-permute-start | bytes 589832 | tf_op jit(solution)/shard_map/ppermute | solution.py:144
  65.1 4.9 %collective-permute-done.12 = f16[384,256]{1,0:T(8,128)(2,1)S(1)} collective-permute-done((f16[384,256]{1,0:T(8,128)(2,1)S(1)}, f16[384,256]{1,0:T(8,128)(2,1)S(1)}, u32[]{:S(2)}, u32[]{:S(2)}) %collective-permute-start.12) | collective-permute-done | bytes 196640 | tf_op jit(solution)/shard_map/ppermute | solution.py:144
  70.1 4.4 %collective-permute-done.13 = f16[384,256]{1,0:T(8,128)(2,1)S(1)} collective-permute-done((f16[384,256]{1,0:T(8,128)(2,1)S(1)}, f16[384,256]{1,0:T(8,128)(2,1)S(1)}, u32[]{:S(2)}, u32[]{:S(2)}) %collective-permute-start.13) | collective-permute-done | bytes 196640 | tf_op jit(solution)/shard_map/ppermute | solution.py:144
  (33 shorter events, 6.2 us)
Async XLA Ops:
  0.0 1.0 %copy-start = (bf16[256,512]{1,0:T(8,128)(2,1)S(1)}, bf16[256,512]{1,0:T(8,128)(2,1)}, u32[]{:S(2)}) copy-start(bf16[256,512]{1,0:T(8,128)(2,1)} %param.6) | copy-start | bytes 786436
  2.2 10.7 %collective-permute-start = (f32[64,256]{1,0:T(8,128)S(1)}, f32[64,256]{1,0:T(8,128)S(1)}, u32[]{:S(2)}, u32[]{:S(2)}) collective-permute-start(f32[64,256]{1,0:T(8,128)S(1)} %get-tuple-element.25), channel_id=1, source_target_pairs={{0,2},{1,3},{2,0},{3,1},{4,6},{5,7},{6,4},{7,5},{8,10},{9,11},{10,... | collective-permute-start | bytes 196616 | tf_op jit(solution)/shard_map/ppermute | solution.py:144
  6.0 6.9 %collective-permute-start.1 = (f32[64,256]{1,0:T(8,128)S(1)}, f32[64,256]{1,0:T(8,128)S(1)}, u32[]{:S(2)}, u32[]{:S(2)}) collective-permute-start(f32[64,256]{1,0:T(8,128)S(1)} %get-tuple-element.27), channel_id=1, source_target_pairs={{0,1},{1,2},{2,3},{3,0},{4,5},{5,6},{6,7},{7,4},{8,9},{9,10},{10,1... | collective-permute-start | bytes 196616 | tf_op jit(solution)/shard_map/ppermute | solution.py:144
  6.4 6.5 %collective-permute-start.2 = (f32[64,256]{1,0:T(8,128)S(1)}, f32[64,256]{1,0:T(8,128)S(1)}, u32[]{:S(2)}, u32[]{:S(2)}) collective-permute-start(f32[64,256]{1,0:T(8,128)S(1)} %get-tuple-element.26), channel_id=1, source_target_pairs={{0,3},{1,0},{2,1},{3,2},{4,7},{5,4},{6,5},{7,6},{8,11},{9,8},{10,9... | collective-permute-start | bytes 196616 | tf_op jit(solution)/shard_map/ppermute | solution.py:144
  12.9 5.5 %copy-start.3 = (bf16[16,256]{1,0:T(8,128)(2,1)S(1)}, bf16[16,256]{1,0:T(8,128)(2,1)}, u32[]{:S(2)}) copy-start(bf16[16,256]{1,0:T(8,128)(2,1)} %shard_map.64) | copy-start | bytes 24580
  13.7 4.7 %collective-permute-start.3 = (bf16[80,256]{1,0:T(8,128)(2,1)S(1)}, bf16[80,256]{1,0:T(8,128)(2,1)S(1)}, u32[]{:S(2)}, u32[]{:S(2)}) collective-permute-start(bf16[80,256]{1,0:T(8,128)(2,1)S(1)} %pad_maximum_fusion.1), channel_id=1, source_target_pairs={{0,4},{4,0},{8,12},{12,8},{16,20},{20,16},{24,28},{28,24},{1,5},{5... | collective-permute-start | bytes 122888 | tf_op jit(solution)/shard_map/ppermute | solution.py:139
  16.5 24.2 %collective-permute-start.9 = (bf16[1536,256]{1,0:T(8,128)(2,1)S(1)}, bf16[1536,256]{1,0:T(8,128)(2,1)S(1)}, u32[]{:S(2)}, u32[]{:S(2)}) collective-permute-start(bf16[1536,256]{1,0:T(8,128)(2,1)S(1)} %constant_dynamic-slice_fusion.3.refs_0_.refs_1_), channel_id=1, source_target_pairs={{0,32},{32,0},{64,96},{96,64},{128,160},{160,128},{192,224},{224,1... | collective-permute-start | bytes 2359304 | tf_op jit(solution)/shard_map/ppermute | solution.py:139
  18.5 9.7 %collective-permute-start.4 = (bf16[1,144,256]{2,1,0:T(8,128)(2,1)S(1)}, bf16[1,144,256]{2,1,0:T(8,128)(2,1)S(1)}, u32[]{:S(2)}, u32[]{:S(2)}) collective-permute-start(bf16[1,144,256]{2,1,0:T(8,128)(2,1)S(1)} %maximum_bitcast_fusion), channel_id=1, source_target_pairs={{0,8},{4,12},{8,16},{12,20},{16,24},{20,28},{24,0},{28,4},{1,9},{5... | collective-permute-start | bytes 221192 | tf_op jit(solution)/shard_map/ppermute | solution.py:144
  21.5 6.6 %collective-permute-start.5 = (bf16[1,144,256]{2,1,0:T(8,128)(2,1)S(1)}, bf16[1,144,256]{2,1,0:T(8,128)(2,1)S(1)}, u32[]{:S(2)}, u32[]{:S(2)}) collective-permute-start(bf16[1,144,256]{2,1,0:T(8,128)(2,1)S(1)} %maximum_bitcast_fusion), channel_id=1, source_target_pairs={{0,24},{4,28},{8,0},{12,4},{16,8},{20,12},{24,16},{28,20},{1,25},{... | collective-permute-start | bytes 221192 | tf_op jit(solution)/shard_map/ppermute | solution.py:144
  23.7 7.6 %collective-permute-start.6 = (bf16[1,144,256]{2,1,0:T(8,128)(2,1)S(1)}, bf16[1,144,256]{2,1,0:T(8,128)(2,1)S(1)}, u32[]{:S(2)}, u32[]{:S(2)}) collective-permute-start(bf16[1,144,256]{2,1,0:T(8,128)(2,1)S(1)} %maximum_bitcast_fusion), channel_id=1, source_target_pairs={{0,16},{4,20},{8,24},{12,28},{16,0},{20,4},{24,8},{28,12},{1,17},{... | collective-permute-start | bytes 221192 | tf_op jit(solution)/shard_map/ppermute | solution.py:144
  31.4 6.2 %collective-permute-start.7 = (bf16[4,144,256]{2,1,0:T(8,128)(2,1)S(1)}, bf16[4,144,256]{2,1,0:T(8,128)(2,1)S(1)}, u32[]{:S(2)}, u32[]{:S(2)}) collective-permute-start(bf16[4,144,256]{2,1,0:T(8,128)(2,1)S(1)} %pad_maximum_fusion.refs_2_), channel_id=1, source_target_pairs={{0,64},{32,224},{64,128},{96,32},{128,192},{160,96},{192,0},{224,1... | collective-permute-start | bytes 884744 | tf_op jit(solution)/shard_map/ppermute | solution.py:149
  33.9 10.0 %collective-permute-start.10 = (bf16[4,144,256]{2,1,0:T(8,128)(2,1)S(1)}, bf16[4,144,256]{2,1,0:T(8,128)(2,1)S(1)}, u32[]{:S(2)}, u32[]{:S(2)}) collective-permute-start(bf16[4,144,256]{2,1,0:T(8,128)(2,1)S(1)} %pad_maximum_fusion.refs_2_), channel_id=1, source_target_pairs={{0,192},{32,96},{64,0},{96,160},{128,64},{160,224},{192,128},{224,... | collective-permute-start | bytes 884744 | tf_op jit(solution)/shard_map/ppermute | solution.py:149
  37.6 12.8 %collective-permute-start.8 = (bf16[4,144,256]{2,1,0:T(8,128)(2,1)S(1)}, bf16[4,144,256]{2,1,0:T(8,128)(2,1)S(1)}, u32[]{:S(2)}, u32[]{:S(2)}) collective-permute-start(bf16[4,144,256]{2,1,0:T(8,128)(2,1)S(1)} %collective-permute-done.7.refs_2_), channel_id=1, source_target_pairs={{0,64},{32,224},{64,128},{96,32},{128,192},{160,96},{192,0},{224,1... | collective-permute-start | bytes 884744 | tf_op jit(solution)/shard_map/ppermute | solution.py:149
  40.7 3.2 %copy-start.1 = (bf16[1536,256]{1,0:T(8,128)(2,1)}, bf16[1536,256]{1,0:T(8,128)(2,1)S(1)}, u32[]{:S(2)}) copy-start(bf16[1536,256]{1,0:T(8,128)(2,1)S(1)} %collective-permute-done.9.refs_1_.refs_0_) | copy-start | bytes 2359300
  43.9 1.1 %copy-start.2 = (bf16[1536,256]{1,0:T(8,128)(2,1)S(1)}, bf16[1536,256]{1,0:T(8,128)(2,1)}, u32[]{:S(2)}) copy-start(bf16[1536,256]{1,0:T(8,128)(2,1)} %copy-done.1) | copy-start | bytes 2359300
  53.4 7.2 %collective-permute-start.11 = (f32[1536,256]{1,0:T(8,128)}, f32[1536,256]{1,0:T(8,128)}, u32[]{:S(2)}, u32[]{:S(2)}) collective-permute-start(f32[1536,256]{1,0:T(8,128)} %shard_map.68), channel_id=1, source_target_pairs={{0,32},{32,0},{64,96},{96,64},{128,160},{160,128},{192,224},{224,1... | collective-permute-start | bytes 4718600 | tf_op jit(solution)/shard_map/ppermute | solution.py:139
  62.3 7.7 %collective-permute-start.12 = (f16[384,256]{1,0:T(8,128)(2,1)S(1)}, f16[384,256]{1,0:T(8,128)(2,1)S(1)}, u32[]{:S(2)}, u32[]{:S(2)}) collective-permute-start(f16[384,256]{1,0:T(8,128)(2,1)S(1)} %get-tuple-element.18), channel_id=1, source_target_pairs={{0,2},{1,3},{2,0},{3,1},{4,6},{5,7},{6,4},{7,5},{8,10},{9,11},{10,... | collective-permute-start | bytes 589832 | tf_op jit(solution)/shard_map/ppermute | solution.py:144
  62.4 12.1 %collective-permute-start.13 = (f16[384,256]{1,0:T(8,128)(2,1)S(1)}, f16[384,256]{1,0:T(8,128)(2,1)S(1)}, u32[]{:S(2)}, u32[]{:S(2)}) collective-permute-start(f16[384,256]{1,0:T(8,128)(2,1)S(1)} %get-tuple-element.19), channel_id=1, source_target_pairs={{0,1},{1,2},{2,3},{3,0},{4,5},{5,6},{6,7},{7,4},{8,9},{9,10},{10,1... | collective-permute-start | bytes 589832 | tf_op jit(solution)/shard_map/ppermute | solution.py:144
  63.9 10.6 %collective-permute-start.14 = (f16[384,256]{1,0:T(8,128)(2,1)S(1)}, f16[384,256]{1,0:T(8,128)(2,1)S(1)}, u32[]{:S(2)}, u32[]{:S(2)}) collective-permute-start(f16[384,256]{1,0:T(8,128)(2,1)S(1)} %get-tuple-element.20), channel_id=1, source_target_pairs={{0,3},{1,0},{2,1},{3,2},{4,7},{5,4},{6,5},{7,6},{8,11},{9,8},{10,9... | collective-permute-start | bytes 589832 | tf_op jit(solution)/shard_map/ppermute | solution.py:144

commit v3 on v1

--- a/solution.py
+++ b/solution.py
@@ -20,29 +20,45 @@
 
 
 def digits_kernel(where_ref, pos_ref, counts_ref, place_ref, out_ref):
-    shift, half = where_ref[0], where_ref[1]
+    start, half = where_ref[1], where_ref[2]
     table = place_ref[...]
     high = ((table >> 8) - MIDDLE).astype(jnp.float32).astype(jnp.bfloat16)
     low = (table & 255).astype(jnp.float32).astype(jnp.bfloat16)
     tables = jnp.concatenate([high, low], axis=1)
-    pos = pltpu.roll(pos_ref[...], shift, 1)[:, :128]
-    counts = pltpu.roll(jnp.broadcast_to(counts_ref[...], (8, 256)), shift, 1)[0:1, :128]
+    count = SLOTS // 2
+    lane = lax.broadcasted_iota(jnp.int32, (count, 128), 1)
+    lower = lane < OWN
+    early = pltpu.roll(pos_ref[:count, :], (256 - start) & 255, 1)[:, :128]
+    late = pltpu.roll(pos_ref[count:, :], (256 + OWN - start) & 255, 1)[:, :128]
+    pos = jnp.where(lower, early, late)
     groups = table.shape[0]
-    row = lax.broadcasted_iota(jnp.int32, (groups, 128), 0)
-    lane = lax.broadcasted_iota(jnp.int32, (128, 128), 0)
-    spot = lax.broadcasted_iota(jnp.int32, (1, 128), 1)
-    mine = (spot >= half) & (spot < half + OWN)
-    highs, lows = [], []
-    for k in range(SLOTS):
-        one = pos[k : k + 1, :]
+    row = lax.broadcasted_iota(jnp.int32, (groups, 256), 0)
+    spot = lax.broadcasted_iota(jnp.int32, (128, 256), 0)
+    firsts, seconds = [], []
+    for k in range(count // 2):
+        one = jnp.concatenate([pos[2 * k : 2 * k + 1, :], pos[2 * k + 1 : 2 * k + 2, :]], axis=1)
         hot = jnp.where(row == (one >> 7), 1.0, 0.0).astype(jnp.bfloat16)
         both = lax.dot_general(tables, hot, (((0,), (0,)), ((), ())), preferred_element_type=jnp.float32)
-        pick = lane == (one & 127)
+        pick = spot == (one & 127)
         first = jnp.sum(jnp.where(pick, both[:128], 0.0), axis=0, keepdims=True)
         second = jnp.sum(jnp.where(pick, both[128:], 0.0), axis=0, keepdims=True)
-        used = k < counts
-        highs.append(jnp.where(mine, jnp.where(used, first, NOWHERE), 0.0))
-        lows.append(jnp.where(mine & used, second, 0.0))
+        firsts += [first[:, :128], first[:, 128:]]
+        seconds += [second[:, :128], second[:, 128:]]
+    first = jnp.concatenate(firsts, axis=0)
+    second = jnp.concatenate(seconds, axis=0)
+    counts = jnp.broadcast_to(counts_ref[...], (count, 256))
+    counts = pltpu.roll(counts, (256 + half - start) & 255, 1)[:, :128]
+    mine = (lane >= half) & (lane < half + OWN)
+    slot = lax.broadcasted_iota(jnp.int32, (count, 128), 0)
+
+    def placed(value, shift, used, nothing):
+        return jnp.where(mine, jnp.where(used, pltpu.roll(value, shift, 1), nothing), 0.0)
+
+    highs, lows = [], []
+    for shift, base in ((half, 0), (OWN - half, count)):
+        used = slot + base < counts
+        highs.append(placed(first, shift, used, NOWHERE))
+        lows.append(placed(second, shift, used, 0.0))
     out_ref[...] = jnp.concatenate(
         [jnp.concatenate(highs, axis=0), jnp.concatenate(lows, axis=0)], axis=1
     ).astype(jnp.bfloat16)
@@ -97,31 +113,28 @@
     return jnp.dot(grad, proj, preferred_element_type=jnp.float32)
 
 
-def grads_kernel(blocks, payloads, adds, where_ref, *refs):
-    count = len(blocks)
-    factors, refs = refs[:count], refs[count:]
+def grads_kernel(payloads, adds, where_ref, factor_ref, *refs):
     payload_refs, refs = refs[:payloads], refs[payloads:]
-    olds, refs = refs[: count * adds], refs[count * adds :]
-    outs, (words_ref, word_ref, bit_ref) = refs[:count], refs[count:]
-    for i, which in enumerate(blocks):
-        build_words(where_ref[which], payload_refs, words_ref, word_ref, bit_ref)
-        value = block_grads(factors[i], payload_refs, words_ref)
-        outs[i][...] = olds[i][...] + value if adds else value
+    olds, (out_ref, words_ref, word_ref, bit_ref) = refs[:adds], refs[adds:]
+    build_words(where_ref[0], payload_refs, words_ref, word_ref, bit_ref)
+    value = block_grads(factor_ref, payload_refs, words_ref)
+    out_ref[...] = olds[0][...] + value if adds else value
 
 
 VMEM = pl.BlockSpec(memory_space=pltpu.VMEM)
 SMEM = pl.BlockSpec(memory_space=pltpu.SMEM)
 
 
-def add_grads(where, blocks, factors, payloads, olds=()):
-    rows = factors[0].shape[0]
+def add_grads(where, factors, payloads, *olds):
+    rows = factors.shape[0]
     pairs = sum(payload.shape[0] for payload in payloads)
-    work = len(blocks) * rows * pairs * PAIR
+    work = rows * pairs * PAIR
     return pl.pallas_call(
-        functools.partial(grads_kernel, blocks, len(payloads), bool(olds)),
-        out_shape=[jax.ShapeDtypeStruct((rows, 256), jnp.float32)] * len(blocks),
-        in_specs=[SMEM] + [VMEM] * (len(blocks) + len(payloads) + len(olds)),
-        out_specs=[VMEM] * len(blocks),
+        functools.partial(grads_kernel, len(payloads), len(olds)),
+        out_shape=jax.ShapeDtypeStruct((rows, 256), jnp.float32),
+        in_specs=[SMEM] + [VMEM] * (1 + len(payloads) + len(olds)),
+        out_specs=VMEM,
+        input_output_aliases={2 + len(payloads): 0} if olds else {},
         scratch_shapes=[
             pltpu.VMEM((pairs, rows // 32, 128), jnp.int32),
             pltpu.VMEM((pairs, SLOTS, 128), jnp.int32),
@@ -131,7 +144,7 @@
         cost_estimate=pl.CostEstimate(
             flops=4 * work * 256, bytes_accessed=1 << 22, transcendentals=work
         ),
-    )(where, *factors, *payloads, *olds)
+    )(where, factors, *payloads, *olds)
 
 
 def swap(value, axis, bit):
@@ -159,7 +172,8 @@
     partial_value = lax.dot_general(
         queries, basis, (((1,), (1,)), ((), ())), preferred_element_type=jnp.float32
     )
-    others = swap(mine, "label", 1)
+    first_row = label * factors.shape[0] + dp * block
+    where = jnp.stack([first_row, part * OWN, half]).astype(jnp.int32)
     digits = pl.pallas_call(
         digits_kernel,
         out_shape=jax.ShapeDtypeStruct((EXTRA, 256), jnp.bfloat16),
@@ -169,7 +183,7 @@
             flops=1 << 31, bytes_accessed=1 << 19, transcendentals=0
         ),
     )(
-        jnp.stack([(half - part * OWN) & 255, half]).astype(jnp.int32),
+        where,
         positives.T,
         counts.reshape(1, -1),
         placement.reshape(-1, 128),
@@ -194,21 +208,22 @@
         ],
         axis=0,
     )[None]
-    ring = jnp.concatenate([pair] + [shift_by(pair, "dp", step) for step in (2, 6, 4)], axis=0)
-
-    first = label * factors.shape[0] + dp * block
-    other = (label ^ 1) * factors.shape[0] + dp * block
-    where = jnp.stack([first, other]).astype(jnp.int32)
+    others = [shift_by(pair, "dp", step) for step in (2, 6, 4)]
+    ring = jnp.concatenate([pair] + others, axis=0)
+
     near = [turn(ring, 1), turn(ring, -1)]
-    far = [turn(near[0], 1)]
-    sum_mine, sum_other = add_grads(where, (0, 1), (mine, others), (ring,))
-    (sum_other,) = add_grads(where, (1,), (others,), near, (sum_other,))
-    (sum_other,) = add_grads(where, (1,), (others,), far, (sum_other,))
-    received = swap(sum_other, "label", 1)
-    (sum_mine,) = add_grads(where, (0,), (mine,), near + far, (sum_mine,))
+    ring_other = swap(ring, "label", 1)
+    far = turn(near[0], 1)
+    near_other = [swap(value, "label", 1) for value in near]
+    far_other = swap(far, "label", 1)
+    sums = add_grads(where, mine, [ring])
+    sums = add_grads(where, mine, [ring_other], sums)
+    sums = add_grads(where, mine, near, sums)
+    sums = add_grads(where, mine, near_other, sums)
+    sums = add_grads(where, mine, [far, far_other], sums)
 
     order = (2, 1, 3)
-    quarters = [piece_of(sum_mine, step) + piece_of(received, step) for step in (0,) + order]
+    quarters = [piece_of(sums, step) for step in (0,) + order]
     total, *sent = lax.optimization_barrier(
         (quarters[0], *((value * SCALE).astype(LINK) for value in quarters[1:]))
     )

time: 76.7 us -> 73.8 us (0.962)
  starting transfers between devices: 27.8 us -> 37.4 us
  waiting for transfers between devices: 20 us -> 14.2 us
  local copies, waits for them, and re-layouts: 7.63 us -> 2.16 us
  other arithmetic: 3.95 us -> 3.14 us
    ppermute x3 -> x5, starting transfers between devices: 5.15 us -> 12.8 us  [swap(): return lax.ppermute(value, axis, [(i, i ^ bit) for i in range(size)])]
    unnamed x20 -> x4, local copies, waits for them, and re-layouts: 6.43 us -> 0.95 us
    ppermute x3, waiting for transfers between devices: 4.91 us -> 0.01 us  [turn(): lax.ppermute(value, 'label', [(i, (i + (2 - 4 * (i % 2)) * step) % size)...]
    ppermute x9, starting transfers between devices: 16.7 us -> 19.7 us  [shift_by(): lax.ppermute(value, axis, [(i, (i + step * inner) % size) for i in range(...]
    ppermute x9, waiting for transfers between devices: 15.1 us -> 12.8 us  [shift_by(): lax.ppermute(value, axis, [(i, (i + step * inner) % size) for i in range(...]
    convert_element_type x1, other arithmetic: 1.6 us -> 0.14 us  [body(): (value * SCALE).astype(LINK)]
    ppermute x3 -> x5, waiting for transfers between devices: 0.01 us -> 1.4 us  [swap(): return lax.ppermute(value, axis, [(i, i ^ bit) for i in range(size)])]
    pallas_call x1, Pallas kernels: 3.62 us -> 2.46 us  [body(): pl.pallas_call(digits_kernel, out_shape=jax.ShapeDtypeStruct((EXTRA, 256)...]
  transfers between devices with their start and end apart: 15 -> 17, of which waited for: 4 -> 4; matrix products, arithmetic and copies ran while one was open for 3% -> 3% of each run, Pallas kernels for 18% -> 17%
where the time goes in v3:
time: 73.8 us; the launch traced here: 73.6 us
  starting transfers between devices  37.4 us (51%)
  Pallas kernels  15.3 us (21%)
  waiting for transfers between devices  14.2 us (19%)
  other arithmetic  3.14 us (4%)
  local copies, waits for them, and re-layouts  2.16 us (3%)
  matrix products  1.21 us (2%)
    ppermute x9, starting transfers between devices, shift_by(): lax.ppermute(value, axis, [(i, (i + step * inner) % size) for i in range(...  19.7 us
    ppermute x5, starting transfers between devices, swap(): return lax.ppermute(value, axis, [(i, i ^ bit) for i in range(size)])  12.8 us
    ppermute x9, waiting for transfers between devices, shift_by(): lax.ppermute(value, axis, [(i, (i + step * inner) % size) for i in range(...  12.8 us
    pallas_call x5, Pallas kernels, add_grads(): pl.pallas_call(functools.partial(grads_kernel, len(payloads), len(olds)),...  12.8 us
    ppermute x3, starting transfers between devices, turn(): lax.ppermute(value, 'label', [(i, (i + (2 - 4 * (i % 2)) * step) % size)...  4.88 us
    pallas_call x1, Pallas kernels, body(): pl.pallas_call(digits_kernel, out_shape=jax.ShapeDtypeStruct((EXTRA, 256)...  2.46 us
  transfers between devices with their start and end apart: 17, of which 4 were waited for; matrix products, arithmetic and copies ran while one was open for 3% of the time, Pallas kernels for 17%

profile of v3, /device:TPU:1, one launch (start us, length us, event | category | flops | bytes accessed | tf_op | source)
XLA Modules:
  0.0 73.6 jit_solution(1451412295058198550)
XLA Ops:
  1.0 1.2 %fusion = f32[256,256]{1,0:T(8,128)S(1)} fusion(bf16[256,512]{1,0:T(8,128)(2,1)S(1)} %copy-done, bf16[256,512]{1,0:T(8,128)(2,1)} %param.7), kind=kOutput, calls=%fused_computation.18 | convolution fusion | flops 67108864 | bytes 786432 | tf_op jit(solution)/shard_map/dot_general | solution.py:172
  2.2 3.8 %collective-permute-start = (f32[64,256]{1,0:T(8,128)S(1)}, f32[64,256]{1,0:T(8,128)S(1)}, u32[]{:S(2)}, u32[]{:S(2)}) collective-permute-start(f32[64,256]{1,0:T(8,128)S(1)} %get-tuple-element.17), channel_id=1, source_target_pairs={{0,2},{1,3},{2,0},{3,1},{4,6},{5,7},{6,4},{7,5},{8,10},{9,11},{10,... | collective-permute-start | bytes 196616 | tf_op jit(solution)/shard_map/ppermute | solution.py:157
  6.4 2.3 %collective-permute-start.2 = (f32[64,256]{1,0:T(8,128)S(1)}, f32[64,256]{1,0:T(8,128)S(1)}, u32[]{:S(2)}, u32[]{:S(2)}) collective-permute-start(f32[64,256]{1,0:T(8,128)S(1)} %get-tuple-element.18), channel_id=1, source_target_pairs={{0,3},{1,0},{2,1},{3,2},{4,7},{5,4},{6,5},{7,6},{8,11},{9,8},{10,9... | collective-permute-start | bytes 196616 | tf_op jit(solution)/shard_map/ppermute | solution.py:157
  9.3 2.5 %shard_map.64 = bf16[16,256]{1,0:T(8,128)(2,1)} custom-call(s32[3]{0:T(128)} %pad_add_fusion.where_ref, s32[16,256]{1,0:T(8,128)} %bitcast.11, s32[1,256]{1,0:T(1,128)} %bitcast.12, s32[768,128]{1,0:T(8,128)} %bitcast.10), custom_call_target="tpu_custom_call" | custom-call | flops 2147483648 | bytes 524288 | tf_op jit(solution)/shard_map/pallas_call | solution.py:177
  12.6 1.6 %collective-permute-start.3 = (bf16[80,256]{1,0:T(8,128)(2,1)S(1)}, bf16[80,256]{1,0:T(8,128)(2,1)S(1)}, u32[]{:S(2)}, u32[]{:S(2)}) collective-permute-start(bf16[80,256]{1,0:T(8,128)(2,1)S(1)} %pad_maximum_fusion.1), channel_id=1, source_target_pairs={{0,4},{4,0},{8,12},{12,8},{16,20},{20,16},{24,28},{28,24},{1,5},{5... | collective-permute-start | bytes 122888 | tf_op jit(solution)/shard_map/ppermute | solution.py:152
  14.2 1.4 %collective-permute-done.3 = bf16[80,256]{1,0:T(8,128)(2,1)S(1)} collective-permute-done((bf16[80,256]{1,0:T(8,128)(2,1)S(1)}, bf16[80,256]{1,0:T(8,128)(2,1)S(1)}, u32[]{:S(2)}, u32[]{:S(2)}) %collective-permute-start.3) | collective-permute-done | bytes 40992 | tf_op jit(solution)/shard_map/ppermute | solution.py:152
  16.3 3.1 %collective-permute-start.4 = (bf16[1,144,256]{2,1,0:T(8,128)(2,1)S(1)}, bf16[1,144,256]{2,1,0:T(8,128)(2,1)S(1)}, u32[]{:S(2)}, u32[]{:S(2)}) collective-permute-start(bf16[1,144,256]{2,1,0:T(8,128)(2,1)S(1)} %maximum_bitcast_fusion), channel_id=1, source_target_pairs={{0,8},{4,12},{8,16},{12,20},{16,24},{20,28},{24,0},{28,4},{1,9},{5... | collective-permute-start | bytes 221192 | tf_op jit(solution)/shard_map/ppermute | solution.py:157
  19.4 2.9 %collective-permute-start.5 = (bf16[1,144,256]{2,1,0:T(8,128)(2,1)S(1)}, bf16[1,144,256]{2,1,0:T(8,128)(2,1)S(1)}, u32[]{:S(2)}, u32[]{:S(2)}) collective-permute-start(bf16[1,144,256]{2,1,0:T(8,128)(2,1)S(1)} %maximum_bitcast_fusion), channel_id=1, source_target_pairs={{0,24},{4,28},{8,0},{12,4},{16,8},{20,12},{24,16},{28,20},{1,25},{... | collective-permute-start | bytes 221192 | tf_op jit(solution)/shard_map/ppermute | solution.py:157
  22.3 4.4 %collective-permute-start.6 = (bf16[1,144,256]{2,1,0:T(8,128)(2,1)S(1)}, bf16[1,144,256]{2,1,0:T(8,128)(2,1)S(1)}, u32[]{:S(2)}, u32[]{:S(2)}) collective-permute-start(bf16[1,144,256]{2,1,0:T(8,128)(2,1)S(1)} %maximum_bitcast_fusion), channel_id=1, source_target_pairs={{0,16},{4,20},{8,24},{12,28},{16,0},{20,4},{24,8},{28,12},{1,17},{... | collective-permute-start | bytes 221192 | tf_op jit(solution)/shard_map/ppermute | solution.py:157
  26.7 3.5 %collective-permute-done.6 = bf16[1,144,256]{2,1,0:T(8,128)(2,1)S(1)} collective-permute-done((bf16[1,144,256]{2,1,0:T(8,128)(2,1)S(1)}, bf16[1,144,256]{2,1,0:T(8,128)(2,1)S(1)}, u32[]{:S(2)}, u32[]{:S(2)}) %collective-permute-start.6) | collective-permute-done | bytes 73760 | tf_op jit(solution)/shard_map/ppermute | solution.py:157
  30.2 2.6 %collective-permute-start.7 = (bf16[4,144,256]{2,1,0:T(8,128)(2,1)S(1)}, bf16[4,144,256]{2,1,0:T(8,128)(2,1)S(1)}, u32[]{:S(2)}, u32[]{:S(2)}) collective-permute-start(bf16[4,144,256]{2,1,0:T(8,128)(2,1)S(1)} %pad_maximum_fusion.refs_0_), channel_id=1, source_target_pairs={{0,64},{32,224},{64,128},{96,32},{128,192},{160,96},{192,0},{224,1... | collective-permute-start | bytes 884744 | tf_op jit(solution)/shard_map/ppermute | solution.py:162
  32.8 4.5 %collective-permute-start.13 = (bf16[4,144,256]{2,1,0:T(8,128)(2,1)S(1)}, bf16[4,144,256]{2,1,0:T(8,128)(2,1)S(1)}, u32[]{:S(2)}, u32[]{:S(2)}) collective-permute-start(bf16[4,144,256]{2,1,0:T(8,128)(2,1)S(1)} %pad_maximum_fusion.refs_0_), channel_id=1, source_target_pairs={{0,32},{32,0},{64,96},{96,64},{128,160},{160,128},{192,224},{224,1... | collective-permute-start | bytes 884744 | tf_op jit(solution)/shard_map/ppermute | solution.py:152
  37.3 2.3 %collective-permute-start.8 = (bf16[4,144,256]{2,1,0:T(8,128)(2,1)S(1)}, bf16[4,144,256]{2,1,0:T(8,128)(2,1)S(1)}, u32[]{:S(2)}, u32[]{:S(2)}) collective-permute-start(bf16[4,144,256]{2,1,0:T(8,128)(2,1)S(1)} %collective-permute-done.7.refs_0_), channel_id=1, source_target_pairs={{0,64},{32,224},{64,128},{96,32},{128,192},{160,96},{192,0},{224,1... | collective-permute-start | bytes 884744 | tf_op jit(solution)/shard_map/ppermute | solution.py:162
  39.6 1.2 %constant_dynamic-slice_fusion.4.factor_ref = bf16[1536,256]{1,0:T(8,128)(2,1)S(1)} fusion(bf16[12288,256]{1,0:T(8,128)(2,1)} %param.8, s32[]{:T(128)S(6)} %select_n.39), kind=kLoop, calls=%fused_computation.16 | loop fusion | bytes 1572868 | tf_op jit(solution)/shard_map/dynamic_slice | solution.py:171
  40.8 3.9 %collective-permute-start.10 = (bf16[4,144,256]{2,1,0:T(8,128)(2,1)S(1)}, bf16[4,144,256]{2,1,0:T(8,128)(2,1)S(1)}, u32[]{:S(2)}, u32[]{:S(2)}) collective-permute-start(bf16[4,144,256]{2,1,0:T(8,128)(2,1)S(1)} %collective-permute-done.7.refs_0_), channel_id=1, source_target_pairs={{0,32},{32,0},{64,96},{96,64},{128,160},{160,128},{192,224},{224,1... | collective-permute-start | bytes 884744 | tf_op jit(solution)/shard_map/ppermute | solution.py:152
  44.8 1.9 %shard_map.65.refs_1_ = f32[1536,256]{1,0:T(8,128)S(1)} custom-call(s32[3]{0:T(128)S(1)} %copy-done.1, bf16[1536,256]{1,0:T(8,128)(2,1)S(1)} %constant_dynamic-slice_fusion.4.factor_ref, bf16[4,144,256]{2,1,0:T(8,128)(2,1)S(1)} %pad_maximum_fusion.refs_0_), custom_call_target="tpu_custom_call" | custom-call | flops 805306368 | bytes 4194304 | tf_op jit(solution)/shard_map/pallas_call | solution.py:132
  46.7 2.0 %shard_map.66.refs_2_ = f32[1536,256]{1,0:T(8,128)S(1)} custom-call(s32[3]{0:T(128)S(1)} %copy-done.1, bf16[1536,256]{1,0:T(8,128)(2,1)S(1)} %constant_dynamic-slice_fusion.4.factor_ref, bf16[4,144,256]{2,1,0:T(8,128)(2,1)S(1)} %collective-permute-done.13.refs_0_, f32[1536,256]{1,0:T(8,128)S(1)} %shard_map.65.refs_1_), custom_call_target="tpu_custom_call", output_to_operand_aliasing={{}: (3, {})} | custom-call | flops 805306368 | bytes 4194304 | tf_op jit(solution)/shard_map/pallas_call | solution.py:132
  48.7 2.7 %collective-permute-start.9 = (bf16[4,144,256]{2,1,0:T(8,128)(2,1)S(1)}, bf16[4,144,256]{2,1,0:T(8,128)(2,1)S(1)}, u32[]{:S(2)}, u32[]{:S(2)}) collective-permute-start(bf16[4,144,256]{2,1,0:T(8,128)(2,1)S(1)} %collective-permute-done.8.refs_0_), channel_id=1, source_target_pairs={{0,32},{32,0},{64,96},{96,64},{128,160},{160,128},{192,224},{224,1... | collective-permute-start | bytes 884744 | tf_op jit(solution)/shard_map/ppermute | solution.py:152
  51.4 3.0 %shard_map.67.refs_2_ = f32[1536,256]{1,0:T(8,128)S(1)} custom-call(s32[3]{0:T(128)S(1)} %copy-done.1, bf16[1536,256]{1,0:T(8,128)(2,1)S(1)} %constant_dynamic-slice_fusion.4.factor_ref, bf16[4,144,256]{2,1,0:T(8,128)(2,1)S(1)} %collective-permute-done.7.refs_0_, ...), custom_call_target="tpu_custom_call", output_to_operand_aliasing={{}: (4, {})} | custom-call | flops 1610612736 | bytes 4194304 | tf_op jit(solution)/shard_map/pallas_call | solution.py:132
  54.4 3.0 %shard_map.68.refs_2_ = f32[1536,256]{1,0:T(8,128)S(1)} custom-call(s32[3]{0:T(128)S(1)} %copy-done.1, bf16[1536,256]{1,0:T(8,128)(2,1)S(1)} %constant_dynamic-slice_fusion.4.factor_ref, bf16[4,144,256]{2,1,0:T(8,128)(2,1)S(1)} %collective-permute-done.10.refs_0_, ...), custom_call_target="tpu_custom_call", output_to_operand_aliasing={{}: (4, {})} | custom-call | flops 1610612736 | bytes 4194304 | tf_op jit(solution)/shard_map/pallas_call | solution.py:132
  57.4 3.0 %shard_map.69 = f32[1536,256]{1,0:T(8,128)S(1)} custom-call(s32[3]{0:T(128)S(1)} %copy-done.1, bf16[1536,256]{1,0:T(8,128)(2,1)S(1)} %constant_dynamic-slice_fusion.4.factor_ref, bf16[4,144,256]{2,1,0:T(8,128)(2,1)S(1)} %collective-permute-done.8.refs_0_, bf16[4,144,256]{2,1,0:T(8,128)(2,1)S(1)} %collective-permute-done.9.refs_1_, ...), custom_call_target="tpu_custom_call", output_to_operand_aliasing={{}: (4, {})} | custom-call | flops 1610612736 | bytes 4194304 | tf_op jit(solution)/shard_map/pallas_call | solution.py:132
  61.9 1.5 %collective-permute-start.16 = (f16[384,256]{1,0:T(8,128)(2,1)S(1)}, f16[384,256]{1,0:T(8,128)(2,1)S(1)}, u32[]{:S(2)}, u32[]{:S(2)}) collective-permute-start(f16[384,256]{1,0:T(8,128)(2,1)S(1)} %get-tuple-element.12), channel_id=1, source_target_pairs={{0,3},{1,0},{2,1},{3,2},{4,7},{5,4},{6,5},{7,6},{8,11},{9,8},{10,9... | collective-permute-start | bytes 589832 | tf_op jit(solution)/shard_map/ppermute | solution.py:157
  63.4 5.2 %collective-permute-done.14 = f16[384,256]{1,0:T(8,128)(2,1)S(1)} collective-permute-done((f16[384,256]{1,0:T(8,128)(2,1)S(1)}, f16[384,256]{1,0:T(8,128)(2,1)S(1)}, u32[]{:S(2)}, u32[]{:S(2)}) %collective-permute-start.14) | collective-permute-done | bytes 196640 | tf_op jit(solution)/shard_map/ppermute | solution.py:157
  68.7 4.1 %collective-permute-done.15 = f16[384,256]{1,0:T(8,128)(2,1)S(1)} collective-permute-done((f16[384,256]{1,0:T(8,128)(2,1)S(1)}, f16[384,256]{1,0:T(8,128)(2,1)S(1)}, u32[]{:S(2)}, u32[]{:S(2)}) %collective-permute-start.15) | collective-permute-done | bytes 196640 | tf_op jit(solution)/shard_map/ppermute | solution.py:157
  (33 shorter events, 6.0 us)
Async XLA Ops:
  0.0 1.0 %copy-start = (bf16[256,512]{1,0:T(8,128)(2,1)S(1)}, bf16[256,512]{1,0:T(8,128)(2,1)}, u32[]{:S(2)}) copy-start(bf16[256,512]{1,0:T(8,128)(2,1)} %param.6) | copy-start | bytes 786436
  2.2 9.6 %collective-permute-start = (f32[64,256]{1,0:T(8,128)S(1)}, f32[64,256]{1,0:T(8,128)S(1)}, u32[]{:S(2)}, u32[]{:S(2)}) collective-permute-start(f32[64,256]{1,0:T(8,128)S(1)} %get-tuple-element.17), channel_id=1, source_target_pairs={{0,2},{1,3},{2,0},{3,1},{4,6},{5,7},{6,4},{7,5},{8,10},{9,11},{10,... | collective-permute-start | bytes 196616 | tf_op jit(solution)/shard_map/ppermute | solution.py:157
  6.0 5.8 %collective-permute-start.1 = (f32[64,256]{1,0:T(8,128)S(1)}, f32[64,256]{1,0:T(8,128)S(1)}, u32[]{:S(2)}, u32[]{:S(2)}) collective-permute-start(f32[64,256]{1,0:T(8,128)S(1)} %get-tuple-element.19), channel_id=1, source_target_pairs={{0,1},{1,2},{2,3},{3,0},{4,5},{5,6},{6,7},{7,4},{8,9},{9,10},{10,1... | collective-permute-start | bytes 196616 | tf_op jit(solution)/shard_map/ppermute | solution.py:157
  6.4 5.4 %collective-permute-start.2 = (f32[64,256]{1,0:T(8,128)S(1)}, f32[64,256]{1,0:T(8,128)S(1)}, u32[]{:S(2)}, u32[]{:S(2)}) collective-permute-start(f32[64,256]{1,0:T(8,128)S(1)} %get-tuple-element.18), channel_id=1, source_target_pairs={{0,3},{1,0},{2,1},{3,2},{4,7},{5,4},{6,5},{7,6},{8,11},{9,8},{10,9... | collective-permute-start | bytes 196616 | tf_op jit(solution)/shard_map/ppermute | solution.py:157
  11.8 33.0 %copy-start.1 = (s32[3]{0:T(128)S(1)}, s32[3]{0:T(128)}, u32[]{:S(2)}) copy-start(s32[3]{0:T(128)} %pad_add_fusion.where_ref) | copy-start | bytes 40
  12.6 3.0 %collective-permute-start.3 = (bf16[80,256]{1,0:T(8,128)(2,1)S(1)}, bf16[80,256]{1,0:T(8,128)(2,1)S(1)}, u32[]{:S(2)}, u32[]{:S(2)}) collective-permute-start(bf16[80,256]{1,0:T(8,128)(2,1)S(1)} %pad_maximum_fusion.1), channel_id=1, source_target_pairs={{0,4},{4,0},{8,12},{12,8},{16,20},{20,16},{24,28},{28,24},{1,5},{5... | collective-permute-start | bytes 122888 | tf_op jit(solution)/shard_map/ppermute | solution.py:152
  16.3 10.4 %collective-permute-start.4 = (bf16[1,144,256]{2,1,0:T(8,128)(2,1)S(1)}, bf16[1,144,256]{2,1,0:T(8,128)(2,1)S(1)}, u32[]{:S(2)}, u32[]{:S(2)}) collective-permute-start(bf16[1,144,256]{2,1,0:T(8,128)(2,1)S(1)} %maximum_bitcast_fusion), channel_id=1, source_target_pairs={{0,8},{4,12},{8,16},{12,20},{16,24},{20,28},{24,0},{28,4},{1,9},{5... | collective-permute-start | bytes 221192 | tf_op jit(solution)/shard_map/ppermute | solution.py:157
  19.4 7.3 %collective-permute-start.5 = (bf16[1,144,256]{2,1,0:T(8,128)(2,1)S(1)}, bf16[1,144,256]{2,1,0:T(8,128)(2,1)S(1)}, u32[]{:S(2)}, u32[]{:S(2)}) collective-permute-start(bf16[1,144,256]{2,1,0:T(8,128)(2,1)S(1)} %maximum_bitcast_fusion), channel_id=1, source_target_pairs={{0,24},{4,28},{8,0},{12,4},{16,8},{20,12},{24,16},{28,20},{1,25},{... | collective-permute-start | bytes 221192 | tf_op jit(solution)/shard_map/ppermute | solution.py:157
  22.3 7.9 %collective-permute-start.6 = (bf16[1,144,256]{2,1,0:T(8,128)(2,1)S(1)}, bf16[1,144,256]{2,1,0:T(8,128)(2,1)S(1)}, u32[]{:S(2)}, u32[]{:S(2)}) collective-permute-start(bf16[1,144,256]{2,1,0:T(8,128)(2,1)S(1)} %maximum_bitcast_fusion), channel_id=1, source_target_pairs={{0,16},{4,20},{8,24},{12,28},{16,0},{20,4},{24,8},{28,12},{1,17},{... | collective-permute-start | bytes 221192 | tf_op jit(solution)/shard_map/ppermute | solution.py:157
  30.2 7.0 %collective-permute-start.7 = (bf16[4,144,256]{2,1,0:T(8,128)(2,1)S(1)}, bf16[4,144,256]{2,1,0:T(8,128)(2,1)S(1)}, u32[]{:S(2)}, u32[]{:S(2)}) collective-permute-start(bf16[4,144,256]{2,1,0:T(8,128)(2,1)S(1)} %pad_maximum_fusion.refs_0_), channel_id=1, source_target_pairs={{0,64},{32,224},{64,128},{96,32},{128,192},{160,96},{192,0},{224,1... | collective-permute-start | bytes 884744 | tf_op jit(solution)/shard_map/ppermute | solution.py:162
  32.8 11.9 %collective-permute-start.11 = (bf16[4,144,256]{2,1,0:T(8,128)(2,1)S(1)}, bf16[4,144,256]{2,1,0:T(8,128)(2,1)S(1)}, u32[]{:S(2)}, u32[]{:S(2)}) collective-permute-start(bf16[4,144,256]{2,1,0:T(8,128)(2,1)S(1)} %pad_maximum_fusion.refs_0_), channel_id=1, source_target_pairs={{0,192},{32,96},{64,0},{96,160},{128,64},{160,224},{192,128},{224,... | collective-permute-start | bytes 884744 | tf_op jit(solution)/shard_map/ppermute | solution.py:162
  32.8 13.9 %collective-permute-start.13 = (bf16[4,144,256]{2,1,0:T(8,128)(2,1)S(1)}, bf16[4,144,256]{2,1,0:T(8,128)(2,1)S(1)}, u32[]{:S(2)}, u32[]{:S(2)}) collective-permute-start(bf16[4,144,256]{2,1,0:T(8,128)(2,1)S(1)} %pad_maximum_fusion.refs_0_), channel_id=1, source_target_pairs={{0,32},{32,0},{64,96},{96,64},{128,160},{160,128},{192,224},{224,1... | collective-permute-start | bytes 884744 | tf_op jit(solution)/shard_map/ppermute | solution.py:152
  37.3 11.4 %collective-permute-start.8 = (bf16[4,144,256]{2,1,0:T(8,128)(2,1)S(1)}, bf16[4,144,256]{2,1,0:T(8,128)(2,1)S(1)}, u32[]{:S(2)}, u32[]{:S(2)}) collective-permute-start(bf16[4,144,256]{2,1,0:T(8,128)(2,1)S(1)} %collective-permute-done.7.refs_0_), channel_id=1, source_target_pairs={{0,64},{32,224},{64,128},{96,32},{128,192},{160,96},{192,0},{224,1... | collective-permute-start | bytes 884744 | tf_op jit(solution)/shard_map/ppermute | solution.py:162
  40.8 13.6 %collective-permute-start.10 = (bf16[4,144,256]{2,1,0:T(8,128)(2,1)S(1)}, bf16[4,144,256]{2,1,0:T(8,128)(2,1)S(1)}, u32[]{:S(2)}, u32[]{:S(2)}) collective-permute-start(bf16[4,144,256]{2,1,0:T(8,128)(2,1)S(1)} %collective-permute-done.7.refs_0_), channel_id=1, source_target_pairs={{0,32},{32,0},{64,96},{96,64},{128,160},{160,128},{192,224},{224,1... | collective-permute-start | bytes 884744 | tf_op jit(solution)/shard_map/ppermute | solution.py:152
  44.7 9.7 %collective-permute-start.12 = (bf16[4,144,256]{2,1,0:T(8,128)(2,1)S(1)}, bf16[4,144,256]{2,1,0:T(8,128)(2,1)S(1)}, u32[]{:S(2)}, u32[]{:S(2)}) collective-permute-start(bf16[4,144,256]{2,1,0:T(8,128)(2,1)S(1)} %collective-permute-done.11.refs_1_), channel_id=1, source_target_pairs={{0,32},{32,0},{64,96},{96,64},{128,160},{160,128},{192,224},{224,1... | collective-permute-start | bytes 884744 | tf_op jit(solution)/shard_map/ppermute | solution.py:152
  48.7 8.7 %collective-permute-start.9 = (bf16[4,144,256]{2,1,0:T(8,128)(2,1)S(1)}, bf16[4,144,256]{2,1,0:T(8,128)(2,1)S(1)}, u32[]{:S(2)}, u32[]{:S(2)}) collective-permute-start(bf16[4,144,256]{2,1,0:T(8,128)(2,1)S(1)} %collective-permute-done.8.refs_0_), channel_id=1, source_target_pairs={{0,32},{32,0},{64,96},{96,64},{128,160},{160,128},{192,224},{224,1... | collective-permute-start | bytes 884744 | tf_op jit(solution)/shard_map/ppermute | solution.py:152
  60.5 8.1 %collective-permute-start.14 = (f16[384,256]{1,0:T(8,128)(2,1)S(1)}, f16[384,256]{1,0:T(8,128)(2,1)S(1)}, u32[]{:S(2)}, u32[]{:S(2)}) collective-permute-start(f16[384,256]{1,0:T(8,128)(2,1)S(1)} %get-tuple-element.10), channel_id=1, source_target_pairs={{0,2},{1,3},{2,0},{3,1},{4,6},{5,7},{6,4},{7,5},{8,10},{9,11},{10,... | collective-permute-start | bytes 589832 | tf_op jit(solution)/shard_map/ppermute | solution.py:157
  60.7 12.0 %collective-permute-start.15 = (f16[384,256]{1,0:T(8,128)(2,1)S(1)}, f16[384,256]{1,0:T(8,128)(2,1)S(1)}, u32[]{:S(2)}, u32[]{:S(2)}) collective-permute-start(f16[384,256]{1,0:T(8,128)(2,1)S(1)} %get-tuple-element.11), channel_id=1, source_target_pairs={{0,1},{1,2},{2,3},{3,0},{4,5},{5,6},{6,7},{7,4},{8,9},{9,10},{10,1... | collective-permute-start | bytes 589832 | tf_op jit(solution)/shard_map/ppermute | solution.py:157
  61.9 10.9 %collective-permute-start.16 = (f16[384,256]{1,0:T(8,128)(2,1)S(1)}, f16[384,256]{1,0:T(8,128)(2,1)S(1)}, u32[]{:S(2)}, u32[]{:S(2)}) collective-permute-start(f16[384,256]{1,0:T(8,128)(2,1)S(1)} %get-tuple-element.12), channel_id=1, source_target_pairs={{0,3},{1,0},{2,1},{3,2},{4,7},{5,4},{6,5},{7,6},{8,11},{9,8},{10,9... | collective-permute-start | bytes 589832 | tf_op jit(solution)/shard_map/ppermute | solution.py:157

commit v4 on v3

--- a/solution.py
+++ b/solution.py
@@ -19,8 +19,14 @@
 NOWHERE = -250.0
 
 
-def digits_kernel(where_ref, pos_ref, counts_ref, place_ref, out_ref):
-    start, half = where_ref[1], where_ref[2]
+def digits_kernel(pos_in, counts_in, place_in, out_ref, pos_ref, counts_ref, place_ref, sem):
+    pairs = ((place_in, place_ref), (pos_in, pos_ref), (counts_in, counts_ref))
+    copies = [pltpu.make_async_copy(a, b, sem.at[i]) for i, (a, b) in enumerate(pairs)]
+    for copy in copies:
+        copy.start()
+    for copy in copies:
+        copy.wait()
+    start, half = lax.axis_index("basis") * OWN, (lax.axis_index("dp") & 1) * OWN
     table = place_ref[...]
     high = ((table >> 8) - MIDDLE).astype(jnp.float32).astype(jnp.bfloat16)
     low = (table & 255).astype(jnp.float32).astype(jnp.bfloat16)
@@ -113,28 +119,29 @@
     return jnp.dot(grad, proj, preferred_element_type=jnp.float32)
 
 
-def grads_kernel(payloads, adds, where_ref, factor_ref, *refs):
+def grads_kernel(payloads, adds, factor_ref, *refs):
     payload_refs, refs = refs[:payloads], refs[payloads:]
     olds, (out_ref, words_ref, word_ref, bit_ref) = refs[:adds], refs[adds:]
-    build_words(where_ref[0], payload_refs, words_ref, word_ref, bit_ref)
+    place = lax.axis_index("label") * lax.axis_size("dp") + lax.axis_index("dp")
+    base = place * factor_ref.shape[0]
+    build_words(base, payload_refs, words_ref, word_ref, bit_ref)
     value = block_grads(factor_ref, payload_refs, words_ref)
     out_ref[...] = olds[0][...] + value if adds else value
 
 
 VMEM = pl.BlockSpec(memory_space=pltpu.VMEM)
-SMEM = pl.BlockSpec(memory_space=pltpu.SMEM)
-
-
-def add_grads(where, factors, payloads, *olds):
+ANY = pl.BlockSpec(memory_space=pl.ANY)
+
+
+def add_grads(factors, payloads, *olds):
     rows = factors.shape[0]
     pairs = sum(payload.shape[0] for payload in payloads)
     work = rows * pairs * PAIR
     return pl.pallas_call(
         functools.partial(grads_kernel, len(payloads), len(olds)),
         out_shape=jax.ShapeDtypeStruct((rows, 256), jnp.float32),
-        in_specs=[SMEM] + [VMEM] * (1 + len(payloads) + len(olds)),
+        in_specs=[VMEM] * (1 + len(payloads) + len(olds)),
         out_specs=VMEM,
-        input_output_aliases={2 + len(payloads): 0} if olds else {},
         scratch_shapes=[
             pltpu.VMEM((pairs, rows // 32, 128), jnp.int32),
             pltpu.VMEM((pairs, SLOTS, 128), jnp.int32),
@@ -144,7 +151,7 @@
         cost_estimate=pl.CostEstimate(
             flops=4 * work * 256, bytes_accessed=1 << 22, transcendentals=work
         ),
-    )(where, factors, *payloads, *olds)
+    )(factors, *payloads, *olds)
 
 
 def swap(value, axis, bit):
@@ -165,25 +172,27 @@
 
 
 def body(queries, basis, factors, positives, counts, placement):
-    label, dp, part = lax.axis_index("label"), lax.axis_index("dp"), lax.axis_index("basis")
+    dp, part = lax.axis_index("dp"), lax.axis_index("basis")
     block = factors.shape[0] // lax.axis_size("dp")
-    half = (dp & 1) * OWN
     mine = lax.dynamic_slice_in_dim(factors, dp * block, block, 0)
     partial_value = lax.dot_general(
         queries, basis, (((1,), (1,)), ((), ())), preferred_element_type=jnp.float32
     )
-    first_row = label * factors.shape[0] + dp * block
-    where = jnp.stack([first_row, part * OWN, half]).astype(jnp.int32)
     digits = pl.pallas_call(
         digits_kernel,
         out_shape=jax.ShapeDtypeStruct((EXTRA, 256), jnp.bfloat16),
-        in_specs=[SMEM, VMEM, VMEM, VMEM],
+        in_specs=[ANY, ANY, ANY],
         out_specs=VMEM,
+        scratch_shapes=[
+            pltpu.VMEM(positives.shape[::-1], jnp.int32),
+            pltpu.VMEM((1, counts.shape[0]), jnp.int32),
+            pltpu.VMEM((placement.shape[0] // 128, 128), jnp.int32),
+            pltpu.SemaphoreType.DMA((3,)),
+        ],
         cost_estimate=pl.CostEstimate(
             flops=1 << 31, bytes_accessed=1 << 19, transcendentals=0
         ),
     )(
-        where,
         positives.T,
         counts.reshape(1, -1),
         placement.reshape(-1, 128),
@@ -197,7 +206,7 @@
     moved = [shift_by(piece_of(partial_value, step), "basis", step) for step in (2, 1, 3)]
     for value in moved:
         rows = rows + value
-    own = jnp.concatenate([rows.astype(jnp.bfloat16), digits], axis=0)
+    own = lax.optimization_barrier(jnp.concatenate([rows.astype(jnp.bfloat16), digits], axis=0))
     next_own = swap(own, "dp", 1)
     even = dp & 1 == 0
     pair = jnp.concatenate(
@@ -211,16 +220,17 @@
     others = [shift_by(pair, "dp", step) for step in (2, 6, 4)]
     ring = jnp.concatenate([pair] + others, axis=0)
 
-    near = [turn(ring, 1), turn(ring, -1)]
+    near = [turn(ring, 1)]
+    near.append(turn(ring, -1))
     ring_other = swap(ring, "label", 1)
     far = turn(near[0], 1)
     near_other = [swap(value, "label", 1) for value in near]
     far_other = swap(far, "label", 1)
-    sums = add_grads(where, mine, [ring])
-    sums = add_grads(where, mine, [ring_other], sums)
-    sums = add_grads(where, mine, near, sums)
-    sums = add_grads(where, mine, near_other, sums)
-    sums = add_grads(where, mine, [far, far_other], sums)
+    sums = add_grads(mine, [ring])
+    sums = add_grads(mine, [ring_other], sums)
+    sums = add_grads(mine, near, sums)
+    sums = add_grads(mine, near_other, sums)
+    sums = add_grads(mine, [far, far_other], sums)
 
     order = (2, 1, 3)
     quarters = [piece_of(sums, step) for step in (0,) + order]

time: 73.8 us -> 71 us (0.962)
  Pallas kernels: 15.3 us -> 12.2 us
  starting transfers between devices: 37.4 us -> 39.3 us
  other arithmetic: 3.14 us -> 1.79 us
    pallas_call x5, Pallas kernels: 12.8 us -> 9.7 us  [add_grads(): pl.pallas_call(functools.partial(grads_kernel, len(payloads), len(olds)),...]
    ppermute x5, starting transfers between devices: 12.8 us -> 14 us  [swap(): return lax.ppermute(value, axis, [(i, i ^ bit) for i in range(size)])]
  transfers between devices with their start and end apart: 17 -> 17, of which waited for: 4 -> 4; matrix products, arithmetic and copies ran while one was open for 3% -> 2% of each run, Pallas kernels for 17% -> 14%
where the time goes in v4:
time: 71 us; the launch traced here: 70.7 us
  starting transfers between devices  39.3 us (55%)
  waiting for transfers between devices  14 us (20%)
  Pallas kernels  12.2 us (17%)
  local copies, waits for them, and re-layouts  2.16 us (3%)
  other arithmetic  1.79 us (3%)
  matrix products  1.21 us (2%)
    ppermute x9, starting transfers between devices, shift_by(): lax.ppermute(value, axis, [(i, (i + step * inner) % size) for i in range(...  20.4 us
    ppermute x5, starting transfers between devices, swap(): return lax.ppermute(value, axis, [(i, i ^ bit) for i in range(size)])  14 us
    ppermute x9, waiting for transfers between devices, shift_by(): lax.ppermute(value, axis, [(i, (i + step * inner) % size) for i in range(...  12.6 us
    pallas_call x5, Pallas kernels, add_grads(): pl.pallas_call(functools.partial(grads_kernel, len(payloads), len(olds)),...  9.7 us
    ppermute x3, starting transfers between devices, turn(): lax.ppermute(value, 'label', [(i, (i + (2 - 4 * (i % 2)) * step) % size)...  4.88 us
    pallas_call x1, Pallas kernels, body(): pl.pallas_call(digits_kernel, out_shape=jax.ShapeDtypeStruct((EXTRA, 256)...  2.45 us
  transfers between devices with their start and end apart: 17, of which 4 were waited for; matrix products, arithmetic and copies ran while one was open for 2% of the time, Pallas kernels for 14%

profile of v4, /device:TPU:1, one launch (start us, length us, event | category | flops | bytes accessed | tf_op | source)
XLA Modules:
  0.0 70.7 jit_solution(15777761529087486468)
XLA Ops:
  1.0 1.2 %fusion = f32[256,256]{1,0:T(8,128)S(1)} fusion(bf16[256,512]{1,0:T(8,128)(2,1)S(1)} %copy-done, bf16[256,512]{1,0:T(8,128)(2,1)} %param.7), kind=kOutput, calls=%fused_computation.17 | convolution fusion | flops 67108864 | bytes 786432 | tf_op jit(solution)/shard_map/dot_general | solution.py:178
  2.2 3.8 %collective-permute-start = (f32[64,256]{1,0:T(8,128)S(1)}, f32[64,256]{1,0:T(8,128)S(1)}, u32[]{:S(2)}, u32[]{:S(2)}) collective-permute-start(f32[64,256]{1,0:T(8,128)S(1)} %get-tuple-element.17), channel_id=1, source_target_pairs={{0,2},{1,3},{2,0},{3,1},{4,6},{5,7},{6,4},{7,5},{8,10},{9,11},{10,... | collective-permute-start | bytes 196616 | tf_op jit(solution)/shard_map/ppermute | solution.py:164
  6.4 2.3 %collective-permute-start.2 = (f32[64,256]{1,0:T(8,128)S(1)}, f32[64,256]{1,0:T(8,128)S(1)}, u32[]{:S(2)}, u32[]{:S(2)}) collective-permute-start(f32[64,256]{1,0:T(8,128)S(1)} %get-tuple-element.18), channel_id=1, source_target_pairs={{0,3},{1,0},{2,1},{3,2},{4,7},{5,4},{6,5},{7,6},{8,11},{9,8},{10,9... | collective-permute-start | bytes 196616 | tf_op jit(solution)/shard_map/ppermute | solution.py:164
  8.7 2.5 %shard_map.64 = bf16[16,256]{1,0:T(8,128)(2,1)} custom-call(s32[16,256]{1,0:T(8,128)} %bitcast.8, s32[1,256]{1,0:T(1,128)} %bitcast.9, s32[768,128]{1,0:T(8,128)} %bitcast.7), custom_call_target="tpu_custom_call" | custom-call | flops 2147483648 | bytes 524288 | tf_op jit(solution)/shard_map/pallas_call | solution.py:181
  11.9 1.6 %collective-permute-start.3 = (bf16[80,256]{1,0:T(8,128)(2,1)S(1)}, bf16[80,256]{1,0:T(8,128)(2,1)S(1)}, u32[]{:S(2)}, u32[]{:S(2)}) collective-permute-start(bf16[80,256]{1,0:T(8,128)(2,1)S(1)} %pad_maximum_fusion.1), channel_id=1, source_target_pairs={{0,4},{4,0},{8,12},{12,8},{16,20},{20,16},{24,28},{28,24},{1,5},{5... | collective-permute-start | bytes 122888 | tf_op jit(solution)/shard_map/ppermute | solution.py:159
  13.6 1.4 %collective-permute-done.3 = bf16[80,256]{1,0:T(8,128)(2,1)S(1)} collective-permute-done((bf16[80,256]{1,0:T(8,128)(2,1)S(1)}, bf16[80,256]{1,0:T(8,128)(2,1)S(1)}, u32[]{:S(2)}, u32[]{:S(2)}) %collective-permute-start.3) | collective-permute-done | bytes 40992 | tf_op jit(solution)/shard_map/ppermute | solution.py:159
  15.0 3.1 %collective-permute-start.4 = (bf16[1,144,256]{2,1,0:T(8,128)(2,1)S(1)}, bf16[1,144,256]{2,1,0:T(8,128)(2,1)S(1)}, u32[]{:S(2)}, u32[]{:S(2)}) collective-permute-start(bf16[1,144,256]{2,1,0:T(8,128)(2,1)S(1)} %maximum_bitcast_fusion), channel_id=1, source_target_pairs={{0,8},{4,12},{8,16},{12,20},{16,24},{20,28},{24,0},{28,4},{1,9},{5... | collective-permute-start | bytes 221192 | tf_op jit(solution)/shard_map/ppermute | solution.py:164
  18.1 2.9 %collective-permute-start.5 = (bf16[1,144,256]{2,1,0:T(8,128)(2,1)S(1)}, bf16[1,144,256]{2,1,0:T(8,128)(2,1)S(1)}, u32[]{:S(2)}, u32[]{:S(2)}) collective-permute-start(bf16[1,144,256]{2,1,0:T(8,128)(2,1)S(1)} %maximum_bitcast_fusion), channel_id=1, source_target_pairs={{0,24},{4,28},{8,0},{12,4},{16,8},{20,12},{24,16},{28,20},{1,25},{... | collective-permute-start | bytes 221192 | tf_op jit(solution)/shard_map/ppermute | solution.py:164
  21.0 4.4 %collective-permute-start.6 = (bf16[1,144,256]{2,1,0:T(8,128)(2,1)S(1)}, bf16[1,144,256]{2,1,0:T(8,128)(2,1)S(1)}, u32[]{:S(2)}, u32[]{:S(2)}) collective-permute-start(bf16[1,144,256]{2,1,0:T(8,128)(2,1)S(1)} %maximum_bitcast_fusion), channel_id=1, source_target_pairs={{0,16},{4,20},{8,24},{12,28},{16,0},{20,4},{24,8},{28,12},{1,17},{... | collective-permute-start | bytes 221192 | tf_op jit(solution)/shard_map/ppermute | solution.py:164
  25.4 3.5 %collective-permute-done.6 = bf16[1,144,256]{2,1,0:T(8,128)(2,1)S(1)} collective-permute-done((bf16[1,144,256]{2,1,0:T(8,128)(2,1)S(1)}, bf16[1,144,256]{2,1,0:T(8,128)(2,1)S(1)}, u32[]{:S(2)}, u32[]{:S(2)}) %collective-permute-start.6) | collective-permute-done | bytes 73760 | tf_op jit(solution)/shard_map/ppermute | solution.py:164
  28.9 2.6 %collective-permute-start.7 = (bf16[4,144,256]{2,1,0:T(8,128)(2,1)S(1)}, bf16[4,144,256]{2,1,0:T(8,128)(2,1)S(1)}, u32[]{:S(2)}, u32[]{:S(2)}) collective-permute-start(bf16[4,144,256]{2,1,0:T(8,128)(2,1)S(1)} %pad_maximum_fusion.refs_0_), channel_id=1, source_target_pairs={{0,64},{32,224},{64,128},{96,32},{128,192},{160,96},{192,0},{224,1... | collective-permute-start | bytes 884744 | tf_op jit(solution)/shard_map/ppermute | solution.py:169
  31.5 4.5 %collective-permute-start.13 = (bf16[4,144,256]{2,1,0:T(8,128)(2,1)S(1)}, bf16[4,144,256]{2,1,0:T(8,128)(2,1)S(1)}, u32[]{:S(2)}, u32[]{:S(2)}) collective-permute-start(bf16[4,144,256]{2,1,0:T(8,128)(2,1)S(1)} %pad_maximum_fusion.refs_0_), channel_id=1, source_target_pairs={{0,32},{32,0},{64,96},{96,64},{128,160},{160,128},{192,224},{224,1... | collective-permute-start | bytes 884744 | tf_op jit(solution)/shard_map/ppermute | solution.py:159
  35.9 2.3 %collective-permute-start.8 = (bf16[4,144,256]{2,1,0:T(8,128)(2,1)S(1)}, bf16[4,144,256]{2,1,0:T(8,128)(2,1)S(1)}, u32[]{:S(2)}, u32[]{:S(2)}) collective-permute-start(bf16[4,144,256]{2,1,0:T(8,128)(2,1)S(1)} %collective-permute-done.7.refs_0_), channel_id=1, source_target_pairs={{0,64},{32,224},{64,128},{96,32},{128,192},{160,96},{192,0},{224,1... | collective-permute-start | bytes 884744 | tf_op jit(solution)/shard_map/ppermute | solution.py:169
  38.2 1.2 %constant_dynamic-slice_fusion.4.factor_ref = bf16[1536,256]{1,0:T(8,128)(2,1)S(1)} fusion(bf16[12288,256]{1,0:T(8,128)(2,1)} %param.8, s32[]{:T(128)S(6)} %select_n.39), kind=kLoop, calls=%fused_computation.16 | loop fusion | bytes 1572868 | tf_op jit(solution)/shard_map/dynamic_slice | solution.py:177
  39.4 3.9 %collective-permute-start.10 = (bf16[4,144,256]{2,1,0:T(8,128)(2,1)S(1)}, bf16[4,144,256]{2,1,0:T(8,128)(2,1)S(1)}, u32[]{:S(2)}, u32[]{:S(2)}) collective-permute-start(bf16[4,144,256]{2,1,0:T(8,128)(2,1)S(1)} %collective-permute-done.7.refs_0_), channel_id=1, source_target_pairs={{0,32},{32,0},{64,96},{96,64},{128,160},{160,128},{192,224},{224,1... | collective-permute-start | bytes 884744 | tf_op jit(solution)/shard_map/ppermute | solution.py:159
  43.5 1.3 %shard_map.65.refs_1_ = f32[1536,256]{1,0:T(8,128)S(1)} custom-call(bf16[1536,256]{1,0:T(8,128)(2,1)S(1)} %constant_dynamic-slice_fusion.4.factor_ref, bf16[4,144,256]{2,1,0:T(8,128)(2,1)S(1)} %pad_maximum_fusion.refs_0_), custom_call_target="tpu_custom_call" | custom-call | flops 805306368 | bytes 4194304 | tf_op jit(solution)/shard_map/pallas_call | solution.py:140
  44.8 1.3 %shard_map.66.refs_2_ = f32[1536,256]{1,0:T(8,128)S(1)} custom-call(bf16[1536,256]{1,0:T(8,128)(2,1)S(1)} %constant_dynamic-slice_fusion.4.factor_ref, bf16[4,144,256]{2,1,0:T(8,128)(2,1)S(1)} %collective-permute-done.13.refs_0_, f32[1536,256]{1,0:T(8,128)S(1)} %shard_map.65.refs_1_), custom_call_target="tpu_custom_call" | custom-call | flops 805306368 | bytes 4194304 | tf_op jit(solution)/shard_map/pallas_call | solution.py:140
  46.2 3.9 %collective-permute-start.9 = (bf16[4,144,256]{2,1,0:T(8,128)(2,1)S(1)}, bf16[4,144,256]{2,1,0:T(8,128)(2,1)S(1)}, u32[]{:S(2)}, u32[]{:S(2)}) collective-permute-start(bf16[4,144,256]{2,1,0:T(8,128)(2,1)S(1)} %collective-permute-done.8.refs_0_), channel_id=1, source_target_pairs={{0,32},{32,0},{64,96},{96,64},{128,160},{160,128},{192,224},{224,1... | collective-permute-start | bytes 884744 | tf_op jit(solution)/shard_map/ppermute | solution.py:159
  50.0 2.3 %shard_map.67.refs_2_ = f32[1536,256]{1,0:T(8,128)S(1)} custom-call(bf16[1536,256]{1,0:T(8,128)(2,1)S(1)} %constant_dynamic-slice_fusion.4.factor_ref, bf16[4,144,256]{2,1,0:T(8,128)(2,1)S(1)} %collective-permute-done.7.refs_0_, bf16[4,144,256]{2,1,0:T(8,128)(2,1)S(1)} %collective-permute-done.11.refs_1_, f32[1536,256]{1,0:T(8,128)S(1)} %shard_map.66.refs_2_), custom_call_target="tpu_custom_call" | custom-call | flops 1610612736 | bytes 4194304 | tf_op jit(solution)/shard_map/pallas_call | solution.py:140
  52.4 2.4 %shard_map.68.refs_2_ = f32[1536,256]{1,0:T(8,128)S(1)} custom-call(bf16[1536,256]{1,0:T(8,128)(2,1)S(1)} %constant_dynamic-slice_fusion.4.factor_ref, bf16[4,144,256]{2,1,0:T(8,128)(2,1)S(1)} %collective-permute-done.10.refs_0_, bf16[4,144,256]{2,1,0:T(8,128)(2,1)S(1)} %collective-permute-done.12.refs_1_, f32[1536,256]{1,0:T(8,128)S(1)} %shard_map.67.refs_2_), custom_call_target="tpu_custom_call" | custom-call | flops 1610612736 | bytes 4194304 | tf_op jit(solution)/shard_map/pallas_call | solution.py:140
  54.8 2.4 %shard_map.69 = f32[1536,256]{1,0:T(8,128)S(1)} custom-call(bf16[1536,256]{1,0:T(8,128)(2,1)S(1)} %constant_dynamic-slice_fusion.4.factor_ref, bf16[4,144,256]{2,1,0:T(8,128)(2,1)S(1)} %collective-permute-done.8.refs_0_, bf16[4,144,256]{2,1,0:T(8,128)(2,1)S(1)} %collective-permute-done.9.refs_1_, f32[1536,256]{1,0:T(8,128)S(1)} %shard_map.68.refs_2_), custom_call_target="tpu_custom_call" | custom-call | flops 1610612736 | bytes 4194304 | tf_op jit(solution)/shard_map/pallas_call | solution.py:140
  59.3 1.5 %collective-permute-start.16 = (f16[384,256]{1,0:T(8,128)(2,1)S(1)}, f16[384,256]{1,0:T(8,128)(2,1)S(1)}, u32[]{:S(2)}, u32[]{:S(2)}) collective-permute-start(f16[384,256]{1,0:T(8,128)(2,1)S(1)} %get-tuple-element.12), channel_id=1, source_target_pairs={{0,3},{1,0},{2,1},{3,2},{4,7},{5,4},{6,5},{7,6},{8,11},{9,8},{10,9... | collective-permute-start | bytes 589832 | tf_op jit(solution)/shard_map/ppermute | solution.py:164
  60.8 4.6 %collective-permute-done.14 = f16[384,256]{1,0:T(8,128)(2,1)S(1)} collective-permute-done((f16[384,256]{1,0:T(8,128)(2,1)S(1)}, f16[384,256]{1,0:T(8,128)(2,1)S(1)}, u32[]{:S(2)}, u32[]{:S(2)}) %collective-permute-start.14) | collective-permute-done | bytes 196640 | tf_op jit(solution)/shard_map/ppermute | solution.py:164
  65.4 4.5 %collective-permute-done.15 = f16[384,256]{1,0:T(8,128)(2,1)S(1)} collective-permute-done((f16[384,256]{1,0:T(8,128)(2,1)S(1)}, f16[384,256]{1,0:T(8,128)(2,1)S(1)}, u32[]{:S(2)}, u32[]{:S(2)}) %collective-permute-start.15) | collective-permute-done | bytes 196640 | tf_op jit(solution)/shard_map/ppermute | solution.py:164
  (30 shorter events, 5.3 us)
Async XLA Ops:
  0.0 1.0 %copy-start = (bf16[256,512]{1,0:T(8,128)(2,1)S(1)}, bf16[256,512]{1,0:T(8,128)(2,1)}, u32[]{:S(2)}) copy-start(bf16[256,512]{1,0:T(8,128)(2,1)} %param.6) | copy-start | bytes 786436
  2.2 9.0 %collective-permute-start = (f32[64,256]{1,0:T(8,128)S(1)}, f32[64,256]{1,0:T(8,128)S(1)}, u32[]{:S(2)}, u32[]{:S(2)}) collective-permute-start(f32[64,256]{1,0:T(8,128)S(1)} %get-tuple-element.17), channel_id=1, source_target_pairs={{0,2},{1,3},{2,0},{3,1},{4,6},{5,7},{6,4},{7,5},{8,10},{9,11},{10,... | collective-permute-start | bytes 196616 | tf_op jit(solution)/shard_map/ppermute | solution.py:164
  6.0 5.2 %collective-permute-start.1 = (f32[64,256]{1,0:T(8,128)S(1)}, f32[64,256]{1,0:T(8,128)S(1)}, u32[]{:S(2)}, u32[]{:S(2)}) collective-permute-start(f32[64,256]{1,0:T(8,128)S(1)} %get-tuple-element.19), channel_id=1, source_target_pairs={{0,1},{1,2},{2,3},{3,0},{4,5},{5,6},{6,7},{7,4},{8,9},{9,10},{10,1... | collective-permute-start | bytes 196616 | tf_op jit(solution)/shard_map/ppermute | solution.py:164
  6.4 4.8 %collective-permute-start.2 = (f32[64,256]{1,0:T(8,128)S(1)}, f32[64,256]{1,0:T(8,128)S(1)}, u32[]{:S(2)}, u32[]{:S(2)}) collective-permute-start(f32[64,256]{1,0:T(8,128)S(1)} %get-tuple-element.18), channel_id=1, source_target_pairs={{0,3},{1,0},{2,1},{3,2},{4,7},{5,4},{6,5},{7,6},{8,11},{9,8},{10,9... | collective-permute-start | bytes 196616 | tf_op jit(solution)/shard_map/ppermute | solution.py:164
  11.9 3.0 %collective-permute-start.3 = (bf16[80,256]{1,0:T(8,128)(2,1)S(1)}, bf16[80,256]{1,0:T(8,128)(2,1)S(1)}, u32[]{:S(2)}, u32[]{:S(2)}) collective-permute-start(bf16[80,256]{1,0:T(8,128)(2,1)S(1)} %pad_maximum_fusion.1), channel_id=1, source_target_pairs={{0,4},{4,0},{8,12},{12,8},{16,20},{20,16},{24,28},{28,24},{1,5},{5... | collective-permute-start | bytes 122888 | tf_op jit(solution)/shard_map/ppermute | solution.py:159
  15.0 10.4 %collective-permute-start.4 = (bf16[1,144,256]{2,1,0:T(8,128)(2,1)S(1)}, bf16[1,144,256]{2,1,0:T(8,128)(2,1)S(1)}, u32[]{:S(2)}, u32[]{:S(2)}) collective-permute-start(bf16[1,144,256]{2,1,0:T(8,128)(2,1)S(1)} %maximum_bitcast_fusion), channel_id=1, source_target_pairs={{0,8},{4,12},{8,16},{12,20},{16,24},{20,28},{24,0},{28,4},{1,9},{5... | collective-permute-start | bytes 221192 | tf_op jit(solution)/shard_map/ppermute | solution.py:164
  18.1 7.3 %collective-permute-start.5 = (bf16[1,144,256]{2,1,0:T(8,128)(2,1)S(1)}, bf16[1,144,256]{2,1,0:T(8,128)(2,1)S(1)}, u32[]{:S(2)}, u32[]{:S(2)}) collective-permute-start(bf16[1,144,256]{2,1,0:T(8,128)(2,1)S(1)} %maximum_bitcast_fusion), channel_id=1, source_target_pairs={{0,24},{4,28},{8,0},{12,4},{16,8},{20,12},{24,16},{28,20},{1,25},{... | collective-permute-start | bytes 221192 | tf_op jit(solution)/shard_map/ppermute | solution.py:164
  21.0 7.9 %collective-permute-start.6 = (bf16[1,144,256]{2,1,0:T(8,128)(2,1)S(1)}, bf16[1,144,256]{2,1,0:T(8,128)(2,1)S(1)}, u32[]{:S(2)}, u32[]{:S(2)}) collective-permute-start(bf16[1,144,256]{2,1,0:T(8,128)(2,1)S(1)} %maximum_bitcast_fusion), channel_id=1, source_target_pairs={{0,16},{4,20},{8,24},{12,28},{16,0},{20,4},{24,8},{28,12},{1,17},{... | collective-permute-start | bytes 221192 | tf_op jit(solution)/shard_map/ppermute | solution.py:164
  28.9 7.0 %collective-permute-start.7 = (bf16[4,144,256]{2,1,0:T(8,128)(2,1)S(1)}, bf16[4,144,256]{2,1,0:T(8,128)(2,1)S(1)}, u32[]{:S(2)}, u32[]{:S(2)}) collective-permute-start(bf16[4,144,256]{2,1,0:T(8,128)(2,1)S(1)} %pad_maximum_fusion.refs_0_), channel_id=1, source_target_pairs={{0,64},{32,224},{64,128},{96,32},{128,192},{160,96},{192,0},{224,1... | collective-permute-start | bytes 884744 | tf_op jit(solution)/shard_map/ppermute | solution.py:169
  31.5 11.9 %collective-permute-start.11 = (bf16[4,144,256]{2,1,0:T(8,128)(2,1)S(1)}, bf16[4,144,256]{2,1,0:T(8,128)(2,1)S(1)}, u32[]{:S(2)}, u32[]{:S(2)}) collective-permute-start(bf16[4,144,256]{2,1,0:T(8,128)(2,1)S(1)} %pad_maximum_fusion.refs_0_), channel_id=1, source_target_pairs={{0,192},{32,96},{64,0},{96,160},{128,64},{160,224},{192,128},{224,... | collective-permute-start | bytes 884744 | tf_op jit(solution)/shard_map/ppermute | solution.py:169
  31.5 13.3 %collective-permute-start.13 = (bf16[4,144,256]{2,1,0:T(8,128)(2,1)S(1)}, bf16[4,144,256]{2,1,0:T(8,128)(2,1)S(1)}, u32[]{:S(2)}, u32[]{:S(2)}) collective-permute-start(bf16[4,144,256]{2,1,0:T(8,128)(2,1)S(1)} %pad_maximum_fusion.refs_0_), channel_id=1, source_target_pairs={{0,32},{32,0},{64,96},{96,64},{128,160},{160,128},{192,224},{224,1... | collective-permute-start | bytes 884744 | tf_op jit(solution)/shard_map/ppermute | solution.py:159
  35.9 10.2 %collective-permute-start.8 = (bf16[4,144,256]{2,1,0:T(8,128)(2,1)S(1)}, bf16[4,144,256]{2,1,0:T(8,128)(2,1)S(1)}, u32[]{:S(2)}, u32[]{:S(2)}) collective-permute-start(bf16[4,144,256]{2,1,0:T(8,128)(2,1)S(1)} %collective-permute-done.7.refs_0_), channel_id=1, source_target_pairs={{0,64},{32,224},{64,128},{96,32},{128,192},{160,96},{192,0},{224,1... | collective-permute-start | bytes 884744 | tf_op jit(solution)/shard_map/ppermute | solution.py:169
  39.4 13.0 %collective-permute-start.10 = (bf16[4,144,256]{2,1,0:T(8,128)(2,1)S(1)}, bf16[4,144,256]{2,1,0:T(8,128)(2,1)S(1)}, u32[]{:S(2)}, u32[]{:S(2)}) collective-permute-start(bf16[4,144,256]{2,1,0:T(8,128)(2,1)S(1)} %collective-permute-done.7.refs_0_), channel_id=1, source_target_pairs={{0,32},{32,0},{64,96},{96,64},{128,160},{160,128},{192,224},{224,1... | collective-permute-start | bytes 884744 | tf_op jit(solution)/shard_map/ppermute | solution.py:159
  43.4 9.0 %collective-permute-start.12 = (bf16[4,144,256]{2,1,0:T(8,128)(2,1)S(1)}, bf16[4,144,256]{2,1,0:T(8,128)(2,1)S(1)}, u32[]{:S(2)}, u32[]{:S(2)}) collective-permute-start(bf16[4,144,256]{2,1,0:T(8,128)(2,1)S(1)} %collective-permute-done.11.refs_1_), channel_id=1, source_target_pairs={{0,32},{32,0},{64,96},{96,64},{128,160},{160,128},{192,224},{224,1... | collective-permute-start | bytes 884744 | tf_op jit(solution)/shard_map/ppermute | solution.py:159
  46.2 8.6 %collective-permute-start.9 = (bf16[4,144,256]{2,1,0:T(8,128)(2,1)S(1)}, bf16[4,144,256]{2,1,0:T(8,128)(2,1)S(1)}, u32[]{:S(2)}, u32[]{:S(2)}) collective-permute-start(bf16[4,144,256]{2,1,0:T(8,128)(2,1)S(1)} %collective-permute-done.8.refs_0_), channel_id=1, source_target_pairs={{0,32},{32,0},{64,96},{96,64},{128,160},{160,128},{192,224},{224,1... | collective-permute-start | bytes 884744 | tf_op jit(solution)/shard_map/ppermute | solution.py:159
  57.3 8.1 %collective-permute-start.14 = (f16[384,256]{1,0:T(8,128)(2,1)S(1)}, f16[384,256]{1,0:T(8,128)(2,1)S(1)}, u32[]{:S(2)}, u32[]{:S(2)}) collective-permute-start(f16[384,256]{1,0:T(8,128)(2,1)S(1)} %get-tuple-element.10), channel_id=1, source_target_pairs={{0,2},{1,3},{2,0},{3,1},{4,6},{5,7},{6,4},{7,5},{8,10},{9,11},{10,... | collective-permute-start | bytes 589832 | tf_op jit(solution)/shard_map/ppermute | solution.py:164
  58.1 11.8 %collective-permute-start.15 = (f16[384,256]{1,0:T(8,128)(2,1)S(1)}, f16[384,256]{1,0:T(8,128)(2,1)S(1)}, u32[]{:S(2)}, u32[]{:S(2)}) collective-permute-start(f16[384,256]{1,0:T(8,128)(2,1)S(1)} %get-tuple-element.11), channel_id=1, source_target_pairs={{0,1},{1,2},{2,3},{3,0},{4,5},{5,6},{6,7},{7,4},{8,9},{9,10},{10,1... | collective-permute-start | bytes 589832 | tf_op jit(solution)/shard_map/ppermute | solution.py:164
  59.3 10.7 %collective-permute-start.16 = (f16[384,256]{1,0:T(8,128)(2,1)S(1)}, f16[384,256]{1,0:T(8,128)(2,1)S(1)}, u32[]{:S(2)}, u32[]{:S(2)}) collective-permute-start(f16[384,256]{1,0:T(8,128)(2,1)S(1)} %get-tuple-element.12), channel_id=1, source_target_pairs={{0,3},{1,0},{2,1},{3,2},{4,7},{5,4},{6,5},{7,6},{8,11},{9,8},{10,9... | collective-permute-start | bytes 589832 | tf_op jit(solution)/shard_map/ppermute | solution.py:164

commit v5 on v4

--- a/solution.py
+++ b/solution.py
@@ -229,11 +229,11 @@
     sums = add_grads(mine, [ring])
     sums = add_grads(mine, [ring_other], sums)
     sums = add_grads(mine, near, sums)
-    sums = add_grads(mine, near_other, sums)
-    sums = add_grads(mine, [far, far_other], sums)
+    later = add_grads(mine, near_other)
+    later = add_grads(mine, [far, far_other], later)
 
     order = (2, 1, 3)
-    quarters = [piece_of(sums, step) for step in (0,) + order]
+    quarters = [piece_of(sums, step) + piece_of(later, step) for step in (0,) + order]
     total, *sent = lax.optimization_barrier(
         (quarters[0], *((value * SCALE).astype(LINK) for value in quarters[1:]))
     )

time: 71 us -> 71.1 us (level)
  no operation moved by 1% of the time
where the time goes in v5:
time: 71.1 us; the launch traced here: 70.9 us
  starting transfers between devices  39.3 us (55%)
  waiting for transfers between devices  14 us (20%)
  Pallas kernels  12.2 us (17%)
  local copies, waits for them, and re-layouts  2.16 us (3%)
  other arithmetic  1.9 us (3%)
  matrix products  1.21 us (2%)
    ppermute x9, starting transfers between devices, shift_by(): lax.ppermute(value, axis, [(i, (i + step * inner) % size) for i in range(...  20.4 us
    ppermute x5, starting transfers between devices, swap(): return lax.ppermute(value, axis, [(i, i ^ bit) for i in range(size)])  14 us
    ppermute x9, waiting for transfers between devices, shift_by(): lax.ppermute(value, axis, [(i, (i + step * inner) % size) for i in range(...  12.6 us
    pallas_call x5, Pallas kernels, add_grads(): pl.pallas_call(functools.partial(grads_kernel, len(payloads), len(olds)),...  9.7 us
    ppermute x3, starting transfers between devices, turn(): lax.ppermute(value, 'label', [(i, (i + (2 - 4 * (i % 2)) * step) % size)...  4.88 us
    pallas_call x1, Pallas kernels, body(): pl.pallas_call(digits_kernel, out_shape=jax.ShapeDtypeStruct((EXTRA, 256)...  2.45 us
  transfers between devices with their start and end apart: 17, of which 4 were waited for; matrix products, arithmetic and copies ran while one was open for 2% of the time, Pallas kernels for 14%

profile of v5, /device:TPU:1, one launch (start us, length us, event | category | flops | bytes accessed | tf_op | source)
XLA Modules:
  0.0 70.9 jit_solution(3736315028459392373)
XLA Ops:
  1.0 1.2 %fusion = f32[256,256]{1,0:T(8,128)S(1)} fusion(bf16[256,512]{1,0:T(8,128)(2,1)S(1)} %copy-done, bf16[256,512]{1,0:T(8,128)(2,1)} %param.7), kind=kOutput, calls=%fused_computation.17 | convolution fusion | flops 67108864 | bytes 786432 | tf_op jit(solution)/shard_map/dot_general | solution.py:178
  2.2 3.8 %collective-permute-start = (f32[64,256]{1,0:T(8,128)S(1)}, f32[64,256]{1,0:T(8,128)S(1)}, u32[]{:S(2)}, u32[]{:S(2)}) collective-permute-start(f32[64,256]{1,0:T(8,128)S(1)} %get-tuple-element.17), channel_id=1, source_target_pairs={{0,2},{1,3},{2,0},{3,1},{4,6},{5,7},{6,4},{7,5},{8,10},{9,11},{10,... | collective-permute-start | bytes 196616 | tf_op jit(solution)/shard_map/ppermute | solution.py:164
  6.4 2.3 %collective-permute-start.2 = (f32[64,256]{1,0:T(8,128)S(1)}, f32[64,256]{1,0:T(8,128)S(1)}, u32[]{:S(2)}, u32[]{:S(2)}) collective-permute-start(f32[64,256]{1,0:T(8,128)S(1)} %get-tuple-element.18), channel_id=1, source_target_pairs={{0,3},{1,0},{2,1},{3,2},{4,7},{5,4},{6,5},{7,6},{8,11},{9,8},{10,9... | collective-permute-start | bytes 196616 | tf_op jit(solution)/shard_map/ppermute | solution.py:164
  8.7 2.5 %shard_map.64 = bf16[16,256]{1,0:T(8,128)(2,1)} custom-call(s32[16,256]{1,0:T(8,128)} %bitcast.8, s32[1,256]{1,0:T(1,128)} %bitcast.9, s32[768,128]{1,0:T(8,128)} %bitcast.7), custom_call_target="tpu_custom_call" | custom-call | flops 2147483648 | bytes 524288 | tf_op jit(solution)/shard_map/pallas_call | solution.py:181
  11.9 1.6 %collective-permute-start.3 = (bf16[80,256]{1,0:T(8,128)(2,1)S(1)}, bf16[80,256]{1,0:T(8,128)(2,1)S(1)}, u32[]{:S(2)}, u32[]{:S(2)}) collective-permute-start(bf16[80,256]{1,0:T(8,128)(2,1)S(1)} %pad_maximum_fusion.1), channel_id=1, source_target_pairs={{0,4},{4,0},{8,12},{12,8},{16,20},{20,16},{24,28},{28,24},{1,5},{5... | collective-permute-start | bytes 122888 | tf_op jit(solution)/shard_map/ppermute | solution.py:159
  13.6 1.4 %collective-permute-done.3 = bf16[80,256]{1,0:T(8,128)(2,1)S(1)} collective-permute-done((bf16[80,256]{1,0:T(8,128)(2,1)S(1)}, bf16[80,256]{1,0:T(8,128)(2,1)S(1)}, u32[]{:S(2)}, u32[]{:S(2)}) %collective-permute-start.3) | collective-permute-done | bytes 40992 | tf_op jit(solution)/shard_map/ppermute | solution.py:159
  15.0 3.1 %collective-permute-start.4 = (bf16[1,144,256]{2,1,0:T(8,128)(2,1)S(1)}, bf16[1,144,256]{2,1,0:T(8,128)(2,1)S(1)}, u32[]{:S(2)}, u32[]{:S(2)}) collective-permute-start(bf16[1,144,256]{2,1,0:T(8,128)(2,1)S(1)} %maximum_bitcast_fusion), channel_id=1, source_target_pairs={{0,8},{4,12},{8,16},{12,20},{16,24},{20,28},{24,0},{28,4},{1,9},{5... | collective-permute-start | bytes 221192 | tf_op jit(solution)/shard_map/ppermute | solution.py:164
  18.1 2.9 %collective-permute-start.5 = (bf16[1,144,256]{2,1,0:T(8,128)(2,1)S(1)}, bf16[1,144,256]{2,1,0:T(8,128)(2,1)S(1)}, u32[]{:S(2)}, u32[]{:S(2)}) collective-permute-start(bf16[1,144,256]{2,1,0:T(8,128)(2,1)S(1)} %maximum_bitcast_fusion), channel_id=1, source_target_pairs={{0,24},{4,28},{8,0},{12,4},{16,8},{20,12},{24,16},{28,20},{1,25},{... | collective-permute-start | bytes 221192 | tf_op jit(solution)/shard_map/ppermute | solution.py:164
  21.0 4.4 %collective-permute-start.6 = (bf16[1,144,256]{2,1,0:T(8,128)(2,1)S(1)}, bf16[1,144,256]{2,1,0:T(8,128)(2,1)S(1)}, u32[]{:S(2)}, u32[]{:S(2)}) collective-permute-start(bf16[1,144,256]{2,1,0:T(8,128)(2,1)S(1)} %maximum_bitcast_fusion), channel_id=1, source_target_pairs={{0,16},{4,20},{8,24},{12,28},{16,0},{20,4},{24,8},{28,12},{1,17},{... | collective-permute-start | bytes 221192 | tf_op jit(solution)/shard_map/ppermute | solution.py:164
  25.4 3.5 %collective-permute-done.6 = bf16[1,144,256]{2,1,0:T(8,128)(2,1)S(1)} collective-permute-done((bf16[1,144,256]{2,1,0:T(8,128)(2,1)S(1)}, bf16[1,144,256]{2,1,0:T(8,128)(2,1)S(1)}, u32[]{:S(2)}, u32[]{:S(2)}) %collective-permute-start.6) | collective-permute-done | bytes 73760 | tf_op jit(solution)/shard_map/ppermute | solution.py:164
  28.9 2.6 %collective-permute-start.7 = (bf16[4,144,256]{2,1,0:T(8,128)(2,1)S(1)}, bf16[4,144,256]{2,1,0:T(8,128)(2,1)S(1)}, u32[]{:S(2)}, u32[]{:S(2)}) collective-permute-start(bf16[4,144,256]{2,1,0:T(8,128)(2,1)S(1)} %pad_maximum_fusion.refs_0_), channel_id=1, source_target_pairs={{0,64},{32,224},{64,128},{96,32},{128,192},{160,96},{192,0},{224,1... | collective-permute-start | bytes 884744 | tf_op jit(solution)/shard_map/ppermute | solution.py:169
  31.5 4.5 %collective-permute-start.9 = (bf16[4,144,256]{2,1,0:T(8,128)(2,1)S(1)}, bf16[4,144,256]{2,1,0:T(8,128)(2,1)S(1)}, u32[]{:S(2)}, u32[]{:S(2)}) collective-permute-start(bf16[4,144,256]{2,1,0:T(8,128)(2,1)S(1)} %pad_maximum_fusion.refs_0_), channel_id=1, source_target_pairs={{0,32},{32,0},{64,96},{96,64},{128,160},{160,128},{192,224},{224,1... | collective-permute-start | bytes 884744 | tf_op jit(solution)/shard_map/ppermute | solution.py:159
  35.9 2.3 %collective-permute-start.10 = (bf16[4,144,256]{2,1,0:T(8,128)(2,1)S(1)}, bf16[4,144,256]{2,1,0:T(8,128)(2,1)S(1)}, u32[]{:S(2)}, u32[]{:S(2)}) collective-permute-start(bf16[4,144,256]{2,1,0:T(8,128)(2,1)S(1)} %collective-permute-done.7.refs_0_), channel_id=1, source_target_pairs={{0,64},{32,224},{64,128},{96,32},{128,192},{160,96},{192,0},{224,1... | collective-permute-start | bytes 884744 | tf_op jit(solution)/shard_map/ppermute | solution.py:169
  38.2 1.2 %constant_dynamic-slice_fusion.3.factor_ref = bf16[1536,256]{1,0:T(8,128)(2,1)S(1)} fusion(bf16[12288,256]{1,0:T(8,128)(2,1)} %param.8, s32[]{:T(128)S(6)} %select_n.43), kind=kLoop, calls=%fused_computation.16 | loop fusion | bytes 1572868 | tf_op jit(solution)/shard_map/dynamic_slice | solution.py:177
  39.4 3.9 %collective-permute-start.12 = (bf16[4,144,256]{2,1,0:T(8,128)(2,1)S(1)}, bf16[4,144,256]{2,1,0:T(8,128)(2,1)S(1)}, u32[]{:S(2)}, u32[]{:S(2)}) collective-permute-start(bf16[4,144,256]{2,1,0:T(8,128)(2,1)S(1)} %collective-permute-done.7.refs_0_), channel_id=1, source_target_pairs={{0,32},{32,0},{64,96},{96,64},{128,160},{160,128},{192,224},{224,1... | collective-permute-start | bytes 884744 | tf_op jit(solution)/shard_map/ppermute | solution.py:159
  43.5 1.3 %shard_map.65.refs_1_ = f32[1536,256]{1,0:T(8,128)S(1)} custom-call(bf16[1536,256]{1,0:T(8,128)(2,1)S(1)} %constant_dynamic-slice_fusion.3.factor_ref, bf16[4,144,256]{2,1,0:T(8,128)(2,1)S(1)} %pad_maximum_fusion.refs_0_), custom_call_target="tpu_custom_call" | custom-call | flops 805306368 | bytes 4194304 | tf_op jit(solution)/shard_map/pallas_call | solution.py:140
  44.8 1.3 %shard_map.66.refs_2_ = f32[1536,256]{1,0:T(8,128)S(1)} custom-call(bf16[1536,256]{1,0:T(8,128)(2,1)S(1)} %constant_dynamic-slice_fusion.3.factor_ref, bf16[4,144,256]{2,1,0:T(8,128)(2,1)S(1)} %collective-permute-done.9.refs_0_, f32[1536,256]{1,0:T(8,128)S(1)} %shard_map.65.refs_1_), custom_call_target="tpu_custom_call" | custom-call | flops 805306368 | bytes 4194304 | tf_op jit(solution)/shard_map/pallas_call | solution.py:140
  46.2 3.9 %collective-permute-start.11 = (bf16[4,144,256]{2,1,0:T(8,128)(2,1)S(1)}, bf16[4,144,256]{2,1,0:T(8,128)(2,1)S(1)}, u32[]{:S(2)}, u32[]{:S(2)}) collective-permute-start(bf16[4,144,256]{2,1,0:T(8,128)(2,1)S(1)} %collective-permute-done.10.refs_0_), channel_id=1, source_target_pairs={{0,32},{32,0},{64,96},{96,64},{128,160},{160,128},{192,224},{224,1... | collective-permute-start | bytes 884744 | tf_op jit(solution)/shard_map/ppermute | solution.py:159
  50.0 2.3 %shard_map.67 = f32[1536,256]{1,0:T(8,128)S(1)} custom-call(bf16[1536,256]{1,0:T(8,128)(2,1)S(1)} %constant_dynamic-slice_fusion.3.factor_ref, bf16[4,144,256]{2,1,0:T(8,128)(2,1)S(1)} %collective-permute-done.7.refs_0_, bf16[4,144,256]{2,1,0:T(8,128)(2,1)S(1)} %collective-permute-done.8.refs_1_, f32[1536,256]{1,0:T(8,128)S(1)} %shard_map.66.refs_2_), custom_call_target="tpu_custom_call" | custom-call | flops 1610612736 | bytes 4194304 | tf_op jit(solution)/shard_map/pallas_call | solution.py:140
  52.4 2.4 %shard_map.68.refs_2_ = f32[1536,256]{1,0:T(8,128)S(1)} custom-call(bf16[1536,256]{1,0:T(8,128)(2,1)S(1)} %constant_dynamic-slice_fusion.3.factor_ref, bf16[4,144,256]{2,1,0:T(8,128)(2,1)S(1)} %collective-permute-done.12.refs_0_, bf16[4,144,256]{2,1,0:T(8,128)(2,1)S(1)} %collective-permute-done.13.refs_1_), custom_call_target="tpu_custom_call" | custom-call | flops 1610612736 | bytes 4194304 | tf_op jit(solution)/shard_map/pallas_call | solution.py:140
  54.8 2.4 %shard_map.69 = f32[1536,256]{1,0:T(8,128)S(1)} custom-call(bf16[1536,256]{1,0:T(8,128)(2,1)S(1)} %constant_dynamic-slice_fusion.3.factor_ref, bf16[4,144,256]{2,1,0:T(8,128)(2,1)S(1)} %collective-permute-done.10.refs_0_, bf16[4,144,256]{2,1,0:T(8,128)(2,1)S(1)} %collective-permute-done.11.refs_1_, f32[1536,256]{1,0:T(8,128)S(1)} %shard_map.68.refs_2_), custom_call_target="tpu_custom_call" | custom-call | flops 1610612736 | bytes 4194304 | tf_op jit(solution)/shard_map/pallas_call | solution.py:140
  59.4 1.5 %collective-permute-start.16 = (f16[384,256]{1,0:T(8,128)(2,1)S(1)}, f16[384,256]{1,0:T(8,128)(2,1)S(1)}, u32[]{:S(2)}, u32[]{:S(2)}) collective-permute-start(f16[384,256]{1,0:T(8,128)(2,1)S(1)} %get-tuple-element.12), channel_id=1, source_target_pairs={{0,3},{1,0},{2,1},{3,2},{4,7},{5,4},{6,5},{7,6},{8,11},{9,8},{10,9... | collective-permute-start | bytes 589832 | tf_op jit(solution)/shard_map/ppermute | solution.py:164
  60.9 4.6 %collective-permute-done.14 = f16[384,256]{1,0:T(8,128)(2,1)S(1)} collective-permute-done((f16[384,256]{1,0:T(8,128)(2,1)S(1)}, f16[384,256]{1,0:T(8,128)(2,1)S(1)}, u32[]{:S(2)}, u32[]{:S(2)}) %collective-permute-start.14) | collective-permute-done | bytes 196640 | tf_op jit(solution)/shard_map/ppermute | solution.py:164
  65.6 4.5 %collective-permute-done.15 = f16[384,256]{1,0:T(8,128)(2,1)S(1)} collective-permute-done((f16[384,256]{1,0:T(8,128)(2,1)S(1)}, f16[384,256]{1,0:T(8,128)(2,1)S(1)}, u32[]{:S(2)}, u32[]{:S(2)}) %collective-permute-start.15) | collective-permute-done | bytes 196640 | tf_op jit(solution)/shard_map/ppermute | solution.py:164
  (30 shorter events, 5.4 us)
Async XLA Ops:
  0.0 1.0 %copy-start = (bf16[256,512]{1,0:T(8,128)(2,1)S(1)}, bf16[256,512]{1,0:T(8,128)(2,1)}, u32[]{:S(2)}) copy-start(bf16[256,512]{1,0:T(8,128)(2,1)} %param.6) | copy-start | bytes 786436
  2.2 9.0 %collective-permute-start = (f32[64,256]{1,0:T(8,128)S(1)}, f32[64,256]{1,0:T(8,128)S(1)}, u32[]{:S(2)}, u32[]{:S(2)}) collective-permute-start(f32[64,256]{1,0:T(8,128)S(1)} %get-tuple-element.17), channel_id=1, source_target_pairs={{0,2},{1,3},{2,0},{3,1},{4,6},{5,7},{6,4},{7,5},{8,10},{9,11},{10,... | collective-permute-start | bytes 196616 | tf_op jit(solution)/shard_map/ppermute | solution.py:164
  6.0 5.2 %collective-permute-start.1 = (f32[64,256]{1,0:T(8,128)S(1)}, f32[64,256]{1,0:T(8,128)S(1)}, u32[]{:S(2)}, u32[]{:S(2)}) collective-permute-start(f32[64,256]{1,0:T(8,128)S(1)} %get-tuple-element.19), channel_id=1, source_target_pairs={{0,1},{1,2},{2,3},{3,0},{4,5},{5,6},{6,7},{7,4},{8,9},{9,10},{10,1... | collective-permute-start | bytes 196616 | tf_op jit(solution)/shard_map/ppermute | solution.py:164
  6.4 4.8 %collective-permute-start.2 = (f32[64,256]{1,0:T(8,128)S(1)}, f32[64,256]{1,0:T(8,128)S(1)}, u32[]{:S(2)}, u32[]{:S(2)}) collective-permute-start(f32[64,256]{1,0:T(8,128)S(1)} %get-tuple-element.18), channel_id=1, source_target_pairs={{0,3},{1,0},{2,1},{3,2},{4,7},{5,4},{6,5},{7,6},{8,11},{9,8},{10,9... | collective-permute-start | bytes 196616 | tf_op jit(solution)/shard_map/ppermute | solution.py:164
  11.9 3.0 %collective-permute-start.3 = (bf16[80,256]{1,0:T(8,128)(2,1)S(1)}, bf16[80,256]{1,0:T(8,128)(2,1)S(1)}, u32[]{:S(2)}, u32[]{:S(2)}) collective-permute-start(bf16[80,256]{1,0:T(8,128)(2,1)S(1)} %pad_maximum_fusion.1), channel_id=1, source_target_pairs={{0,4},{4,0},{8,12},{12,8},{16,20},{20,16},{24,28},{28,24},{1,5},{5... | collective-permute-start | bytes 122888 | tf_op jit(solution)/shard_map/ppermute | solution.py:159
  15.0 10.4 %collective-permute-start.4 = (bf16[1,144,256]{2,1,0:T(8,128)(2,1)S(1)}, bf16[1,144,256]{2,1,0:T(8,128)(2,1)S(1)}, u32[]{:S(2)}, u32[]{:S(2)}) collective-permute-start(bf16[1,144,256]{2,1,0:T(8,128)(2,1)S(1)} %maximum_bitcast_fusion), channel_id=1, source_target_pairs={{0,8},{4,12},{8,16},{12,20},{16,24},{20,28},{24,0},{28,4},{1,9},{5... | collective-permute-start | bytes 221192 | tf_op jit(solution)/shard_map/ppermute | solution.py:164
  18.1 7.3 %collective-permute-start.5 = (bf16[1,144,256]{2,1,0:T(8,128)(2,1)S(1)}, bf16[1,144,256]{2,1,0:T(8,128)(2,1)S(1)}, u32[]{:S(2)}, u32[]{:S(2)}) collective-permute-start(bf16[1,144,256]{2,1,0:T(8,128)(2,1)S(1)} %maximum_bitcast_fusion), channel_id=1, source_target_pairs={{0,24},{4,28},{8,0},{12,4},{16,8},{20,12},{24,16},{28,20},{1,25},{... | collective-permute-start | bytes 221192 | tf_op jit(solution)/shard_map/ppermute | solution.py:164
  21.0 7.9 %collective-permute-start.6 = (bf16[1,144,256]{2,1,0:T(8,128)(2,1)S(1)}, bf16[1,144,256]{2,1,0:T(8,128)(2,1)S(1)}, u32[]{:S(2)}, u32[]{:S(2)}) collective-permute-start(bf16[1,144,256]{2,1,0:T(8,128)(2,1)S(1)} %maximum_bitcast_fusion), channel_id=1, source_target_pairs={{0,16},{4,20},{8,24},{12,28},{16,0},{20,4},{24,8},{28,12},{1,17},{... | collective-permute-start | bytes 221192 | tf_op jit(solution)/shard_map/ppermute | solution.py:164
  28.9 7.0 %collective-permute-start.7 = (bf16[4,144,256]{2,1,0:T(8,128)(2,1)S(1)}, bf16[4,144,256]{2,1,0:T(8,128)(2,1)S(1)}, u32[]{:S(2)}, u32[]{:S(2)}) collective-permute-start(bf16[4,144,256]{2,1,0:T(8,128)(2,1)S(1)} %pad_maximum_fusion.refs_0_), channel_id=1, source_target_pairs={{0,64},{32,224},{64,128},{96,32},{128,192},{160,96},{192,0},{224,1... | collective-permute-start | bytes 884744 | tf_op jit(solution)/shard_map/ppermute | solution.py:169
  31.5 11.9 %collective-permute-start.8 = (bf16[4,144,256]{2,1,0:T(8,128)(2,1)S(1)}, bf16[4,144,256]{2,1,0:T(8,128)(2,1)S(1)}, u32[]{:S(2)}, u32[]{:S(2)}) collective-permute-start(bf16[4,144,256]{2,1,0:T(8,128)(2,1)S(1)} %pad_maximum_fusion.refs_0_), channel_id=1, source_target_pairs={{0,192},{32,96},{64,0},{96,160},{128,64},{160,224},{192,128},{224,... | collective-permute-start | bytes 884744 | tf_op jit(solution)/shard_map/ppermute | solution.py:169
  31.5 13.3 %collective-permute-start.9 = (bf16[4,144,256]{2,1,0:T(8,128)(2,1)S(1)}, bf16[4,144,256]{2,1,0:T(8,128)(2,1)S(1)}, u32[]{:S(2)}, u32[]{:S(2)}) collective-permute-start(bf16[4,144,256]{2,1,0:T(8,128)(2,1)S(1)} %pad_maximum_fusion.refs_0_), channel_id=1, source_target_pairs={{0,32},{32,0},{64,96},{96,64},{128,160},{160,128},{192,224},{224,1... | collective-permute-start | bytes 884744 | tf_op jit(solution)/shard_map/ppermute | solution.py:159
  35.9 10.2 %collective-permute-start.10 = (bf16[4,144,256]{2,1,0:T(8,128)(2,1)S(1)}, bf16[4,144,256]{2,1,0:T(8,128)(2,1)S(1)}, u32[]{:S(2)}, u32[]{:S(2)}) collective-permute-start(bf16[4,144,256]{2,1,0:T(8,128)(2,1)S(1)} %collective-permute-done.7.refs_0_), channel_id=1, source_target_pairs={{0,64},{32,224},{64,128},{96,32},{128,192},{160,96},{192,0},{224,1... | collective-permute-start | bytes 884744 | tf_op jit(solution)/shard_map/ppermute | solution.py:169
  39.4 13.0 %collective-permute-start.12 = (bf16[4,144,256]{2,1,0:T(8,128)(2,1)S(1)}, bf16[4,144,256]{2,1,0:T(8,128)(2,1)S(1)}, u32[]{:S(2)}, u32[]{:S(2)}) collective-permute-start(bf16[4,144,256]{2,1,0:T(8,128)(2,1)S(1)} %collective-permute-done.7.refs_0_), channel_id=1, source_target_pairs={{0,32},{32,0},{64,96},{96,64},{128,160},{160,128},{192,224},{224,1... | collective-permute-start | bytes 884744 | tf_op jit(solution)/shard_map/ppermute | solution.py:159
  43.4 9.0 %collective-permute-start.13 = (bf16[4,144,256]{2,1,0:T(8,128)(2,1)S(1)}, bf16[4,144,256]{2,1,0:T(8,128)(2,1)S(1)}, u32[]{:S(2)}, u32[]{:S(2)}) collective-permute-start(bf16[4,144,256]{2,1,0:T(8,128)(2,1)S(1)} %collective-permute-done.8.refs_1_), channel_id=1, source_target_pairs={{0,32},{32,0},{64,96},{96,64},{128,160},{160,128},{192,224},{224,1... | collective-permute-start | bytes 884744 | tf_op jit(solution)/shard_map/ppermute | solution.py:159
  46.2 8.6 %collective-permute-start.11 = (bf16[4,144,256]{2,1,0:T(8,128)(2,1)S(1)}, bf16[4,144,256]{2,1,0:T(8,128)(2,1)S(1)}, u32[]{:S(2)}, u32[]{:S(2)}) collective-permute-start(bf16[4,144,256]{2,1,0:T(8,128)(2,1)S(1)} %collective-permute-done.10.refs_0_), channel_id=1, source_target_pairs={{0,32},{32,0},{64,96},{96,64},{128,160},{160,128},{192,224},{224,1... | collective-permute-start | bytes 884744 | tf_op jit(solution)/shard_map/ppermute | solution.py:159
  57.4 8.1 %collective-permute-start.14 = (f16[384,256]{1,0:T(8,128)(2,1)S(1)}, f16[384,256]{1,0:T(8,128)(2,1)S(1)}, u32[]{:S(2)}, u32[]{:S(2)}) collective-permute-start(f16[384,256]{1,0:T(8,128)(2,1)S(1)} %get-tuple-element.10), channel_id=1, source_target_pairs={{0,2},{1,3},{2,0},{3,1},{4,6},{5,7},{6,4},{7,5},{8,10},{9,11},{10,... | collective-permute-start | bytes 589832 | tf_op jit(solution)/shard_map/ppermute | solution.py:164
  58.2 11.8 %collective-permute-start.15 = (f16[384,256]{1,0:T(8,128)(2,1)S(1)}, f16[384,256]{1,0:T(8,128)(2,1)S(1)}, u32[]{:S(2)}, u32[]{:S(2)}) collective-permute-start(f16[384,256]{1,0:T(8,128)(2,1)S(1)} %get-tuple-element.11), channel_id=1, source_target_pairs={{0,1},{1,2},{2,3},{3,0},{4,5},{5,6},{6,7},{7,4},{8,9},{9,10},{10,1... | collective-permute-start | bytes 589832 | tf_op jit(solution)/shard_map/ppermute | solution.py:164
  59.4 10.7 %collective-permute-start.16 = (f16[384,256]{1,0:T(8,128)(2,1)S(1)}, f16[384,256]{1,0:T(8,128)(2,1)S(1)}, u32[]{:S(2)}, u32[]{:S(2)}) collective-permute-start(f16[384,256]{1,0:T(8,128)(2,1)S(1)} %get-tuple-element.12), channel_id=1, source_target_pairs={{0,3},{1,0},{2,1},{3,2},{4,7},{5,4},{6,5},{7,6},{8,11},{9,8},{10,9... | collective-permute-start | bytes 589832 | tf_op jit(solution)/shard_map/ppermute | solution.py:164
